TPU v7x, 256 devices: a whole 4x4x8 slice. The times are simulated.
256 devices in a mesh: seq: 32 (over y, z), ch: 8 (over x, core).
Axes of the slice: x: 4, y: 4, z: 8, core: 2. Of those that a mesh axis runs over, the one named last changes fastest.
Arguments:
- signal: bfloat16 [4096, 8192], P('seq', 'ch'), may hold values from -6 to 6
- gate_values: bfloat16 [4096, 8192], P('seq', 'ch'), may hold values from -6 to 6
- filter_taps: bfloat16 [4096, 8192], P('seq', 'ch'), may hold values from -0.09375 to 0.09375
- skip_gain: float32 [8192], P(('ch', 'seq')), may hold values from -1 to 1
- w_out: bfloat16 [8192, 8192], P('ch', 'seq'), may hold values from -0.0625 to 0.0625
- cotangent: bfloat16 [4096, 8192], P('seq', 'ch'), may hold values from -6 to 6
Outputs:
- grad_input: bfloat16 [4096, 8192], P('seq', 'ch')
- grad_gate: bfloat16 [4096, 8192], P('seq', 'ch')
- grad_filter: bfloat16 [4096, 8192], P('seq', 'ch')
- grad_skip: float32 [8192], P(('ch', 'seq'))
- grad_weight: float32 [8192, 8192], P('ch', 'seq')
All inputs are finite; a program needn't handle non-finite values.
Results may differ from a plain program's by a relative error of at most 0.005.
Values may be sent and summed in bfloat16 or wider, within the bound.
No kernel may reach another device: no remote copies, remote signals or barrier semaphores. Data moves between devices by JAX's collectives and lax.ppermute only.
A program may use at most 128 MiB of HBM per device.

v0:
```python
import math

import jax
import jax.numpy as jnp
import numpy as np
from jax import lax
from jax.experimental import pallas as pl
from jax.experimental.pallas import tpu as pltpu
from jax.sharding import Mesh
from jax.sharding import PartitionSpec as P

NY, NZ, NX, NH = 4, 8, 4, 2
NS = NY * NZ
TOK = 128
CL = 32
CC = 16
FREQ = 2 * NS * TOK
ROOT = 1.0 / math.sqrt(NS * TOK)
bf16, f32 = jnp.bfloat16, jnp.float32


def halves(matrix):
    high = matrix.astype(jnp.bfloat16)
    low = (matrix - high.astype(np.float64)).astype(jnp.bfloat16)
    return high, low


def tables():
    k = np.arange(NS)[:, None] + 0.5
    n = np.arange(NS)[None, :]
    m = np.arange(TOK)[None, :]
    outer = 2.0 * np.pi * k * n / (2 * NS)
    a = np.concatenate([np.cos(outer), -np.sin(outer)], axis=0)
    a_inv = np.concatenate([np.cos(outer).T, -np.sin(outer).T], axis=1) * (2.0 / FREQ)
    turn = 2.0 * np.pi * k * m / FREQ
    inner = 2.0 * np.pi * (np.arange(TOK)[:, None] * m % TOK) / TOK
    c, s = np.cos(inner), np.sin(inner)
    b = np.block([[c, -s], [s, c]])
    b_inv = np.block([[c, s], [-s, c]])
    a_hi, a_lo = halves(a)
    i_hi, i_lo = halves(a_inv)
    b_hi, b_lo = halves(b)
    v_hi, v_lo = halves(b_inv)
    return (
        np.concatenate([a_hi, a_lo], axis=1),
        np.concatenate([i_hi, i_lo], axis=1),
        np.stack([b_hi, b_lo]),
        np.stack([v_hi, v_lo]),
        np.stack([np.cos(turn), np.sin(turn)]).astype(np.float32),
    )


def dot(x, y):
    return jnp.dot(x, y, preferred_element_type=f32)


def split(x):
    high = x.astype(bf16)
    return high, (x - high.astype(f32)).astype(bf16)


def rows_of(ref, c):
    return ref[pl.ds(c, NS, stride=CC), :]


def forward(src, a_ref, b_ref, t_ref):
    x = jnp.concatenate([rows_of(src, c) for c in range(CC)], axis=1).astype(bf16)
    a = a_ref[...]
    z = dot(a[:, :NS], x) + dot(a[:, NS:], x)
    tc, ts = t_ref[0], t_ref[1]
    parts = []
    for c in range(CC):
        re = z[:NS, c * TOK : (c + 1) * TOK]
        im = z[NS:, c * TOK : (c + 1) * TOK]
        parts.append(jnp.concatenate([re * tc + im * ts, im * tc - re * ts], axis=1))
    hi, lo = split(jnp.concatenate(parts, axis=0))
    return dot(hi, b_ref[0]) + dot(hi, b_ref[1]) + dot(lo, b_ref[0])


def inverse(spec, i_ref, v_ref, t_ref, dst):
    hi, lo = split(spec)
    v = dot(hi, v_ref[0]) + dot(hi, v_ref[1]) + dot(lo, v_ref[0])
    tc, ts = t_ref[0], t_ref[1]
    parts = []
    for c in range(CC):
        re = v[c * NS : (c + 1) * NS, :TOK]
        im = v[c * NS : (c + 1) * NS, TOK:]
        parts.append(jnp.concatenate([re * tc - im * ts, im * tc + re * ts], axis=0))
    hi, lo = split(jnp.concatenate(parts, axis=1))
    a = i_ref[...]
    y = dot(a[:, : 2 * NS], hi) + dot(a[:, 2 * NS :], hi) + dot(a[:, : 2 * NS], lo)
    for c in range(CC):
        dst[pl.ds(c, NS, stride=CC), :] = y[:, c * TOK : (c + 1) * TOK]


def times(p, q):
    pr, pi, qr, qi = p[:, :TOK], p[:, TOK:], q[:, :TOK], q[:, TOK:]
    return jnp.concatenate([pr * qr - pi * qi, pr * qi + pi * qr], axis=1)


def times_conj(p, q):
    pr, pi, qr, qi = p[:, :TOK], p[:, TOK:], q[:, :TOK], q[:, TOK:]
    return jnp.concatenate([pr * qr + pi * qi, pi * qr - pr * qi], axis=1)


def flat(x):
    return x.reshape(NS * CC, TOK)


def conv_kernel(in_ref, skip_ref, a_ref, i_ref, b_ref, v_ref, t_ref, mixed_ref, gated_ref, sig_ref, tap_ref, buf):
    buf[...] = flat(in_ref[:, 1].astype(f32))
    tap = forward(buf, a_ref, b_ref, t_ref)
    tap_ref[...] = tap
    buf[...] = flat(in_ref[:, 0].astype(f32))
    sig = forward(buf, a_ref, b_ref, t_ref)
    sig_ref[...] = sig
    inverse(times(sig, tap), i_ref, v_ref, t_ref, buf)
    skip = skip_ref[...]
    for n in range(NS):
        mixed = (buf[n * CC : (n + 1) * CC, :] + skip * in_ref[n, 0].astype(f32)).astype(bf16)
        mixed_ref[n] = mixed
        gated = in_ref[n, 2].astype(f32) * mixed.astype(f32)
        z = n % NZ
        gated_ref[n // NZ, :, z * TOK : (z + 1) * TOK] = gated.astype(bf16)


def back_kernel(gg_ref, in_ref, mixed_ref, sig_ref, tap_ref, skip_ref, a_ref, i_ref, b_ref, v_ref, t_ref, out_ref, gs_ref, buf, gmb):
    total = jnp.zeros((CC, TOK), f32)
    for n in range(NS):
        z = n % NZ
        gg = gg_ref[n // NZ, :, z * TOK : (z + 1) * TOK].astype(f32)
        out_ref[n, 2] = (gg * mixed_ref[n].astype(f32)).astype(bf16)
        gm = (gg * in_ref[n, 2].astype(f32)).astype(bf16).astype(f32)
        gmb[n * CC : (n + 1) * CC, :] = gm
        total = total + gm * in_ref[n, 0].astype(f32)
    gs_ref[...] = total * ROOT
    grad = forward(gmb, a_ref, b_ref, t_ref)
    inverse(times_conj(grad, tap_ref[...]), i_ref, v_ref, t_ref, buf)
    skip = skip_ref[...]
    for n in range(NS):
        rows = slice(n * CC, (n + 1) * CC)
        out_ref[n, 0] = (buf[rows, :] + skip * gmb[rows, :]).astype(bf16)
    inverse(times_conj(grad, sig_ref[...]), i_ref, v_ref, t_ref, buf)
    for n in range(NS):
        rows = slice(n * CC, (n + 1) * CC)
        out_ref[n, 1] = (buf[rows, :] * ROOT).astype(bf16)


def whole(array):
    rank = array.ndim
    return pl.BlockSpec(array.shape, lambda i: (0,) * rank)


STEPS = CL // CC
PACK = pl.BlockSpec((NS, 3, CC, TOK), lambda i: (0, 0, i, 0))
PLAIN = pl.BlockSpec((NS, CC, TOK), lambda i: (0, i, 0))
WIDE = pl.BlockSpec((NY, CC, NZ * TOK), lambda i: (0, i, 0))
SPEC = pl.BlockSpec((CC * NS, 2 * TOK), lambda i: (i, 0))
LANE = pl.BlockSpec((CC, TOK), lambda i: (i, 0))
SHAPE = jax.ShapeDtypeStruct


def conv(cols, skip, tabs):
    return pl.pallas_call(
        conv_kernel,
        grid=(STEPS,),
        in_specs=[PACK, LANE] + [whole(t) for t in tabs],
        out_specs=[PLAIN, WIDE, SPEC, SPEC],
        out_shape=[
            SHAPE((NS, CL, TOK), bf16),
            SHAPE((NY, CL, NZ * TOK), bf16),
            SHAPE((CL * NS, 2 * TOK), f32),
            SHAPE((CL * NS, 2 * TOK), f32),
        ],
        scratch_shapes=[pltpu.VMEM((NS * CC, TOK), f32)],
        name="conv",
    )(cols, skip, *tabs)


def back(gg, cols, mixed, sig, tap, skip, tabs):
    return pl.pallas_call(
        back_kernel,
        grid=(STEPS,),
        in_specs=[WIDE, PACK, PLAIN, SPEC, SPEC, LANE] + [whole(t) for t in tabs],
        out_specs=[PACK, LANE],
        out_shape=[SHAPE((NS, 3, CL, TOK), bf16), SHAPE((CL, TOK), f32)],
        scratch_shapes=[pltpu.VMEM((NS * CC, TOK), f32)] * 2,
        name="back",
    )(gg, cols, mixed, sig, tap, skip, *tabs)


def to_cols_kernel(s_ref, f_ref, g_ref, out_ref):
    for i, ref in enumerate((s_ref, f_ref, g_ref)):
        for b in range(ref.shape[1] // TOK):
            turned = ref[:, b * TOK : (b + 1) * TOK].T
            for j in range(TOK // CL):
                out_ref[b * (TOK // CL) + j, i] = turned[j * CL : (j + 1) * CL, :]


def to_cols(signal, taps, gate):
    width = signal.shape[1]
    span = 4 * TOK
    block = pl.BlockSpec((TOK, span), lambda i: (0, i))
    return pl.pallas_call(
        to_cols_kernel,
        grid=(width // span,),
        in_specs=[block] * 3,
        out_specs=pl.BlockSpec((span // CL, 3, CL, TOK), lambda i: (i, 0, 0, 0)),
        out_shape=SHAPE((NS, 3, CL, TOK), bf16),
        name="to_cols",
    )(signal, taps, gate)


def to_rows_kernel(in_ref, a_ref, b_ref, c_ref):
    for i, ref in enumerate((a_ref, b_ref, c_ref)):
        for b in range(ref.shape[1] // TOK):
            first = b * (TOK // CL)
            stacked = jnp.concatenate([in_ref[first + j, i] for j in range(TOK // CL)], axis=0)
            ref[:, b * TOK : (b + 1) * TOK] = stacked.T


def to_rows(cols):
    span = 4 * TOK
    block = pl.BlockSpec((TOK, span), lambda i: (0, i))
    out = SHAPE((TOK, NS * CL), bf16)
    return pl.pallas_call(
        to_rows_kernel,
        grid=(NS * CL // span,),
        in_specs=[pl.BlockSpec((span // CL, 3, CL, TOK), lambda i: (i, 0, 0, 0))],
        out_specs=[block] * 3,
        out_shape=[out] * 3,
        name="to_rows",
    )(cols)


OWN = (3, 2, 1, 6, 7, 0)
SENT = (4, 5)


def gated_kernel(at, w0, w1, w2, w3, q0, q1, q2, q3, cot_ref, own_ref, sent_ref, acc):
    y, z, x, core = at[0], at[1], at[2], at[3]
    for s, q in enumerate((q0, q1, q2, q3)):
        mine, other = q[0], q[1]
        first = jnp.where(core == 0, mine, other)
        second = jnp.where(core == 0, other, mine)
        cot_ref[(x + s) % NX] = jnp.concatenate([first, second], axis=1)
    total = None
    for r, w in enumerate((w0, w1, w2, w3)):
        part = lax.dot_general(
            w[...], cot_ref[(y + r) % NY], (((1,), (1,)), ((), ())), preferred_element_type=f32
        )
        total = part if total is None else total + part
    acc[...] = total

    def block(offset, b):
        return acc[pl.ds(pl.multiple_of((b * NZ + (z + offset) % NZ) * CL, CL), CL), :]

    for b in range(NY):
        rows = slice(b * CL, (b + 1) * CL)
        for i, offset in enumerate(OWN):
            own_ref[i, rows, :] = block(offset, b)
        for i, offset in enumerate(SENT):
            sent_ref[i, rows, :] = block(offset, b).astype(bf16)


def grad_gated_part(at, ws, qs):
    c, f = ws[0].shape
    t = qs[0].shape[1]
    span = 2 * TOK
    return pl.pallas_call(
        gated_kernel,
        grid_spec=pltpu.PrefetchScalarGridSpec(
            num_scalar_prefetch=1,
            grid=(t // span,),
            in_specs=[pl.BlockSpec((c, f), lambda i, at: (0, 0))] * NY
            + [pl.BlockSpec((NH, span, f // NH), lambda i, at: (0, i, 0))] * NX,
            out_specs=[
                pl.BlockSpec((NX, span, f), lambda i, at: (0, i, 0)),
                pl.BlockSpec((len(OWN), NY * CL, span), lambda i, at: (0, 0, i)),
                pl.BlockSpec((len(SENT), NY * CL, span), lambda i, at: (0, 0, i)),
            ],
            scratch_shapes=[pltpu.VMEM((c, span), f32)],
        ),
        out_shape=[
            SHAPE((NX, t, f), bf16),
            SHAPE((len(OWN), NY * CL, t), f32),
            SHAPE((len(SENT), NY * CL, t), bf16),
        ],
        name="grad_gated",
    )(at, *ws, *qs)


def weight_kernel(at, *refs):
    pieces, cot_ref, outs, gated = refs[: NZ + 1], refs[NZ + 1], refs[NZ + 2 : -1], refs[-1]
    step = pl.program_id(0)

    @pl.when(step == 0)
    def _():
        row = 0
        for piece in pieces:
            gated[row : row + piece.shape[0], :] = piece[...]
            row += piece.shape[0]

    part = (dot(gated[...], cot_ref[0]) * ROOT).astype(bf16)
    for i, out in enumerate(outs):

        @pl.when(step == i)
        def _():
            out[...] = part


def grad_weight_part(at, pieces, cot_all):
    c, t, f = NS * CL, cot_all.shape[1], cot_all.shape[2]
    return pl.pallas_call(
        weight_kernel,
        grid_spec=pltpu.PrefetchScalarGridSpec(
            num_scalar_prefetch=1,
            grid=(NY,),
            in_specs=[pl.BlockSpec(p.shape, lambda i, at: (0, 0)) for p in pieces]
            + [pl.BlockSpec((1, t, f), lambda i, at: ((at[0] + i) % NY, 0, 0))],
            out_specs=[pl.BlockSpec((c, f), lambda i, at: (0, 0))] * NY,
            scratch_shapes=[pltpu.VMEM((c, t), bf16)],
        ),
        out_shape=[SHAPE((c, f), bf16)] * NY,
        name="grad_weight",
    )(at, *pieces, cot_all)


def sum_kernel(at, a_ref, b_ref, c_ref, d_ref, out_ref):
    z = at[1]
    for r in range(NZ):
        for b in range(NY):
            rows = slice((r * NY + b) * CL, (r * NY + b + 1) * CL)
            total = a_ref[rows, :].astype(f32) + b_ref[rows, :].astype(f32)
            total = total + c_ref[rows, :].astype(f32) + d_ref[rows, :].astype(f32)
            out_ref[b, (z + r) % NZ] = total


def weight_sum(at, parts):
    c, f = parts[0].shape
    return pl.pallas_call(
        sum_kernel,
        grid_spec=pltpu.PrefetchScalarGridSpec(
            num_scalar_prefetch=1,
            grid=(f // TOK,),
            in_specs=[pl.BlockSpec((c, TOK), lambda i, at: (0, i))] * NY,
            out_specs=pl.BlockSpec((NY, NZ, CL, TOK), lambda i, at: (0, 0, 0, i)),
        ),
        out_shape=SHAPE((NY, NZ, CL, f), f32),
        name="weight_sum",
    )(at, *parts).reshape(c, f)


def shift(value, axis, by):
    count = lax.axis_size(axis)
    return lax.ppermute(value, axis, [(i, (i + by) % count) for i in range(count)])


def add(received, own):
    return (received.astype(f32) + own).astype(bf16)


def after(value, *earlier):
    return lax.optimization_barrier((value,) + earlier)[0]


def ordered(signal, gate_values, filter_taps, skip_gain, w_out, cotangent):
    tabs = [jnp.asarray(t) for t in tables()]
    seq = ("y", "z")
    at = jnp.stack([lax.axis_index(a) for a in ("y", "z", "x", "core")]).astype(jnp.int32)
    ws = [w_out, shift(w_out, "y", -1), shift(w_out, "y", 2), shift(w_out, "y", 1)]

    pieces = cotangent.reshape(TOK, NZ // NH, NH, TOK).transpose(2, 1, 0, 3)
    pieces = lax.all_to_all(pieces, "core", split_axis=0, concat_axis=0, tiled=True)
    pieces = pieces.reshape(NZ, TOK, TOK)
    pieces = lax.all_to_all(pieces, "z", split_axis=0, concat_axis=0, tiled=True)
    pieces = pieces.reshape(NZ * TOK, TOK)
    chip = jnp.stack([pieces, shift(pieces, "core", 1)])
    chips = [chip, shift(chip, "x", -1), shift(chip, "x", 2), shift(chip, "x", 1)]

    cols = to_cols(after(signal, pieces), filter_taps, gate_values)
    cols = lax.all_to_all(cols, seq, split_axis=0, concat_axis=0, tiled=True)

    cot_all, own, sent = grad_gated_part(after(at, cols), ws, chips)
    up = shift(sent[0], "z", 1)
    down = shift(sent[1], "z", -1)

    skip = jnp.broadcast_to(after(skip_gain, own)[:, None], (CL, TOK))
    mixed, gated, sig_spec, tap_spec = conv(cols, skip, tabs)
    gated = lax.all_to_all(gated, "y", split_axis=0, concat_axis=0, tiled=True)
    gated = gated.reshape(NY * CL, NZ * TOK)

    for i in range(2):
        up, down = lax.optimization_barrier((up, down))
        up, down = add(up, own[i]), add(down, own[3 + i])
        up = shift(up, "z", 1)
        down = shift(down, "z", -1)
    up, down = lax.optimization_barrier((up, down))
    rest = down.astype(f32) + own[5]
    up = shift(add(up, own[2]), "z", 1)
    part = (up.astype(f32) + rest).astype(bf16)

    fore, aft = [gated], [gated]
    for _ in range(3):
        fore.append(shift(fore[-1], "z", 1))
        aft.append(shift(aft[-1], "z", -1))
    half = NY * CL // 2
    far = [shift(fore[-1][:half], "z", 1), shift(aft[-1][half:], "z", -1)]
    ring = [gated] + aft[1:] + far + fore[:0:-1]

    part = part.reshape(NY, CL, NZ * TOK)
    grad_gated = lax.all_to_all(part, "y", split_axis=0, concat_axis=0, tiled=True)
    outs, skip_sum = back(grad_gated, cols, mixed, sig_spec, tap_spec, skip, tabs)
    outs_rows = lax.all_to_all(outs, seq, split_axis=0, concat_axis=0, tiled=True)
    grad_input, grad_filter, grad_gate = to_rows(outs_rows)

    kept, up1, up2, up3 = grad_weight_part(after(at, skip_sum), ring, cot_all)
    moved = [shift(up1, "y", 1), shift(up2, "y", 2), shift(up3, "y", -1)]
    weight = weight_sum(at, [kept] + moved)
    return (grad_input, grad_gate, grad_filter, jnp.sum(skip_sum, axis=1), weight)


def solution(mesh):
    fine = Mesh(mesh.devices.reshape(NY, NZ, NX, NH), ("y", "z", "x", "core"))
    seq, ch = ("y", "z"), ("x", "core")
    rows = P(seq, ch)
    vector = P(ch + seq)
    weights = P(ch, seq)
    return jax.shard_map(
        ordered,
        mesh=fine,
        in_specs=(rows, rows, rows, vector, weights, rows),
        out_specs=(rows, rows, rows, vector, weights),
        check_vma=False,
    )
```

profile of v0, /device:TPU:32, one launch (start us, length us, event | category | flops | bytes accessed | tf_op | source)
XLA Modules:
  0.0 223.5 jit_solution(6762794684899311900)
XLA Ops:
  0.6 1.2 copy.17
  2.0 3.9 %all_to_all.30 = bf16[2,4,128,128]{3,1,2,0:T(4,128)(2,1)S(1)} all-to-all(bf16[2,4,128,128]{3,1,2,0:T(4,128)(2,1)S(1)} %copy.18), channel_id=1, replica_groups=mesh['y'=4,'z'=8,'x'=4,'core'=2] {'core'}, dimensions={0} | all-to-all | bytes 524288 | tf_op jit(solution)/shard_map/all_to_all | solution.py:374
  6.0 19.1 %all_to_all.31 = bf16[8,128,128]{2,1,0:T(8,128)(2,1)S(1)} all-to-all(bf16[8,128,128]{2,1,0:T(8,128)(2,1)S(1)} %bitcast.48), channel_id=1, replica_groups=mesh['y'=4,'z'=8,'x'=4,'core'=2] {'z'}, dimensions={0} | all-to-all | bytes 524288 | tf_op jit(solution)/shard_map/all_to_all | solution.py:376
  25.1 2.1 to_cols.1
  27.2 6.1 %all-to-all-start.2 = ((bf16[32,3,32,128]{3,2,1,0:T(8,128)(2,1)}), bf16[32,3,32,128]{3,2,1,0:T(8,128)(2,1)S(1)}, u32[]{:S(2)}, u32[]{:S(2)}) async-start(bf16[32,3,32,128]{3,2,1,0:T(8,128)(2,1)} %to_cols.1), calls=%async_computation.2 | async-start | bytes 1572864 | tf_op jit(solution)/shard_map/all_to_all | solution.py:382
  33.3 3.1 %collective-permute-start.1 = (bf16[1024,256]{1,0:T(8,128)(2,1)S(1)}, bf16[1024,256]{1,0:T(8,128)(2,1)S(1)}, u32[]{:S(2)}, u32[]{:S(2)}) collective-permute-start(bf16[1024,256]{1,0:T(8,128)(2,1)S(1)} %copy-done.8), channel_id=1, source_target_pairs={{0,128},{64,192},{128,0},{192,64},{1,129},{65,193},{129,1},{193,65... | collective-permute-start | bytes 1572872 | tf_op jit(solution)/shard_map/ppermute | solution.py:356
  36.4 1.2 collective-permute-start
  37.6 0.9 collective-permute-start.2
  38.5 1.6 collective-permute-start.6
  40.1 2.7 %collective-permute-start.5 = (bf16[2,1024,128]{2,1,0:T(8,128)(2,1)S(1)}, bf16[2,1024,128]{2,1,0:T(8,128)(2,1)}, u32[]{:S(2)}, u32[]{:S(2)}) collective-permute-start(bf16[2,1024,128]{2,1,0:T(8,128)(2,1)S(1)} %pad_maximum_fusion.q0), channel_id=1, source_target_pairs={{0,4},{2,6},{4,0},{6,2},{1,5},{3,7},{5,1},{7,3},{8,12},{10,14},{12... | collective-permute-start | bytes 1572872 | tf_op jit(solution)/shard_map/ppermute | solution.py:356
  42.8 14.4 %collective-permute-done.1.w2 = bf16[1024,256]{1,0:T(8,128)(2,1)S(1)} collective-permute-done((bf16[1024,256]{1,0:T(8,128)(2,1)S(1)}, bf16[1024,256]{1,0:T(8,128)(2,1)S(1)}, u32[]{:S(2)}, u32[]{:S(2)}) %collective-permute-start.1) | collective-permute-done | bytes 524320 | tf_op jit(solution)/shard_map/ppermute | solution.py:356
  57.1 2.8 %collective-permute-start.4 = (bf16[2,1024,128]{2,1,0:T(8,128)(2,1)S(1)}, bf16[2,1024,128]{2,1,0:T(8,128)(2,1)}, u32[]{:S(2)}, u32[]{:S(2)}) collective-permute-start(bf16[2,1024,128]{2,1,0:T(8,128)(2,1)S(1)} %pad_maximum_fusion.q0), channel_id=1, source_target_pairs={{0,6},{2,0},{4,2},{6,4},{1,7},{3,1},{5,3},{7,5},{8,14},{10,8},{12,... | collective-permute-start | bytes 1572872 | tf_op jit(solution)/shard_map/ppermute | solution.py:356
  60.5 6.0 %collective-permute-done.w1 = bf16[1024,256]{1,0:T(8,128)(2,1)S(1)} collective-permute-done((bf16[1024,256]{1,0:T(8,128)(2,1)S(1)}, bf16[1024,256]{1,0:T(8,128)(2,1)S(1)}, u32[]{:S(2)}, u32[]{:S(2)}) %collective-permute-start) | collective-permute-done | bytes 524320 | tf_op jit(solution)/shard_map/ppermute | solution.py:356
  67.6 8.1 %grad_gated.1 = (bf16[4,1024,256]{2,1,0:T(8,128)(2,1)}, f32[6,128,1024]{2,1,0:T(8,128)}, bf16[2,128,1024]{2,1,0:T(8,128)(2,1)}) custom-call(s32[4]{0:T(128)} %pad_add_fusion.at, bf16[1024,256]{1,0:T(8,128)(2,1)} %w0.1, bf16[1024,256]{1,0:T(8,128)(2,1)} %copy-done.10, bf16[1024,256]{1,0:T(8,128)(2,1)} %copy-done.9, ...), custom_call_target="tpu_custom_call" | custom-call | tf_op jit(solution)/shard_map/grad_gated/pallas_call | solution.py:270
  75.7 1.2 slice_bitcast_fusion
  77.4 1.7 collective-permute-start.7
  79.1 5.7 %collective-permute-done.8 = bf16[128,1024]{1,0:T(8,128)(2,1)S(1)} collective-permute-done((bf16[128,1024]{1,0:T(8,128)(2,1)S(1)}, bf16[128,1024]{1,0:T(8,128)(2,1)S(1)}, u32[]{:S(2)}, u32[]{:S(2)}) %collective-permute-start.8) | collective-permute-done | bytes 262176 | tf_op jit(solution)/shard_map/ppermute | solution.py:356
  84.7 1.2 collective-permute-done.7
  86.0 1.4 fusion.5
  87.4 3.0 %collective-permute-start.10 = (bf16[128,1024]{1,0:T(8,128)(2,1)S(1)}, bf16[128,1024]{1,0:T(8,128)(2,1)S(1)}, u32[]{:S(2)}, u32[]{:S(2)}) collective-permute-start(bf16[128,1024]{1,0:T(8,128)(2,1)S(1)} %get-tuple-element.59), channel_id=1, source_target_pairs={{0,56},{8,0},{16,8},{24,16},{32,24},{40,32},{48,40},{56,48},{1,57}... | collective-permute-start | bytes 786440 | tf_op jit(solution)/shard_map/ppermute | solution.py:356
  90.4 3.9 %collective-permute-done.10 = bf16[128,1024]{1,0:T(8,128)(2,1)S(1)} collective-permute-done((bf16[128,1024]{1,0:T(8,128)(2,1)S(1)}, bf16[128,1024]{1,0:T(8,128)(2,1)S(1)}, u32[]{:S(2)}, u32[]{:S(2)}) %collective-permute-start.10) | collective-permute-done | bytes 262176 | tf_op jit(solution)/shard_map/ppermute | solution.py:356
  94.3 2.5 %collective-permute-done.9 = bf16[128,1024]{1,0:T(8,128)(2,1)S(1)} collective-permute-done((bf16[128,1024]{1,0:T(8,128)(2,1)S(1)}, bf16[128,1024]{1,0:T(8,128)(2,1)S(1)}, u32[]{:S(2)}, u32[]{:S(2)}) %collective-permute-start.9) | collective-permute-done | bytes 262176 | tf_op jit(solution)/shard_map/ppermute | solution.py:356
  96.9 1.6 collective-permute-start.12
  99.0 4.3 %collective-permute-done.12 = bf16[128,1024]{1,0:T(8,128)(2,1)S(1)} collective-permute-done((bf16[128,1024]{1,0:T(8,128)(2,1)S(1)}, bf16[128,1024]{1,0:T(8,128)(2,1)S(1)}, u32[]{:S(2)}, u32[]{:S(2)}) %collective-permute-start.12) | collective-permute-done | bytes 262176 | tf_op jit(solution)/shard_map/ppermute | solution.py:356
  103.4 3.5 %collective-permute-done.11 = bf16[128,1024]{1,0:T(8,128)(2,1)S(1)} collective-permute-done((bf16[128,1024]{1,0:T(8,128)(2,1)S(1)}, bf16[128,1024]{1,0:T(8,128)(2,1)S(1)}, u32[]{:S(2)}, u32[]{:S(2)}) %collective-permute-start.11) | collective-permute-done | bytes 262176 | tf_op jit(solution)/shard_map/ppermute | solution.py:356
  107.5 6.2 %collective-permute-done.13 = bf16[128,1024]{1,0:T(8,128)(2,1)S(1)} collective-permute-done((bf16[128,1024]{1,0:T(8,128)(2,1)S(1)}, bf16[128,1024]{1,0:T(8,128)(2,1)S(1)}, u32[]{:S(2)}, u32[]{:S(2)}) %collective-permute-start.13) | collective-permute-done | bytes 262176 | tf_op jit(solution)/shard_map/ppermute | solution.py:356
  114.4 4.3 %all-to-all-start.3 = ((bf16[4,32,1024]{2,1,0:T(8,128)(2,1)}), bf16[4,32,1024]{2,1,0:T(8,128)(2,1)S(1)}, u32[]{:S(2)}, u32[]{:S(2)}) async-start(bf16[4,32,1024]{2,1,0:T(8,128)(2,1)} %bitcast.18), calls=%async_computation.3 | async-start | bytes 524288 | tf_op jit(solution)/shard_map/all_to_all | solution.py:412
  119.4 5.9 %conv.1 = (bf16[32,32,128]{2,1,0:T(8,128)(2,1)}, bf16[4,32,1024]{2,1,0:T(8,128)(2,1)}, f32[1024,256]{1,0:T(8,128)}, f32[1024,256]{1,0:T(8,128)}) custom-call(bf16[32,3,32,128]{3,2,1,0:T(8,128)(2,1)} %copy-done, f32[32,128]{1,0:T(8,128)} %broadcast_in_dim.2.skip_ref, bf16[64,64]{1,0:T(8,128)(2,1)} %constant.28.clone.a_ref, ...), custom_call_target="tpu_custom_call" | custom-call | tf_op jit(solution)/shard_map/conv/pallas_call | solution.py:164
  125.4 4.7 %all-to-all-start.5 = ((bf16[4,32,1024]{2,1,0:T(8,128)(2,1)}), bf16[4,32,1024]{2,1,0:T(8,128)(2,1)S(1)}, u32[]{:S(2)}, u32[]{:S(2)}) async-start(bf16[4,32,1024]{2,1,0:T(8,128)(2,1)} %get-tuple-element.51), calls=%async_computation.5 | async-start | bytes 524288 | tf_op jit(solution)/shard_map/all_to_all | solution.py:390
  130.1 7.1 %back.1 = (bf16[32,3,32,128]{3,2,1,0:T(8,128)(2,1)}, f32[32,128]{1,0:T(8,128)}) custom-call(bf16[4,32,1024]{2,1,0:T(8,128)(2,1)} %copy-done.5, bf16[32,3,32,128]{3,2,1,0:T(8,128)(2,1)} %copy-done, bf16[32,32,128]{2,1,0:T(8,128)(2,1)} %get-tuple-element.42.mixed_ref, f32[1024,256]{1,0:T(8,128)} %get-tuple-element.43.sig_ref, ...), custom_call_target="tpu_custom_call" | custom-call | tf_op jit(solution)/shard_map/back/pallas_call | solution.py:181
  137.2 8.4 %all-to-all-start.4 = ((bf16[32,3,32,128]{3,2,1,0:T(8,128)(2,1)}), bf16[32,3,32,128]{3,2,1,0:T(8,128)(2,1)S(1)}, u32[]{:S(2)}, u32[]{:S(2)}) async-start(bf16[32,3,32,128]{3,2,1,0:T(8,128)(2,1)} %get-tuple-element.45), calls=%async_computation.4 | async-start | bytes 1572864 | tf_op jit(solution)/shard_map/all_to_all | solution.py:414
  145.6 1.5 collective-permute-start.17
  147.7 16.7 %collective-permute-done.17.refs_8_ = bf16[128,1024]{1,0:T(8,128)(2,1)S(1)} collective-permute-done((bf16[128,1024]{1,0:T(8,128)(2,1)S(1)}, bf16[128,1024]{1,0:T(8,128)(2,1)S(1)}, u32[]{:S(2)}, u32[]{:S(2)}) %collective-permute-start.17) | collective-permute-done | bytes 262176 | tf_op jit(solution)/shard_map/ppermute | solution.py:356
  165.1 2.7 %collective-permute-start.15 = (bf16[128,1024]{1,0:T(8,128)(2,1)S(1)}, bf16[128,1024]{1,0:T(8,128)(2,1)S(1)}, u32[]{:S(2)}, u32[]{:S(2)}) collective-permute-start(bf16[128,1024]{1,0:T(8,128)(2,1)S(1)} %collective-permute-done.14.refs_1_), channel_id=1, source_target_pairs={{0,56},{8,0},{16,8},{24,16},{32,24},{40,32},{48,40},{56,48},{1,57}... | collective-permute-start | bytes 786440 | tf_op jit(solution)/shard_map/ppermute | solution.py:356
  167.8 6.8 %collective-permute-done.18.refs_7_ = bf16[128,1024]{1,0:T(8,128)(2,1)S(1)} collective-permute-done((bf16[128,1024]{1,0:T(8,128)(2,1)S(1)}, bf16[128,1024]{1,0:T(8,128)(2,1)S(1)}, u32[]{:S(2)}, u32[]{:S(2)}) %collective-permute-start.18) | collective-permute-done | bytes 262176 | tf_op jit(solution)/shard_map/ppermute | solution.py:356
  174.7 3.5 %collective-permute-start.16 = (bf16[128,1024]{1,0:T(8,128)(2,1)S(1)}, bf16[128,1024]{1,0:T(8,128)(2,1)S(1)}, u32[]{:S(2)}, u32[]{:S(2)}) collective-permute-start(bf16[128,1024]{1,0:T(8,128)(2,1)S(1)} %collective-permute-done.15.refs_2_), channel_id=1, source_target_pairs={{0,56},{8,0},{16,8},{24,16},{32,24},{40,32},{48,40},{56,48},{1,57}... | collective-permute-start | bytes 786440 | tf_op jit(solution)/shard_map/ppermute | solution.py:356
  178.2 5.1 %collective-permute-done.19.refs_6_ = bf16[128,1024]{1,0:T(8,128)(2,1)S(1)} collective-permute-done((bf16[128,1024]{1,0:T(8,128)(2,1)S(1)}, bf16[128,1024]{1,0:T(8,128)(2,1)S(1)}, u32[]{:S(2)}, u32[]{:S(2)}) %collective-permute-start.19) | collective-permute-done | bytes 262176 | tf_op jit(solution)/shard_map/ppermute | solution.py:356
  183.5 3.0 %collective-permute-start.21 = (bf16[64,1024]{1,0:T(8,128)(2,1)S(1)}, bf16[64,1024]{1,0:T(8,128)(2,1)S(1)}, u32[]{:S(2)}, u32[]{:S(2)}) collective-permute-start(bf16[64,1024]{1,0:T(8,128)(2,1)S(1)} %slice.41), channel_id=1, source_target_pairs={{0,56},{8,0},{16,8},{24,16},{32,24},{40,32},{48,40},{56,48},{1,57}... | collective-permute-start | bytes 393224 | tf_op jit(solution)/shard_map/ppermute | solution.py:356
  186.5 2.8 %collective-permute-done.20.refs_4_ = bf16[64,1024]{1,0:T(8,128)(2,1)S(1)} collective-permute-done((bf16[64,1024]{1,0:T(8,128)(2,1)S(1)}, bf16[64,1024]{1,0:T(8,128)(2,1)S(1)}, u32[]{:S(2)}, u32[]{:S(2)}) %collective-permute-start.20) | collective-permute-done | bytes 131104 | tf_op jit(solution)/shard_map/ppermute | solution.py:356
  190.0 7.3 %grad_weight.1 = (bf16[1024,256]{1,0:T(8,128)(2,1)}, bf16[1024,256]{1,0:T(8,128)(2,1)}, bf16[1024,256]{1,0:T(8,128)(2,1)}, bf16[1024,256]{1,0:T(8,128)(2,1)}) custom-call(s32[4]{0:T(128)} %pad_add_fusion.at, bf16[128,1024]{1,0:T(8,128)(2,1)} %bitcast.46, bf16[128,1024]{1,0:T(8,128)(2,1)} %copy-done.15, bf16[128,1024]{1,0:T(8,128)(2,1)} %copy-done.17, ...), custom_call_target="tpu_custom_call" | custom-call | tf_op jit(solution)/shard_map/grad_weight/pallas_call | solution.py:314
  197.3 1.3 collective-permute-start.22
  198.6 2.7 %collective-permute-start.23 = (bf16[1024,256]{1,0:T(8,128)(2,1)}, bf16[1024,256]{1,0:T(8,128)(2,1)S(1)}, u32[]{:S(2)}, u32[]{:S(2)}) collective-permute-start(bf16[1024,256]{1,0:T(8,128)(2,1)} %get-tuple-element.55), channel_id=1, source_target_pairs={{0,128},{64,192},{128,0},{192,64},{1,129},{65,193},{129,1},{193,65... | collective-permute-start | bytes 1572872 | tf_op jit(solution)/shard_map/ppermute | solution.py:356
  201.3 1.4 collective-permute-start.24
  203.3 7.6 %collective-permute-done.22.b_ref = bf16[1024,256]{1,0:T(8,128)(2,1)S(1)} collective-permute-done((bf16[1024,256]{1,0:T(8,128)(2,1)}, bf16[1024,256]{1,0:T(8,128)(2,1)S(1)}, u32[]{:S(2)}, u32[]{:S(2)}) %collective-permute-start.22) | collective-permute-done | bytes 524320 | tf_op jit(solution)/shard_map/ppermute | solution.py:356
  210.9 5.6 %collective-permute-done.23.c_ref = bf16[1024,256]{1,0:T(8,128)(2,1)S(1)} collective-permute-done((bf16[1024,256]{1,0:T(8,128)(2,1)}, bf16[1024,256]{1,0:T(8,128)(2,1)S(1)}, u32[]{:S(2)}, u32[]{:S(2)}) %collective-permute-start.23) | collective-permute-done | bytes 524320 | tf_op jit(solution)/shard_map/ppermute | solution.py:356
  217.5 3.1 %weight_sum.1 = f32[4,8,32,256]{3,2,1,0:T(8,128)} custom-call(s32[4]{0:T(128)} %pad_add_fusion.at, bf16[1024,256]{1,0:T(8,128)(2,1)} %get-tuple-element.53.a_ref, bf16[1024,256]{1,0:T(8,128)(2,1)} %copy-done.11, bf16[1024,256]{1,0:T(8,128)(2,1)} %copy-done.12, bf16[1024,256]{1,0:T(8,128)(2,1)} %copy-done.13), custom_call_target="tpu_custom_call" | custom-call | tf_op jit(solution)/shard_map/weight_sum/pallas_call | solution.py:341
  220.6 0.9 copy-done.1
  221.5 2.0 to_rows.1
  (77 shorter events, 9.0 us)
Async XLA Ops:
  0.6 32.7 %copy-start.8 = (bf16[1024,256]{1,0:T(8,128)(2,1)S(1)}, bf16[1024,256]{1,0:T(8,128)(2,1)}, u32[]{:S(2)}) copy-start(bf16[1024,256]{1,0:T(8,128)(2,1)} %w0.1) | copy-start | bytes 1572868
  27.2 33.3 %all-to-all-start.2 = ((bf16[32,3,32,128]{3,2,1,0:T(8,128)(2,1)}), bf16[32,3,32,128]{3,2,1,0:T(8,128)(2,1)S(1)}, u32[]{:S(2)}, u32[]{:S(2)}) async-start(bf16[32,3,32,128]{3,2,1,0:T(8,128)(2,1)} %to_cols.1), calls=%async_computation.2 | async-start | bytes 1572864 | tf_op jit(solution)/shard_map/all_to_all | solution.py:382
  33.3 23.8 %collective-permute-start.1 = (bf16[1024,256]{1,0:T(8,128)(2,1)S(1)}, bf16[1024,256]{1,0:T(8,128)(2,1)S(1)}, u32[]{:S(2)}, u32[]{:S(2)}) collective-permute-start(bf16[1024,256]{1,0:T(8,128)(2,1)S(1)} %copy-done.8), channel_id=1, source_target_pairs={{0,128},{64,192},{128,0},{192,64},{1,129},{65,193},{129,1},{193,65... | collective-permute-start | bytes 1572872 | tf_op jit(solution)/shard_map/ppermute | solution.py:356
  36.4 2.0 collective-permute-start.3
  36.4 30.1 %collective-permute-start = (bf16[1024,256]{1,0:T(8,128)(2,1)S(1)}, bf16[1024,256]{1,0:T(8,128)(2,1)S(1)}, u32[]{:S(2)}, u32[]{:S(2)}) collective-permute-start(bf16[1024,256]{1,0:T(8,128)(2,1)S(1)} %copy-done.8), channel_id=1, source_target_pairs={{0,192},{64,0},{128,64},{192,128},{1,193},{65,1},{129,65},{193,129... | collective-permute-start | bytes 1572872 | tf_op jit(solution)/shard_map/ppermute | solution.py:356
  37.6 29.4 %collective-permute-start.2 = (bf16[1024,256]{1,0:T(8,128)(2,1)S(1)}, bf16[1024,256]{1,0:T(8,128)(2,1)}, u32[]{:S(2)}, u32[]{:S(2)}) collective-permute-start(bf16[1024,256]{1,0:T(8,128)(2,1)S(1)} %copy-done.8), channel_id=1, source_target_pairs={{0,64},{64,128},{128,192},{192,0},{1,65},{65,129},{129,193},{193,1... | collective-permute-start | bytes 1572872 | tf_op jit(solution)/shard_map/ppermute | solution.py:356
  38.5 29.1 %copy-start.3 = (bf16[2,1024,128]{2,1,0:T(8,128)(2,1)}, bf16[2,1024,128]{2,1,0:T(8,128)(2,1)S(1)}, u32[]{:S(2)}) copy-start(bf16[2,1024,128]{2,1,0:T(8,128)(2,1)S(1)} %pad_maximum_fusion.q0) | copy-start | bytes 1572868
  38.5 28.5 %collective-permute-start.6 = (bf16[2,1024,128]{2,1,0:T(8,128)(2,1)S(1)}, bf16[2,1024,128]{2,1,0:T(8,128)(2,1)}, u32[]{:S(2)}, u32[]{:S(2)}) collective-permute-start(bf16[2,1024,128]{2,1,0:T(8,128)(2,1)S(1)} %pad_maximum_fusion.q0), channel_id=1, source_target_pairs={{0,2},{2,4},{4,6},{6,0},{1,3},{3,5},{5,7},{7,1},{8,10},{10,12},{12... | collective-permute-start | bytes 1572872 | tf_op jit(solution)/shard_map/ppermute | solution.py:356
  40.1 26.9 %collective-permute-start.5 = (bf16[2,1024,128]{2,1,0:T(8,128)(2,1)S(1)}, bf16[2,1024,128]{2,1,0:T(8,128)(2,1)}, u32[]{:S(2)}, u32[]{:S(2)}) collective-permute-start(bf16[2,1024,128]{2,1,0:T(8,128)(2,1)S(1)} %pad_maximum_fusion.q0), channel_id=1, source_target_pairs={{0,4},{2,6},{4,0},{6,2},{1,5},{3,7},{5,1},{7,3},{8,12},{10,14},{12... | collective-permute-start | bytes 1572872 | tf_op jit(solution)/shard_map/ppermute | solution.py:356
  57.1 10.5 %copy-start.9 = (bf16[1024,256]{1,0:T(8,128)(2,1)}, bf16[1024,256]{1,0:T(8,128)(2,1)S(1)}, u32[]{:S(2)}) copy-start(bf16[1024,256]{1,0:T(8,128)(2,1)S(1)} %collective-permute-done.1.w2) | copy-start | bytes 1572868
  57.1 10.5 %collective-permute-start.4 = (bf16[2,1024,128]{2,1,0:T(8,128)(2,1)S(1)}, bf16[2,1024,128]{2,1,0:T(8,128)(2,1)}, u32[]{:S(2)}, u32[]{:S(2)}) collective-permute-start(bf16[2,1024,128]{2,1,0:T(8,128)(2,1)S(1)} %pad_maximum_fusion.q0), channel_id=1, source_target_pairs={{0,6},{2,0},{4,2},{6,4},{1,7},{3,1},{5,3},{7,5},{8,14},{10,8},{12,... | collective-permute-start | bytes 1572872 | tf_op jit(solution)/shard_map/ppermute | solution.py:356
  60.5 26.8 %copy-start = (bf16[32,3,32,128]{3,2,1,0:T(8,128)(2,1)}, bf16[32,3,32,128]{3,2,1,0:T(8,128)(2,1)S(1)}, u32[]{:S(2)}) copy-start(bf16[32,3,32,128]{3,2,1,0:T(8,128)(2,1)S(1)} %all-to-all-done.2.in_ref) | copy-start | bytes 2359300
  66.5 1.1 copy-start.10
  75.7 21.0 %copy-start.2 = (f32[6,128,1024]{2,1,0:T(8,128)S(1)}, f32[6,128,1024]{2,1,0:T(8,128)}, u32[]{:S(2)}) copy-start(f32[6,128,1024]{2,1,0:T(8,128)} %get-tuple-element.35) | copy-start | bytes 9437188
  77.0 7.8 %collective-permute-start.8 = (bf16[128,1024]{1,0:T(8,128)(2,1)S(1)}, bf16[128,1024]{1,0:T(8,128)(2,1)S(1)}, u32[]{:S(2)}, u32[]{:S(2)}) collective-permute-start(bf16[128,1024]{1,0:T(8,128)(2,1)S(1)} %get-tuple-element.61), channel_id=1, source_target_pairs={{0,56},{8,0},{16,8},{24,16},{32,24},{40,32},{48,40},{56,48},{1,57}... | collective-permute-start | bytes 786440 | tf_op jit(solution)/shard_map/ppermute | solution.py:356
  77.4 8.6 %collective-permute-start.7 = (bf16[128,1024]{1,0:T(8,128)(2,1)S(1)}, bf16[128,1024]{1,0:T(8,128)(2,1)S(1)}, u32[]{:S(2)}, u32[]{:S(2)}) collective-permute-start(bf16[128,1024]{1,0:T(8,128)(2,1)S(1)} %get-tuple-element.62), channel_id=1, source_target_pairs={{0,8},{8,16},{16,24},{24,32},{32,40},{40,48},{48,56},{56,0},{1,9},... | collective-permute-start | bytes 786440 | tf_op jit(solution)/shard_map/ppermute | solution.py:356
  86.0 32.7 %copy-start.21 = (f32[32]{0:T(128)S(1)}, f32[32]{0:T(128)}, u32[]{:S(2)}) copy-start(f32[32]{0:T(128)} %param.14) | copy-start | bytes 388
  87.4 6.9 %collective-permute-start.10 = (bf16[128,1024]{1,0:T(8,128)(2,1)S(1)}, bf16[128,1024]{1,0:T(8,128)(2,1)S(1)}, u32[]{:S(2)}, u32[]{:S(2)}) collective-permute-start(bf16[128,1024]{1,0:T(8,128)(2,1)S(1)} %get-tuple-element.59), channel_id=1, source_target_pairs={{0,56},{8,0},{16,8},{24,16},{32,24},{40,32},{48,40},{56,48},{1,57}... | collective-permute-start | bytes 786440 | tf_op jit(solution)/shard_map/ppermute | solution.py:356
  90.4 6.4 %collective-permute-start.9 = (bf16[128,1024]{1,0:T(8,128)(2,1)S(1)}, bf16[128,1024]{1,0:T(8,128)(2,1)S(1)}, u32[]{:S(2)}, u32[]{:S(2)}) collective-permute-start(bf16[128,1024]{1,0:T(8,128)(2,1)S(1)} %get-tuple-element.60), channel_id=1, source_target_pairs={{0,8},{8,16},{16,24},{24,32},{32,40},{40,48},{48,56},{56,0},{1,9},... | collective-permute-start | bytes 786440 | tf_op jit(solution)/shard_map/ppermute | solution.py:356
  96.9 6.4 %collective-permute-start.12 = (bf16[128,1024]{1,0:T(8,128)(2,1)S(1)}, bf16[128,1024]{1,0:T(8,128)(2,1)S(1)}, u32[]{:S(2)}, u32[]{:S(2)}) collective-permute-start(bf16[128,1024]{1,0:T(8,128)(2,1)S(1)} %get-tuple-element.57), channel_id=1, source_target_pairs={{0,56},{8,0},{16,8},{24,16},{32,24},{40,32},{48,40},{56,48},{1,57}... | collective-permute-start | bytes 786440 | tf_op jit(solution)/shard_map/ppermute | solution.py:356
  98.5 8.4 %collective-permute-start.11 = (bf16[128,1024]{1,0:T(8,128)(2,1)S(1)}, bf16[128,1024]{1,0:T(8,128)(2,1)S(1)}, u32[]{:S(2)}, u32[]{:S(2)}) collective-permute-start(bf16[128,1024]{1,0:T(8,128)(2,1)S(1)} %get-tuple-element.58), channel_id=1, source_target_pairs={{0,8},{8,16},{16,24},{24,32},{32,40},{40,48},{48,56},{56,0},{1,9},... | collective-permute-start | bytes 786440 | tf_op jit(solution)/shard_map/ppermute | solution.py:356
  107.0 6.6 %collective-permute-start.13 = (bf16[128,1024]{1,0:T(8,128)(2,1)S(1)}, bf16[128,1024]{1,0:T(8,128)(2,1)S(1)}, u32[]{:S(2)}, u32[]{:S(2)}) collective-permute-start(bf16[128,1024]{1,0:T(8,128)(2,1)S(1)} %fusion.2), channel_id=1, source_target_pairs={{0,8},{8,16},{16,24},{24,32},{32,40},{40,48},{48,56},{56,0},{1,9},... | collective-permute-start | bytes 786440 | tf_op jit(solution)/shard_map/ppermute | solution.py:356
  114.4 11.0 %all-to-all-start.3 = ((bf16[4,32,1024]{2,1,0:T(8,128)(2,1)}), bf16[4,32,1024]{2,1,0:T(8,128)(2,1)S(1)}, u32[]{:S(2)}, u32[]{:S(2)}) async-start(bf16[4,32,1024]{2,1,0:T(8,128)(2,1)} %bitcast.18), calls=%async_computation.3 | async-start | bytes 524288 | tf_op jit(solution)/shard_map/all_to_all | solution.py:412
  125.4 4.7 %copy-start.5 = (bf16[4,32,1024]{2,1,0:T(8,128)(2,1)}, bf16[4,32,1024]{2,1,0:T(8,128)(2,1)S(1)}, u32[]{:S(2)}) copy-start(bf16[4,32,1024]{2,1,0:T(8,128)(2,1)S(1)} %all-to-all-done.3.gg_ref) | copy-start | bytes 786436
  125.4 11.8 %all-to-all-start.5 = ((bf16[4,32,1024]{2,1,0:T(8,128)(2,1)}), bf16[4,32,1024]{2,1,0:T(8,128)(2,1)S(1)}, u32[]{:S(2)}, u32[]{:S(2)}) async-start(bf16[4,32,1024]{2,1,0:T(8,128)(2,1)} %get-tuple-element.51), calls=%async_computation.5 | async-start | bytes 524288 | tf_op jit(solution)/shard_map/all_to_all | solution.py:390
  137.2 52.2 %copy-start.4 = (bf16[4,32,1024]{2,1,0:T(8,128)(2,1)}, bf16[4,32,1024]{2,1,0:T(8,128)(2,1)S(1)}, u32[]{:S(2)}) copy-start(bf16[4,32,1024]{2,1,0:T(8,128)(2,1)S(1)} %all-to-all-done.5) | copy-start | bytes 786436
  137.2 65.5 %copy-start.20 = (f32[32,128]{1,0:T(8,128)S(1)}, f32[32,128]{1,0:T(8,128)}, u32[]{:S(2)}) copy-start(f32[32,128]{1,0:T(8,128)} %get-tuple-element.49) | copy-start | bytes 49156
  137.2 83.4 %all-to-all-start.4 = ((bf16[32,3,32,128]{3,2,1,0:T(8,128)(2,1)}), bf16[32,3,32,128]{3,2,1,0:T(8,128)(2,1)S(1)}, u32[]{:S(2)}, u32[]{:S(2)}) async-start(bf16[32,3,32,128]{3,2,1,0:T(8,128)(2,1)} %get-tuple-element.45), calls=%async_computation.4 | async-start | bytes 1572864 | tf_op jit(solution)/shard_map/all_to_all | solution.py:414
  145.6 18.8 %collective-permute-start.17 = (bf16[128,1024]{1,0:T(8,128)(2,1)S(1)}, bf16[128,1024]{1,0:T(8,128)(2,1)S(1)}, u32[]{:S(2)}, u32[]{:S(2)}) collective-permute-start(bf16[128,1024]{1,0:T(8,128)(2,1)S(1)} %bitcast.44), channel_id=1, source_target_pairs={{0,8},{8,16},{16,24},{24,32},{32,40},{40,48},{48,56},{56,0},{1,9},... | collective-permute-start | bytes 786440 | tf_op jit(solution)/shard_map/ppermute | solution.py:356
  147.1 18.0 %collective-permute-start.14 = (bf16[128,1024]{1,0:T(8,128)(2,1)S(1)}, bf16[128,1024]{1,0:T(8,128)(2,1)S(1)}, u32[]{:S(2)}, u32[]{:S(2)}) collective-permute-start(bf16[128,1024]{1,0:T(8,128)(2,1)S(1)} %bitcast.45), channel_id=1, source_target_pairs={{0,56},{8,0},{16,8},{24,16},{32,24},{40,32},{48,40},{56,48},{1,57}... | collective-permute-start | bytes 786440 | tf_op jit(solution)/shard_map/ppermute | solution.py:356
  164.4 24.9 %copy-start.14 = (bf16[128,1024]{1,0:T(8,128)(2,1)}, bf16[128,1024]{1,0:T(8,128)(2,1)S(1)}, u32[]{:S(2)}) copy-start(bf16[128,1024]{1,0:T(8,128)(2,1)S(1)} %collective-permute-done.17.refs_8_) | copy-start | bytes 786436
  164.4 10.2 %collective-permute-start.18 = (bf16[128,1024]{1,0:T(8,128)(2,1)S(1)}, bf16[128,1024]{1,0:T(8,128)(2,1)S(1)}, u32[]{:S(2)}, u32[]{:S(2)}) collective-permute-start(bf16[128,1024]{1,0:T(8,128)(2,1)S(1)} %collective-permute-done.17.refs_8_), channel_id=1, source_target_pairs={{0,8},{8,16},{16,24},{24,32},{32,40},{40,48},{48,56},{56,0},{1,9},... | collective-permute-start | bytes 786440 | tf_op jit(solution)/shard_map/ppermute | solution.py:356
  165.1 24.2 %copy-start.15 = (bf16[128,1024]{1,0:T(8,128)(2,1)}, bf16[128,1024]{1,0:T(8,128)(2,1)S(1)}, u32[]{:S(2)}) copy-start(bf16[128,1024]{1,0:T(8,128)(2,1)S(1)} %collective-permute-done.14.refs_1_) | copy-start | bytes 786436
  165.1 9.5 %collective-permute-start.15 = (bf16[128,1024]{1,0:T(8,128)(2,1)S(1)}, bf16[128,1024]{1,0:T(8,128)(2,1)S(1)}, u32[]{:S(2)}, u32[]{:S(2)}) collective-permute-start(bf16[128,1024]{1,0:T(8,128)(2,1)S(1)} %collective-permute-done.14.refs_1_), channel_id=1, source_target_pairs={{0,56},{8,0},{16,8},{24,16},{32,24},{40,32},{48,40},{56,48},{1,57}... | collective-permute-start | bytes 786440 | tf_op jit(solution)/shard_map/ppermute | solution.py:356
  174.6 14.7 %copy-start.16 = (bf16[128,1024]{1,0:T(8,128)(2,1)}, bf16[128,1024]{1,0:T(8,128)(2,1)S(1)}, u32[]{:S(2)}) copy-start(bf16[128,1024]{1,0:T(8,128)(2,1)S(1)} %collective-permute-done.18.refs_7_) | copy-start | bytes 786436
  174.6 8.7 %collective-permute-start.19 = (bf16[128,1024]{1,0:T(8,128)(2,1)S(1)}, bf16[128,1024]{1,0:T(8,128)(2,1)S(1)}, u32[]{:S(2)}, u32[]{:S(2)}) collective-permute-start(bf16[128,1024]{1,0:T(8,128)(2,1)S(1)} %collective-permute-done.18.refs_7_), channel_id=1, source_target_pairs={{0,8},{8,16},{16,24},{24,32},{32,40},{40,48},{48,56},{56,0},{1,9},... | collective-permute-start | bytes 786440 | tf_op jit(solution)/shard_map/ppermute | solution.py:356
  174.7 14.7 %copy-start.17 = (bf16[128,1024]{1,0:T(8,128)(2,1)}, bf16[128,1024]{1,0:T(8,128)(2,1)S(1)}, u32[]{:S(2)}) copy-start(bf16[128,1024]{1,0:T(8,128)(2,1)S(1)} %collective-permute-done.15.refs_2_) | copy-start | bytes 786436
  174.7 8.8 %collective-permute-start.16 = (bf16[128,1024]{1,0:T(8,128)(2,1)S(1)}, bf16[128,1024]{1,0:T(8,128)(2,1)S(1)}, u32[]{:S(2)}, u32[]{:S(2)}) collective-permute-start(bf16[128,1024]{1,0:T(8,128)(2,1)S(1)} %collective-permute-done.15.refs_2_), channel_id=1, source_target_pairs={{0,56},{8,0},{16,8},{24,16},{32,24},{40,32},{48,40},{56,48},{1,57}... | collective-permute-start | bytes 786440 | tf_op jit(solution)/shard_map/ppermute | solution.py:356
  183.3 6.0 %copy-start.6 = (bf16[128,1024]{1,0:T(8,128)(2,1)}, bf16[128,1024]{1,0:T(8,128)(2,1)S(1)}, u32[]{:S(2)}) copy-start(bf16[128,1024]{1,0:T(8,128)(2,1)S(1)} %collective-permute-done.19.refs_6_) | copy-start | bytes 786436
  183.3 6.0 %collective-permute-start.20 = (bf16[64,1024]{1,0:T(8,128)(2,1)S(1)}, bf16[64,1024]{1,0:T(8,128)(2,1)S(1)}, u32[]{:S(2)}, u32[]{:S(2)}) collective-permute-start(bf16[64,1024]{1,0:T(8,128)(2,1)S(1)} %slice.40), channel_id=1, source_target_pairs={{0,8},{8,16},{16,24},{24,32},{32,40},{40,48},{48,56},{56,0},{1,9},... | collective-permute-start | bytes 393224 | tf_op jit(solution)/shard_map/ppermute | solution.py:356
  183.4 5.9 %copy-start.7 = (bf16[128,1024]{1,0:T(8,128)(2,1)}, bf16[128,1024]{1,0:T(8,128)(2,1)S(1)}, u32[]{:S(2)}) copy-start(bf16[128,1024]{1,0:T(8,128)(2,1)S(1)} %collective-permute-done.16.refs_3_) | copy-start | bytes 786436
  183.5 5.9 %collective-permute-start.21 = (bf16[64,1024]{1,0:T(8,128)(2,1)S(1)}, bf16[64,1024]{1,0:T(8,128)(2,1)S(1)}, u32[]{:S(2)}, u32[]{:S(2)}) collective-permute-start(bf16[64,1024]{1,0:T(8,128)(2,1)S(1)} %slice.41), channel_id=1, source_target_pairs={{0,56},{8,0},{16,8},{24,16},{32,24},{40,32},{48,40},{56,48},{1,57}... | collective-permute-start | bytes 393224 | tf_op jit(solution)/shard_map/ppermute | solution.py:356
  197.3 13.6 %collective-permute-start.22 = (bf16[1024,256]{1,0:T(8,128)(2,1)}, bf16[1024,256]{1,0:T(8,128)(2,1)S(1)}, u32[]{:S(2)}, u32[]{:S(2)}) collective-permute-start(bf16[1024,256]{1,0:T(8,128)(2,1)} %get-tuple-element.54), channel_id=1, source_target_pairs={{0,64},{64,128},{128,192},{192,0},{1,65},{65,129},{129,193},{193,1... | collective-permute-start | bytes 1572872 | tf_op jit(solution)/shard_map/ppermute | solution.py:356
  198.6 18.0 %collective-permute-start.23 = (bf16[1024,256]{1,0:T(8,128)(2,1)}, bf16[1024,256]{1,0:T(8,128)(2,1)S(1)}, u32[]{:S(2)}, u32[]{:S(2)}) collective-permute-start(bf16[1024,256]{1,0:T(8,128)(2,1)} %get-tuple-element.55), channel_id=1, source_target_pairs={{0,128},{64,192},{128,0},{192,64},{1,129},{65,193},{129,1},{193,65... | collective-permute-start | bytes 1572872 | tf_op jit(solution)/shard_map/ppermute | solution.py:356
  201.3 15.3 %collective-permute-start.24 = (bf16[1024,256]{1,0:T(8,128)(2,1)}, bf16[1024,256]{1,0:T(8,128)(2,1)S(1)}, u32[]{:S(2)}, u32[]{:S(2)}) collective-permute-start(bf16[1024,256]{1,0:T(8,128)(2,1)} %get-tuple-element.56), channel_id=1, source_target_pairs={{0,192},{64,0},{128,64},{192,128},{1,193},{65,1},{129,65},{193,129... | collective-permute-start | bytes 1572872 | tf_op jit(solution)/shard_map/ppermute | solution.py:356
  210.9 5.8 %copy-start.11 = (bf16[1024,256]{1,0:T(8,128)(2,1)}, bf16[1024,256]{1,0:T(8,128)(2,1)S(1)}, u32[]{:S(2)}) copy-start(bf16[1024,256]{1,0:T(8,128)(2,1)S(1)} %collective-permute-done.22.b_ref) | copy-start | bytes 1572868
  216.6 0.8 copy-start.13
  220.6 0.9 copy-start.1
  (3 other events, 2.2 us)
where the time goes:
time: 227 us; the launch traced here: 223 us
  waiting for transfers between devices  93.8 us (41%)
  starting transfers between devices  60.8 us (27%)
  Pallas kernels  35.5 us (16%)
  blocking collectives  23 us (10%)
  local copies, waits for them, and re-layouts  5.75 us (3%)
  other arithmetic  3.66 us (2%)
    ppermute x25, waiting for transfers between devices, shift(): lax.ppermute(value, axis, [(i, (i + by) % count) for i in range(count)])  93.6 us
    ppermute x25, starting transfers between devices, shift(): lax.ppermute(value, axis, [(i, (i + by) % count) for i in range(count)])  37.4 us
    all_to_all x1, blocking collectives, ordered(): lax.all_to_all(pieces, 'z', split_axis=0, concat_axis=0, tiled=True)  19.1 us
    all_to_all x1, starting transfers between devices, ordered(): lax.all_to_all(outs, seq, split_axis=0, concat_axis=0, tiled=True)  8.37 us
    pallas_call x1, Pallas kernels, grad_gated_part(): pl.pallas_call(gated_kernel, grid_spec=pltpu.PrefetchScalarGridSpec(num_s...  8.11 us
    pallas_call x1, Pallas kernels, grad_weight_part(): pl.pallas_call(weight_kernel, grid_spec=pltpu.PrefetchScalarGridSpec(num_...  7.29 us
    pallas_call x1, Pallas kernels, back(): pl.pallas_call(back_kernel, grid=(STEPS,), in_specs=[WIDE, PACK, PLAIN, S...  7.08 us
    all_to_all x1, starting transfers between devices, ordered(): cols = lax.all_to_all(cols, seq, split_axis=0, concat_axis=0, tiled=True)  6.09 us
  transfers between devices with their start and end apart: 29, of which 19 were waited for; matrix products, arithmetic and copies ran while one was open for 1% of the time, Pallas kernels for 10%

commit v1 on v0

--- a/solution.py
+++ b/solution.py
@@ -237,57 +237,78 @@
 SENT = (4, 5)
 
 
-def gated_kernel(at, w0, w1, w2, w3, q0, q1, q2, q3, cot_ref, own_ref, sent_ref, acc):
-    y, z, x, core = at[0], at[1], at[2], at[3]
-    for s, q in enumerate((q0, q1, q2, q3)):
-        mine, other = q[0], q[1]
+def product(at, offsets, ws, cot_ref):
+    y, z = at[0], at[1]
+    total = None
+    for r, w in enumerate(ws):
+        rows = [
+            w[pl.ds(pl.multiple_of((b * NZ + (z + offset) % NZ) * CL, CL), CL), :]
+            for offset in offsets
+            for b in range(NY)
+        ]
+        part = lax.dot_general(
+            jnp.concatenate(rows, axis=0),
+            cot_ref[(y + r) % NY],
+            (((1,), (1,)), ((), ())),
+            preferred_element_type=f32,
+        )
+        total = part if total is None else total + part
+    return total
+
+
+def opening_kernel(at, w0, w1, w2, w3, m0, m1, m2, m3, o0, o1, o2, o3, cot_ref, up_ref, down_ref):
+    x, core = at[2], at[3]
+    for s, (m, o) in enumerate(((m0, o0), (m1, o1), (m2, o2), (m3, o3))):
+        mine, other = m[...], o[...]
         first = jnp.where(core == 0, mine, other)
         second = jnp.where(core == 0, other, mine)
         cot_ref[(x + s) % NX] = jnp.concatenate([first, second], axis=1)
-    total = None
-    for r, w in enumerate((w0, w1, w2, w3)):
-        part = lax.dot_general(
-            w[...], cot_ref[(y + r) % NY], (((1,), (1,)), ((), ())), preferred_element_type=f32
-        )
-        total = part if total is None else total + part
-    acc[...] = total
-
-    def block(offset, b):
-        return acc[pl.ds(pl.multiple_of((b * NZ + (z + offset) % NZ) * CL, CL), CL), :]
-
-    for b in range(NY):
-        rows = slice(b * CL, (b + 1) * CL)
-        for i, offset in enumerate(OWN):
-            own_ref[i, rows, :] = block(offset, b)
-        for i, offset in enumerate(SENT):
-            sent_ref[i, rows, :] = block(offset, b).astype(bf16)
-
-
-def grad_gated_part(at, ws, qs):
+    total = product(at, SENT, (w0, w1, w2, w3), cot_ref)
+    up_ref[...] = total[: NY * CL].astype(bf16)
+    down_ref[...] = total[NY * CL :].astype(bf16)
+
+
+def opening_part(at, ws, mine, other):
     c, f = ws[0].shape
-    t = qs[0].shape[1]
+    t = mine[0].shape[0]
     span = 2 * TOK
-    return pl.pallas_call(
-        gated_kernel,
+    chain = pl.BlockSpec((NY * CL, span), lambda i, at: (0, i))
+    return pl.pallas_call(
+        opening_kernel,
         grid_spec=pltpu.PrefetchScalarGridSpec(
             num_scalar_prefetch=1,
             grid=(t // span,),
             in_specs=[pl.BlockSpec((c, f), lambda i, at: (0, 0))] * NY
-            + [pl.BlockSpec((NH, span, f // NH), lambda i, at: (0, i, 0))] * NX,
-            out_specs=[
-                pl.BlockSpec((NX, span, f), lambda i, at: (0, i, 0)),
-                pl.BlockSpec((len(OWN), NY * CL, span), lambda i, at: (0, 0, i)),
-                pl.BlockSpec((len(SENT), NY * CL, span), lambda i, at: (0, 0, i)),
-            ],
-            scratch_shapes=[pltpu.VMEM((c, span), f32)],
+            + [pl.BlockSpec((span, f // NH), lambda i, at: (i, 0))] * (2 * NX),
+            out_specs=[pl.BlockSpec((NX, span, f), lambda i, at: (0, i, 0)), chain, chain],
         ),
-        out_shape=[
-            SHAPE((NX, t, f), bf16),
-            SHAPE((len(OWN), NY * CL, t), f32),
-            SHAPE((len(SENT), NY * CL, t), bf16),
-        ],
-        name="grad_gated",
-    )(at, *ws, *qs)
+        out_shape=[SHAPE((NX, t, f), bf16), SHAPE((NY * CL, t), bf16), SHAPE((NY * CL, t), bf16)],
+        name="opening",
+    )(at, *ws, *mine, *other)
+
+
+def staying_kernel(at, w0, w1, w2, w3, cot_ref, own_ref):
+    total = product(at, OWN, (w0, w1, w2, w3), cot_ref)
+    for i in range(len(OWN)):
+        own_ref[i] = total[i * NY * CL : (i + 1) * NY * CL]
+
+
+def staying_part(at, ws, cot_all):
+    c, f = ws[0].shape
+    t = cot_all.shape[1]
+    span = 2 * TOK
+    return pl.pallas_call(
+        staying_kernel,
+        grid_spec=pltpu.PrefetchScalarGridSpec(
+            num_scalar_prefetch=1,
+            grid=(t // span,),
+            in_specs=[pl.BlockSpec((c, f), lambda i, at: (0, 0))] * NY
+            + [pl.BlockSpec((NX, span, f), lambda i, at: (0, i, 0))],
+            out_specs=pl.BlockSpec((len(OWN), NY * CL, span), lambda i, at: (0, 0, i)),
+        ),
+        out_shape=SHAPE((len(OWN), NY * CL, t), f32),
+        name="staying",
+    )(at, *ws, cot_all)
 
 
 def weight_kernel(at, *refs):
@@ -368,27 +389,28 @@
     tabs = [jnp.asarray(t) for t in tables()]
     seq = ("y", "z")
     at = jnp.stack([lax.axis_index(a) for a in ("y", "z", "x", "core")]).astype(jnp.int32)
-    ws = [w_out, shift(w_out, "y", -1), shift(w_out, "y", 2), shift(w_out, "y", 1)]
 
     pieces = cotangent.reshape(TOK, NZ // NH, NH, TOK).transpose(2, 1, 0, 3)
     pieces = lax.all_to_all(pieces, "core", split_axis=0, concat_axis=0, tiled=True)
-    pieces = pieces.reshape(NZ, TOK, TOK)
-    pieces = lax.all_to_all(pieces, "z", split_axis=0, concat_axis=0, tiled=True)
-    pieces = pieces.reshape(NZ * TOK, TOK)
-    chip = jnp.stack([pieces, shift(pieces, "core", 1)])
-    chips = [chip, shift(chip, "x", -1), shift(chip, "x", 2), shift(chip, "x", 1)]
+    piece = lax.all_to_all(pieces.reshape(NZ, TOK, TOK), "z", split_axis=0, concat_axis=0, tiled=True)
+    piece = piece.reshape(NZ * TOK, TOK)
 
     cols = to_cols(after(signal, pieces), filter_taps, gate_values)
     cols = lax.all_to_all(cols, seq, split_axis=0, concat_axis=0, tiled=True)
-
-    cot_all, own, sent = grad_gated_part(after(at, cols), ws, chips)
-    up = shift(sent[0], "z", 1)
-    down = shift(sent[1], "z", -1)
-
-    skip = jnp.broadcast_to(after(skip_gain, own)[:, None], (CL, TOK))
+    ws = [w_out, shift(w_out, "y", -1), shift(w_out, "y", 2), shift(w_out, "y", 1)]
+    skip = jnp.broadcast_to(skip_gain[:, None], (CL, TOK))
+
+    other = shift(piece, "core", 1)
+    mine = [piece, shift(piece, "x", -1), shift(piece, "x", 2), shift(piece, "x", 1)]
     mixed, gated, sig_spec, tap_spec = conv(cols, skip, tabs)
     gated = lax.all_to_all(gated, "y", split_axis=0, concat_axis=0, tiled=True)
     gated = gated.reshape(NY * CL, NZ * TOK)
+    other = [other] + [shift(m, "core", 1) for m in mine[1:]]
+
+    cot_all, up, down = opening_part(at, ws, mine, other)
+    up = shift(up, "z", 1)
+    down = shift(down, "z", -1)
+    own = staying_part(at, ws, cot_all)
 
     for i in range(2):
         up, down = lax.optimization_barrier((up, down))
@@ -412,11 +434,10 @@
     grad_gated = lax.all_to_all(part, "y", split_axis=0, concat_axis=0, tiled=True)
     outs, skip_sum = back(grad_gated, cols, mixed, sig_spec, tap_spec, skip, tabs)
     outs_rows = lax.all_to_all(outs, seq, split_axis=0, concat_axis=0, tiled=True)
-    grad_input, grad_filter, grad_gate = to_rows(outs_rows)
-
-    kept, up1, up2, up3 = grad_weight_part(after(at, skip_sum), ring, cot_all)
+    kept, up1, up2, up3 = grad_weight_part(at, ring, cot_all)
     moved = [shift(up1, "y", 1), shift(up2, "y", 2), shift(up3, "y", -1)]
     weight = weight_sum(at, [kept] + moved)
+    grad_input, grad_filter, grad_gate = to_rows(outs_rows)
     return (grad_input, grad_gate, grad_filter, jnp.sum(skip_sum, axis=1), weight)
 
 

time: 227 us -> 227 us (level)
  blocking collectives: 23 us -> 3.94 us
  starting transfers between devices: 60.8 us -> 72.8 us
  Pallas kernels: 35.5 us -> 40.1 us
    all_to_all x1 -> x0, blocking collectives: 19.1 us -> none  [ordered(): lax.all_to_all(pieces, 'z', split_axis=0, concat_axis=0, tiled=True)]
    all_to_all x0 -> x1, waiting for transfers between devices: none -> 10.1 us  [ordered(): lax.all_to_all(pieces.reshape(NZ, TOK, TOK), 'z', split_axis=0, concat_ax...]
    ppermute x25 -> x28, waiting for transfers between devices: 93.6 us -> 84.4 us  [shift(): lax.ppermute(value, axis, [(i, (i + by) % count) for i in range(count)])]
    all_to_all x0 -> x1, starting transfers between devices: none -> 8.57 us  [ordered(): lax.all_to_all(pieces.reshape(NZ, TOK, TOK), 'z', split_axis=0, concat_ax...]
    pallas_call x1 -> x2, Pallas kernels: 8.11 us -> 12.7 us  [the longest x1 6.56 us: staying_part(): pl.pallas_call(staying_kernel, grid_spec=pltpu.PrefetchScalarGridSpec(num...]
    all_to_all x1, starting transfers between devices: 6.09 us -> 8.93 us  [ordered(): cols = lax.all_to_all(cols, seq, split_axis=0, concat_axis=0, tiled=True)]
    all_to_all x1, starting transfers between devices: 8.37 us -> 10.9 us  [ordered(): lax.all_to_all(outs, seq, split_axis=0, concat_axis=0, tiled=True)]
    ppermute x25 -> x28, starting transfers between devices: 37.4 us -> 35.6 us  [shift(): lax.ppermute(value, axis, [(i, (i + by) % count) for i in range(count)])]
  transfers between devices with their start and end apart: 29 -> 33, of which waited for: 19 -> 19; matrix products, arithmetic and copies ran while one was open for 1% -> 3% of each run, Pallas kernels for 10% -> 14%
where the time goes in v1:
time: 227 us; the launch traced here: 224 us
  waiting for transfers between devices  94.6 us (42%)
  starting transfers between devices  72.8 us (32%)
  Pallas kernels  40.1 us (18%)
  local copies, waits for them, and re-layouts  6.05 us (3%)
  other arithmetic  5.65 us (2%)
  blocking collectives  3.94 us (2%)
    ppermute x28, waiting for transfers between devices, shift(): lax.ppermute(value, axis, [(i, (i + by) % count) for i in range(count)])  84.4 us
    ppermute x28, starting transfers between devices, shift(): lax.ppermute(value, axis, [(i, (i + by) % count) for i in range(count)])  35.6 us
    all_to_all x1, starting transfers between devices, ordered(): lax.all_to_all(outs, seq, split_axis=0, concat_axis=0, tiled=True)  10.9 us
    all_to_all x1, waiting for transfers between devices, ordered(): lax.all_to_all(pieces.reshape(NZ, TOK, TOK), 'z', split_axis=0, concat_ax...  10.1 us
    all_to_all x1, starting transfers between devices, ordered(): cols = lax.all_to_all(cols, seq, split_axis=0, concat_axis=0, tiled=True)  8.93 us
    all_to_all x1, starting transfers between devices, ordered(): lax.all_to_all(pieces.reshape(NZ, TOK, TOK), 'z', split_axis=0, concat_ax...  8.57 us
    pallas_call x1, Pallas kernels, grad_weight_part(): pl.pallas_call(weight_kernel, grid_spec=pltpu.PrefetchScalarGridSpec(num_...  7.28 us
    pallas_call x1, Pallas kernels, back(): pl.pallas_call(back_kernel, grid=(STEPS,), in_specs=[WIDE, PACK, PLAIN, S...  7.06 us
  transfers between devices with their start and end apart: 33, of which 19 were waited for; matrix products, arithmetic and copies ran while one was open for 3% of the time, Pallas kernels for 14%

profile of v1, /device:TPU:32, one launch (start us, length us, event | category | flops | bytes accessed | tf_op | source)
XLA Modules:
  0.0 224.1 jit_solution(16239945643370579374)
XLA Ops:
  0.6 3.1 %collective-permute-start = (bf16[1024,256]{1,0:T(8,128)(2,1)}, bf16[1024,256]{1,0:T(8,128)(2,1)S(1)}, u32[]{:S(2)}, u32[]{:S(2)}) collective-permute-start(bf16[1024,256]{1,0:T(8,128)(2,1)} %w0.3), channel_id=1, source_target_pairs={{0,192},{64,0},{128,64},{192,128},{1,193},{65,1},{129,65},{193,129... | collective-permute-start | bytes 1572872 | tf_op jit(solution)/shard_map/ppermute | solution.py:377
  3.7 1.1 copy.17
  5.1 3.9 %all_to_all.30 = bf16[2,4,128,128]{3,1,2,0:T(4,128)(2,1)S(1)} all-to-all(bf16[2,4,128,128]{3,1,2,0:T(4,128)(2,1)S(1)} %copy.18), channel_id=1, replica_groups=mesh['y'=4,'z'=8,'x'=4,'core'=2] {'core'}, dimensions={0} | all-to-all | bytes 524288 | tf_op jit(solution)/shard_map/all_to_all | solution.py:394
  9.7 8.6 %all-to-all-start.1 = ((bf16[8,128,128]{2,1,0:T(8,128)(2,1)}), bf16[8,128,128]{2,1,0:T(8,128)(2,1)S(1)}, u32[]{:S(2)}, u32[]{:S(2)}) async-start(bf16[8,128,128]{2,1,0:T(8,128)(2,1)} %bitcast.6), calls=%async_computation.1 | async-start | bytes 524288 | tf_op jit(solution)/shard_map/all_to_all | solution.py:395
  18.9 10.1 %all-to-all-done.1 = bf16[8,128,128]{2,1,0:T(8,128)(2,1)S(1)} async-done(((bf16[8,128,128]{2,1,0:T(8,128)(2,1)}), bf16[8,128,128]{2,1,0:T(8,128)(2,1)S(1)}, u32[]{:S(2)}, u32[]{:S(2)}) %all-to-all-start.1) | async-done | bytes 262176 | tf_op jit(solution)/shard_map/all_to_all | solution.py:395
  29.0 2.8 %collective-permute-start.3 = (bf16[1024,128]{1,0:T(8,128)(2,1)S(1)}, bf16[1024,128]{1,0:T(8,128)(2,1)S(1)}, u32[]{:S(2)}, u32[]{:S(2)}) collective-permute-start(bf16[1024,128]{1,0:T(8,128)(2,1)S(1)} %bitcast.50), channel_id=1, source_target_pairs={{0,6},{2,0},{4,2},{6,4},{1,7},{3,1},{5,3},{7,5},{8,14},{10,8},{12,... | collective-permute-start | bytes 786440 | tf_op jit(solution)/shard_map/ppermute | solution.py:377
  33.5 1.3 collective-permute-done.1.w2
  34.8 5.7 %collective-permute-done.3.m1 = bf16[1024,128]{1,0:T(8,128)(2,1)S(1)} collective-permute-done((bf16[1024,128]{1,0:T(8,128)(2,1)S(1)}, bf16[1024,128]{1,0:T(8,128)(2,1)S(1)}, u32[]{:S(2)}, u32[]{:S(2)}) %collective-permute-start.3) | collective-permute-done | bytes 262176 | tf_op jit(solution)/shard_map/ppermute | solution.py:377
  40.5 0.9 collective-permute-done.4.m2
  41.5 2.8 %collective-permute-done.5.m3 = bf16[1024,128]{1,0:T(8,128)(2,1)S(1)} collective-permute-done((bf16[1024,128]{1,0:T(8,128)(2,1)S(1)}, bf16[1024,128]{1,0:T(8,128)(2,1)S(1)}, u32[]{:S(2)}, u32[]{:S(2)}) %collective-permute-start.5) | collective-permute-done | bytes 262176 | tf_op jit(solution)/shard_map/ppermute | solution.py:377
  46.2 6.2 %opening.1 = (bf16[4,1024,256]{2,1,0:T(8,128)(2,1)}, bf16[128,1024]{1,0:T(8,128)(2,1)}, bf16[128,1024]{1,0:T(8,128)(2,1)}) custom-call(s32[4]{0:T(128)} %pad_add_fusion.at, bf16[1024,256]{1,0:T(8,128)(2,1)} %w0.3, bf16[1024,256]{1,0:T(8,128)(2,1)} %copy-done.2, bf16[1024,256]{1,0:T(8,128)(2,1)} %copy-done.3, bf16[1024,256]{1,0:T(8,128)(2,1)} %copy-done.4, ...), custom_call_target="tpu_custom_call" | custom-call | tf_op jit(solution)/shard_map/opening/pallas_call | solution.py:276
  52.4 1.1 collective-permute-start.10
  53.5 1.8 collective-permute-start.11
  55.2 6.6 %staying.1 = f32[6,128,1024]{2,1,0:T(8,128)} custom-call(s32[4]{0:T(128)} %pad_add_fusion.at, bf16[1024,256]{1,0:T(8,128)(2,1)} %w0.3, bf16[1024,256]{1,0:T(8,128)(2,1)} %copy-done.2, bf16[1024,256]{1,0:T(8,128)(2,1)} %copy-done.3, bf16[1024,256]{1,0:T(8,128)(2,1)} %copy-done.4, bf16[4,1024,256]{2,1,0:T(8,128)(2,1)} %get-tuple-element.31.cot_ref.refs_9_), custom_call_target="tpu_custom_call" | custom-call | tf_op jit(solution)/shard_map/staying/pallas_call | solution.py:300
  62.3 2.4 %fusion.10 = (bf16[128,1024]{1,0:T(8,128)(2,1)}, bf16[128,1024]{1,0:T(8,128)(2,1)}) fusion(f32[6,128,1024]{2,1,0:T(8,128)} %staying.1, bf16[128,1024]{1,0:T(8,128)(2,1)} %collective-permute-done.11, bf16[128,1024]{1,0:T(8,128)(2,1)S(1)} %collective-permute-done.10), kind=kLoop, calls=%fused_computation.15 | loop fusion | flops 786432 | bytes 2097152 | tf_op jit(solution)/shard_map/convert_element_type | solution.py:381
  64.7 1.3 collective-permute-start.12
  66.0 1.6 collective-permute-start.13
  67.6 2.1 to_cols.1
  69.7 8.9 %all-to-all-start.3 = ((bf16[32,3,32,128]{3,2,1,0:T(8,128)(2,1)}), bf16[32,3,32,128]{3,2,1,0:T(8,128)(2,1)}, u32[]{:S(2)}, u32[]{:S(2)}) async-start(bf16[32,3,32,128]{3,2,1,0:T(8,128)(2,1)} %to_cols.1), calls=%async_computation.3 | async-start | bytes 1572864 | tf_op jit(solution)/shard_map/all_to_all | solution.py:399
  78.7 1.1 fusion.6
  79.8 1.7 collective-permute-start.14
  82.0 18.5 %collective-permute-done.14 = bf16[128,1024]{1,0:T(8,128)(2,1)S(1)} collective-permute-done((bf16[128,1024]{1,0:T(8,128)(2,1)S(1)}, bf16[128,1024]{1,0:T(8,128)(2,1)S(1)}, u32[]{:S(2)}, u32[]{:S(2)}) %collective-permute-start.14) | collective-permute-done | bytes 262176 | tf_op jit(solution)/shard_map/ppermute | solution.py:377
  100.5 1.2 collective-permute-done.15
  101.8 1.6 collective-permute-start.16
  103.4 5.9 %collective-permute-done.16 = bf16[128,1024]{1,0:T(8,128)(2,1)S(1)} collective-permute-done((bf16[128,1024]{1,0:T(8,128)(2,1)S(1)}, bf16[128,1024]{1,0:T(8,128)(2,1)S(1)}, u32[]{:S(2)}, u32[]{:S(2)}) %collective-permute-start.16) | collective-permute-done | bytes 262176 | tf_op jit(solution)/shard_map/ppermute | solution.py:377
  110.1 4.1 %all-to-all-start.2 = ((bf16[4,32,1024]{2,1,0:T(8,128)(2,1)}), bf16[4,32,1024]{2,1,0:T(8,128)(2,1)S(1)}, u32[]{:S(2)}, u32[]{:S(2)}) async-start(bf16[4,32,1024]{2,1,0:T(8,128)(2,1)} %bitcast.14), calls=%async_computation.2 | async-start | bytes 524288 | tf_op jit(solution)/shard_map/all_to_all | solution.py:434
  114.9 5.9 %conv.1 = (bf16[32,32,128]{2,1,0:T(8,128)(2,1)}, bf16[4,32,1024]{2,1,0:T(8,128)(2,1)}, f32[1024,256]{1,0:T(8,128)}, f32[1024,256]{1,0:T(8,128)}) custom-call(bf16[32,3,32,128]{3,2,1,0:T(8,128)(2,1)} %all-to-all-done.3.in_ref, f32[32,128]{1,0:T(8,128)} %broadcast_in_dim.2.skip_ref, bf16[64,64]{1,0:T(8,128)(2,1)} %constant.28.clone.a_ref, ...), custom_call_target="tpu_custom_call" | custom-call | tf_op jit(solution)/shard_map/conv/pallas_call | solution.py:164
  120.9 4.7 %all-to-all-start.5 = ((bf16[4,32,1024]{2,1,0:T(8,128)(2,1)}), bf16[4,32,1024]{2,1,0:T(8,128)(2,1)S(1)}, u32[]{:S(2)}, u32[]{:S(2)}) async-start(bf16[4,32,1024]{2,1,0:T(8,128)(2,1)} %get-tuple-element.46), calls=%async_computation.5 | async-start | bytes 524288 | tf_op jit(solution)/shard_map/all_to_all | solution.py:406
  125.6 7.1 %back.1 = (bf16[32,3,32,128]{3,2,1,0:T(8,128)(2,1)}, f32[32,128]{1,0:T(8,128)}) custom-call(bf16[4,32,1024]{2,1,0:T(8,128)(2,1)} %copy-done.7, bf16[32,3,32,128]{3,2,1,0:T(8,128)(2,1)} %all-to-all-done.3.in_ref, bf16[32,32,128]{2,1,0:T(8,128)(2,1)} %get-tuple-element.38.mixed_ref, f32[1024,256]{1,0:T(8,128)} %get-tuple-element.39.sig_ref, ...), custom_call_target="tpu_custom_call" | custom-call | tf_op jit(solution)/shard_map/back/pallas_call | solution.py:181
  132.7 10.9 %all-to-all-start.4 = ((bf16[32,3,32,128]{3,2,1,0:T(8,128)(2,1)}), bf16[32,3,32,128]{3,2,1,0:T(8,128)(2,1)S(1)}, u32[]{:S(2)}, u32[]{:S(2)}) async-start(bf16[32,3,32,128]{3,2,1,0:T(8,128)(2,1)} %get-tuple-element.41), calls=%async_computation.4 | async-start | bytes 1572864 | tf_op jit(solution)/shard_map/all_to_all | solution.py:436
  143.6 1.5 collective-permute-start.20
  145.7 18.5 %collective-permute-done.20.refs_8_ = bf16[128,1024]{1,0:T(8,128)(2,1)S(1)} collective-permute-done((bf16[128,1024]{1,0:T(8,128)(2,1)S(1)}, bf16[128,1024]{1,0:T(8,128)(2,1)S(1)}, u32[]{:S(2)}, u32[]{:S(2)}) %collective-permute-start.20) | collective-permute-done | bytes 262176 | tf_op jit(solution)/shard_map/ppermute | solution.py:377
  164.2 1.5 collective-permute-start.21
  165.6 1.5 collective-permute-start.18
  167.1 4.4 %collective-permute-done.21.refs_7_ = bf16[128,1024]{1,0:T(8,128)(2,1)S(1)} collective-permute-done((bf16[128,1024]{1,0:T(8,128)(2,1)S(1)}, bf16[128,1024]{1,0:T(8,128)(2,1)S(1)}, u32[]{:S(2)}, u32[]{:S(2)}) %collective-permute-start.21) | collective-permute-done | bytes 262176 | tf_op jit(solution)/shard_map/ppermute | solution.py:377
  172.2 2.4 %collective-permute-start.19 = (bf16[128,1024]{1,0:T(8,128)(2,1)S(1)}, bf16[128,1024]{1,0:T(8,128)(2,1)S(1)}, u32[]{:S(2)}, u32[]{:S(2)}) collective-permute-start(bf16[128,1024]{1,0:T(8,128)(2,1)S(1)} %collective-permute-done.18.refs_2_), channel_id=1, source_target_pairs={{0,56},{8,0},{16,8},{24,16},{32,24},{40,32},{48,40},{56,48},{1,57}... | collective-permute-start | bytes 786440 | tf_op jit(solution)/shard_map/ppermute | solution.py:377
  174.7 4.3 %collective-permute-done.22.refs_6_ = bf16[128,1024]{1,0:T(8,128)(2,1)S(1)} collective-permute-done((bf16[128,1024]{1,0:T(8,128)(2,1)S(1)}, bf16[128,1024]{1,0:T(8,128)(2,1)S(1)}, u32[]{:S(2)}, u32[]{:S(2)}) %collective-permute-start.22) | collective-permute-done | bytes 262176 | tf_op jit(solution)/shard_map/ppermute | solution.py:377
  179.3 3.7 %collective-permute-start.24 = (bf16[64,1024]{1,0:T(8,128)(2,1)S(1)}, bf16[64,1024]{1,0:T(8,128)(2,1)S(1)}, u32[]{:S(2)}, u32[]{:S(2)}) collective-permute-start(bf16[64,1024]{1,0:T(8,128)(2,1)S(1)} %slice.39), channel_id=1, source_target_pairs={{0,56},{8,0},{16,8},{24,16},{32,24},{40,32},{48,40},{56,48},{1,57}... | collective-permute-start | bytes 393224 | tf_op jit(solution)/shard_map/ppermute | solution.py:377
  183.0 2.6 %collective-permute-done.23.refs_4_ = bf16[64,1024]{1,0:T(8,128)(2,1)S(1)} collective-permute-done((bf16[64,1024]{1,0:T(8,128)(2,1)S(1)}, bf16[64,1024]{1,0:T(8,128)(2,1)S(1)}, u32[]{:S(2)}, u32[]{:S(2)}) %collective-permute-start.23) | collective-permute-done | bytes 131104 | tf_op jit(solution)/shard_map/ppermute | solution.py:377
  186.9 7.3 %grad_weight.1 = (bf16[1024,256]{1,0:T(8,128)(2,1)}, bf16[1024,256]{1,0:T(8,128)(2,1)}, bf16[1024,256]{1,0:T(8,128)(2,1)}, bf16[1024,256]{1,0:T(8,128)(2,1)}) custom-call(s32[4]{0:T(128)} %pad_add_fusion.at, bf16[128,1024]{1,0:T(8,128)(2,1)} %bitcast.57, bf16[128,1024]{1,0:T(8,128)(2,1)} %copy-done.20, bf16[128,1024]{1,0:T(8,128)(2,1)} %copy-done.22, ...), custom_call_target="tpu_custom_call" | custom-call | tf_op jit(solution)/shard_map/grad_weight/pallas_call | solution.py:335
  194.2 1.5 collective-permute-start.25
  195.6 2.8 %collective-permute-start.26 = (bf16[1024,256]{1,0:T(8,128)(2,1)}, bf16[1024,256]{1,0:T(8,128)(2,1)S(1)}, u32[]{:S(2)}, u32[]{:S(2)}) collective-permute-start(bf16[1024,256]{1,0:T(8,128)(2,1)} %get-tuple-element.49), channel_id=1, source_target_pairs={{0,128},{64,192},{128,0},{192,64},{1,129},{65,193},{129,1},{193,65... | collective-permute-start | bytes 1572872 | tf_op jit(solution)/shard_map/ppermute | solution.py:377
  198.4 1.4 collective-permute-start.27
  200.4 9.2 %collective-permute-done.25.b_ref = bf16[1024,256]{1,0:T(8,128)(2,1)S(1)} collective-permute-done((bf16[1024,256]{1,0:T(8,128)(2,1)}, bf16[1024,256]{1,0:T(8,128)(2,1)S(1)}, u32[]{:S(2)}, u32[]{:S(2)}) %collective-permute-start.25) | collective-permute-done | bytes 524320 | tf_op jit(solution)/shard_map/ppermute | solution.py:377
  209.6 7.5 %collective-permute-done.26.c_ref = bf16[1024,256]{1,0:T(8,128)(2,1)S(1)} collective-permute-done((bf16[1024,256]{1,0:T(8,128)(2,1)}, bf16[1024,256]{1,0:T(8,128)(2,1)S(1)}, u32[]{:S(2)}, u32[]{:S(2)}) %collective-permute-start.26) | collective-permute-done | bytes 524320 | tf_op jit(solution)/shard_map/ppermute | solution.py:377
  218.1 3.1 %weight_sum.1 = f32[4,8,32,256]{3,2,1,0:T(8,128)} custom-call(s32[4]{0:T(128)} %pad_add_fusion.at, bf16[1024,256]{1,0:T(8,128)(2,1)} %get-tuple-element.47.a_ref, bf16[1024,256]{1,0:T(8,128)(2,1)} %copy-done.10, bf16[1024,256]{1,0:T(8,128)(2,1)} %copy-done.11, bf16[1024,256]{1,0:T(8,128)(2,1)} %copy-done.12), custom_call_target="tpu_custom_call" | custom-call | tf_op jit(solution)/shard_map/weight_sum/pallas_call | solution.py:362
  221.2 0.9 copy-done.1
  222.1 2.0 to_rows.1
  (93 shorter events, 12.4 us)
Async XLA Ops:
  0.6 32.0 %collective-permute-start = (bf16[1024,256]{1,0:T(8,128)(2,1)}, bf16[1024,256]{1,0:T(8,128)(2,1)S(1)}, u32[]{:S(2)}, u32[]{:S(2)}) collective-permute-start(bf16[1024,256]{1,0:T(8,128)(2,1)} %w0.3), channel_id=1, source_target_pairs={{0,192},{64,0},{128,64},{192,128},{1,193},{65,1},{129,65},{193,129... | collective-permute-start | bytes 1572872 | tf_op jit(solution)/shard_map/ppermute | solution.py:377
  9.7 19.3 %all-to-all-start.1 = ((bf16[8,128,128]{2,1,0:T(8,128)(2,1)}), bf16[8,128,128]{2,1,0:T(8,128)(2,1)S(1)}, u32[]{:S(2)}, u32[]{:S(2)}) async-start(bf16[8,128,128]{2,1,0:T(8,128)(2,1)} %bitcast.6), calls=%async_computation.1 | async-start | bytes 524288 | tf_op jit(solution)/shard_map/all_to_all | solution.py:395
  18.3 16.5 %collective-permute-start.1 = (bf16[1024,256]{1,0:T(8,128)(2,1)}, bf16[1024,256]{1,0:T(8,128)(2,1)S(1)}, u32[]{:S(2)}, u32[]{:S(2)}) collective-permute-start(bf16[1024,256]{1,0:T(8,128)(2,1)} %w0.3), channel_id=1, source_target_pairs={{0,128},{64,192},{128,0},{192,64},{1,129},{65,193},{129,1},{193,65... | collective-permute-start | bytes 1572872 | tf_op jit(solution)/shard_map/ppermute | solution.py:377
  29.0 16.9 %copy-start.5 = (bf16[8,128,128]{2,1,0:T(8,128)(2,1)}, bf16[8,128,128]{2,1,0:T(8,128)(2,1)S(1)}, u32[]{:S(2)}) copy-start(bf16[8,128,128]{2,1,0:T(8,128)(2,1)S(1)} %all-to-all-done.1) | copy-start | bytes 786436
  29.0 11.5 %collective-permute-start.3 = (bf16[1024,128]{1,0:T(8,128)(2,1)S(1)}, bf16[1024,128]{1,0:T(8,128)(2,1)S(1)}, u32[]{:S(2)}, u32[]{:S(2)}) collective-permute-start(bf16[1024,128]{1,0:T(8,128)(2,1)S(1)} %bitcast.50), channel_id=1, source_target_pairs={{0,6},{2,0},{4,2},{6,4},{1,7},{3,1},{5,3},{7,5},{8,14},{10,8},{12,... | collective-permute-start | bytes 786440 | tf_op jit(solution)/shard_map/ppermute | solution.py:377
  31.8 13.3 %collective-permute-start.2 = (bf16[1024,256]{1,0:T(8,128)(2,1)}, bf16[1024,256]{1,0:T(8,128)(2,1)S(1)}, u32[]{:S(2)}, u32[]{:S(2)}) collective-permute-start(bf16[1024,256]{1,0:T(8,128)(2,1)} %w0.3), channel_id=1, source_target_pairs={{0,64},{64,128},{128,192},{192,0},{1,65},{65,129},{129,193},{193,1... | collective-permute-start | bytes 1572872 | tf_op jit(solution)/shard_map/ppermute | solution.py:377
  31.8 9.7 %collective-permute-start.4 = (bf16[1024,128]{1,0:T(8,128)(2,1)S(1)}, bf16[1024,128]{1,0:T(8,128)(2,1)S(1)}, u32[]{:S(2)}, u32[]{:S(2)}) collective-permute-start(bf16[1024,128]{1,0:T(8,128)(2,1)S(1)} %bitcast.51), channel_id=1, source_target_pairs={{0,4},{2,6},{4,0},{6,2},{1,5},{3,7},{5,1},{7,3},{8,12},{10,14},{12... | collective-permute-start | bytes 786440 | tf_op jit(solution)/shard_map/ppermute | solution.py:377
  32.6 13.3 %copy-start.2 = (bf16[1024,256]{1,0:T(8,128)(2,1)}, bf16[1024,256]{1,0:T(8,128)(2,1)S(1)}, u32[]{:S(2)}) copy-start(bf16[1024,256]{1,0:T(8,128)(2,1)S(1)} %collective-permute-done.w1) | copy-start | bytes 1572868
  32.6 11.6 %collective-permute-start.5 = (bf16[1024,128]{1,0:T(8,128)(2,1)S(1)}, bf16[1024,128]{1,0:T(8,128)(2,1)S(1)}, u32[]{:S(2)}, u32[]{:S(2)}) collective-permute-start(bf16[1024,128]{1,0:T(8,128)(2,1)S(1)} %bitcast.52), channel_id=1, source_target_pairs={{0,2},{2,4},{4,6},{6,0},{1,3},{3,5},{5,7},{7,1},{8,10},{10,12},{12... | collective-permute-start | bytes 786440 | tf_op jit(solution)/shard_map/ppermute | solution.py:377
  34.8 11.1 %copy-start.3 = (bf16[1024,256]{1,0:T(8,128)(2,1)}, bf16[1024,256]{1,0:T(8,128)(2,1)S(1)}, u32[]{:S(2)}) copy-start(bf16[1024,256]{1,0:T(8,128)(2,1)S(1)} %collective-permute-done.1.w2) | copy-start | bytes 1572868
  34.8 10.3 %collective-permute-start.6 = (bf16[1024,128]{1,0:T(8,128)(2,1)S(1)}, bf16[1024,128]{1,0:T(8,128)(2,1)S(1)}, u32[]{:S(2)}, u32[]{:S(2)}) collective-permute-start(bf16[1024,128]{1,0:T(8,128)(2,1)S(1)} %bitcast.53), channel_id=1, source_target_pairs={{0,1},{1,0},{2,3},{3,2},{4,5},{5,4},{6,7},{7,6},{8,9},{9,8},{10,11... | collective-permute-start | bytes 786440 | tf_op jit(solution)/shard_map/ppermute | solution.py:377
  40.5 5.4 %copy-start.13 = (bf16[1024,128]{1,0:T(8,128)(2,1)}, bf16[1024,128]{1,0:T(8,128)(2,1)S(1)}, u32[]{:S(2)}) copy-start(bf16[1024,128]{1,0:T(8,128)(2,1)S(1)} %collective-permute-done.3.m1) | copy-start | bytes 786436
  40.5 4.6 %collective-permute-start.7 = (bf16[1024,128]{1,0:T(8,128)(2,1)S(1)}, bf16[1024,128]{1,0:T(8,128)(2,1)S(1)}, u32[]{:S(2)}, u32[]{:S(2)}) collective-permute-start(bf16[1024,128]{1,0:T(8,128)(2,1)S(1)} %collective-permute-done.3.m1), channel_id=1, source_target_pairs={{0,1},{1,0},{2,3},{3,2},{4,5},{5,4},{6,7},{7,6},{8,9},{9,8},{10,11... | collective-permute-start | bytes 786440 | tf_op jit(solution)/shard_map/ppermute | solution.py:377
  41.5 3.7 %collective-permute-start.8 = (bf16[1024,128]{1,0:T(8,128)(2,1)S(1)}, bf16[1024,128]{1,0:T(8,128)(2,1)S(1)}, u32[]{:S(2)}, u32[]{:S(2)}) collective-permute-start(bf16[1024,128]{1,0:T(8,128)(2,1)S(1)} %collective-permute-done.4.m2), channel_id=1, source_target_pairs={{0,1},{1,0},{2,3},{3,2},{4,5},{5,4},{6,7},{7,6},{8,9},{9,8},{10,11... | collective-permute-start | bytes 786440 | tf_op jit(solution)/shard_map/ppermute | solution.py:377
  44.2 1.7 collective-permute-start.9
  52.4 9.9 %collective-permute-start.10 = (bf16[128,1024]{1,0:T(8,128)(2,1)}, bf16[128,1024]{1,0:T(8,128)(2,1)S(1)}, u32[]{:S(2)}, u32[]{:S(2)}) collective-permute-start(bf16[128,1024]{1,0:T(8,128)(2,1)} %get-tuple-element.28), channel_id=1, source_target_pairs={{0,8},{8,16},{16,24},{24,32},{32,40},{40,48},{48,56},{56,0},{1,9},... | collective-permute-start | bytes 786440 | tf_op jit(solution)/shard_map/ppermute | solution.py:377
  53.5 8.8 %collective-permute-start.11 = (bf16[128,1024]{1,0:T(8,128)(2,1)}, bf16[128,1024]{1,0:T(8,128)(2,1)}, u32[]{:S(2)}, u32[]{:S(2)}) collective-permute-start(bf16[128,1024]{1,0:T(8,128)(2,1)} %get-tuple-element.29), channel_id=1, source_target_pairs={{0,56},{8,0},{16,8},{24,16},{32,24},{40,32},{48,40},{56,48},{1,57}... | collective-permute-start | bytes 786440 | tf_op jit(solution)/shard_map/ppermute | solution.py:377
  61.8 16.8 %copy-start = (f32[6,128,1024]{2,1,0:T(8,128)S(1)}, f32[6,128,1024]{2,1,0:T(8,128)}, u32[]{:S(2)}) copy-start(f32[6,128,1024]{2,1,0:T(8,128)} %staying.1) | copy-start | bytes 9437188
  64.7 13.9 %collective-permute-start.12 = (bf16[128,1024]{1,0:T(8,128)(2,1)}, bf16[128,1024]{1,0:T(8,128)(2,1)S(1)}, u32[]{:S(2)}, u32[]{:S(2)}) collective-permute-start(bf16[128,1024]{1,0:T(8,128)(2,1)} %get-tuple-element.54), channel_id=1, source_target_pairs={{0,8},{8,16},{16,24},{24,32},{32,40},{40,48},{48,56},{56,0},{1,9},... | collective-permute-start | bytes 786440 | tf_op jit(solution)/shard_map/ppermute | solution.py:377
  66.0 12.6 %collective-permute-start.13 = (bf16[128,1024]{1,0:T(8,128)(2,1)}, bf16[128,1024]{1,0:T(8,128)(2,1)}, u32[]{:S(2)}, u32[]{:S(2)}) collective-permute-start(bf16[128,1024]{1,0:T(8,128)(2,1)} %get-tuple-element.53), channel_id=1, source_target_pairs={{0,56},{8,0},{16,8},{24,16},{32,24},{40,32},{48,40},{56,48},{1,57}... | collective-permute-start | bytes 786440 | tf_op jit(solution)/shard_map/ppermute | solution.py:377
  69.7 44.6 %copy-start.26 = (f32[32]{0:T(128)S(1)}, f32[32]{0:T(128)}, u32[]{:S(2)}) copy-start(f32[32]{0:T(128)} %param.14) | copy-start | bytes 388
  69.7 40.4 %all-to-all-start.3 = ((bf16[32,3,32,128]{3,2,1,0:T(8,128)(2,1)}), bf16[32,3,32,128]{3,2,1,0:T(8,128)(2,1)}, u32[]{:S(2)}, u32[]{:S(2)}) async-start(bf16[32,3,32,128]{3,2,1,0:T(8,128)(2,1)} %to_cols.1), calls=%async_computation.3 | async-start | bytes 1572864 | tf_op jit(solution)/shard_map/all_to_all | solution.py:399
  79.8 20.8 %collective-permute-start.14 = (bf16[128,1024]{1,0:T(8,128)(2,1)S(1)}, bf16[128,1024]{1,0:T(8,128)(2,1)S(1)}, u32[]{:S(2)}, u32[]{:S(2)}) collective-permute-start(bf16[128,1024]{1,0:T(8,128)(2,1)S(1)} %get-tuple-element.52), channel_id=1, source_target_pairs={{0,8},{8,16},{16,24},{24,32},{32,40},{40,48},{48,56},{56,0},{1,9},... | collective-permute-start | bytes 786440 | tf_op jit(solution)/shard_map/ppermute | solution.py:377
  81.5 20.2 %collective-permute-start.15 = (bf16[128,1024]{1,0:T(8,128)(2,1)S(1)}, bf16[128,1024]{1,0:T(8,128)(2,1)S(1)}, u32[]{:S(2)}, u32[]{:S(2)}) collective-permute-start(bf16[128,1024]{1,0:T(8,128)(2,1)S(1)} %get-tuple-element.51), channel_id=1, source_target_pairs={{0,56},{8,0},{16,8},{24,16},{32,24},{40,32},{48,40},{56,48},{1,57}... | collective-permute-start | bytes 786440 | tf_op jit(solution)/shard_map/ppermute | solution.py:377
  101.8 7.5 %collective-permute-start.16 = (bf16[128,1024]{1,0:T(8,128)(2,1)S(1)}, bf16[128,1024]{1,0:T(8,128)(2,1)S(1)}, u32[]{:S(2)}, u32[]{:S(2)}) collective-permute-start(bf16[128,1024]{1,0:T(8,128)(2,1)S(1)} %fusion.4), channel_id=1, source_target_pairs={{0,8},{8,16},{16,24},{24,32},{32,40},{40,48},{48,56},{56,0},{1,9},... | collective-permute-start | bytes 786440 | tf_op jit(solution)/shard_map/ppermute | solution.py:377
  110.1 10.8 %all-to-all-start.2 = ((bf16[4,32,1024]{2,1,0:T(8,128)(2,1)}), bf16[4,32,1024]{2,1,0:T(8,128)(2,1)S(1)}, u32[]{:S(2)}, u32[]{:S(2)}) async-start(bf16[4,32,1024]{2,1,0:T(8,128)(2,1)} %bitcast.14), calls=%async_computation.2 | async-start | bytes 524288 | tf_op jit(solution)/shard_map/all_to_all | solution.py:434
  120.9 11.7 %all-to-all-start.5 = ((bf16[4,32,1024]{2,1,0:T(8,128)(2,1)}), bf16[4,32,1024]{2,1,0:T(8,128)(2,1)S(1)}, u32[]{:S(2)}, u32[]{:S(2)}) async-start(bf16[4,32,1024]{2,1,0:T(8,128)(2,1)} %get-tuple-element.46), calls=%async_computation.5 | async-start | bytes 524288 | tf_op jit(solution)/shard_map/all_to_all | solution.py:406
  132.7 53.0 %copy-start.6 = (bf16[4,32,1024]{2,1,0:T(8,128)(2,1)}, bf16[4,32,1024]{2,1,0:T(8,128)(2,1)S(1)}, u32[]{:S(2)}) copy-start(bf16[4,32,1024]{2,1,0:T(8,128)(2,1)S(1)} %all-to-all-done.5) | copy-start | bytes 786436
  132.7 67.1 %copy-start.25 = (f32[32,128]{1,0:T(8,128)S(1)}, f32[32,128]{1,0:T(8,128)}, u32[]{:S(2)}) copy-start(f32[32,128]{1,0:T(8,128)} %get-tuple-element.45) | copy-start | bytes 49156
  132.7 88.5 %all-to-all-start.4 = ((bf16[32,3,32,128]{3,2,1,0:T(8,128)(2,1)}), bf16[32,3,32,128]{3,2,1,0:T(8,128)(2,1)S(1)}, u32[]{:S(2)}, u32[]{:S(2)}) async-start(bf16[32,3,32,128]{3,2,1,0:T(8,128)(2,1)} %get-tuple-element.41), calls=%async_computation.4 | async-start | bytes 1572864 | tf_op jit(solution)/shard_map/all_to_all | solution.py:436
  143.6 20.6 %collective-permute-start.20 = (bf16[128,1024]{1,0:T(8,128)(2,1)S(1)}, bf16[128,1024]{1,0:T(8,128)(2,1)S(1)}, u32[]{:S(2)}, u32[]{:S(2)}) collective-permute-start(bf16[128,1024]{1,0:T(8,128)(2,1)S(1)} %bitcast.55), channel_id=1, source_target_pairs={{0,8},{8,16},{16,24},{24,32},{32,40},{40,48},{48,56},{56,0},{1,9},... | collective-permute-start | bytes 786440 | tf_op jit(solution)/shard_map/ppermute | solution.py:377
  145.1 20.5 %collective-permute-start.17 = (bf16[128,1024]{1,0:T(8,128)(2,1)S(1)}, bf16[128,1024]{1,0:T(8,128)(2,1)S(1)}, u32[]{:S(2)}, u32[]{:S(2)}) collective-permute-start(bf16[128,1024]{1,0:T(8,128)(2,1)S(1)} %bitcast.56), channel_id=1, source_target_pairs={{0,56},{8,0},{16,8},{24,16},{32,24},{40,32},{48,40},{56,48},{1,57}... | collective-permute-start | bytes 786440 | tf_op jit(solution)/shard_map/ppermute | solution.py:377
  164.2 21.6 %copy-start.18 = (bf16[128,1024]{1,0:T(8,128)(2,1)}, bf16[128,1024]{1,0:T(8,128)(2,1)S(1)}, u32[]{:S(2)}) copy-start(bf16[128,1024]{1,0:T(8,128)(2,1)S(1)} %collective-permute-done.20.refs_8_) | copy-start | bytes 786436
  164.2 7.3 %collective-permute-start.21 = (bf16[128,1024]{1,0:T(8,128)(2,1)S(1)}, bf16[128,1024]{1,0:T(8,128)(2,1)S(1)}, u32[]{:S(2)}, u32[]{:S(2)}) collective-permute-start(bf16[128,1024]{1,0:T(8,128)(2,1)S(1)} %collective-permute-done.20.refs_8_), channel_id=1, source_target_pairs={{0,8},{8,16},{16,24},{24,32},{32,40},{40,48},{48,56},{56,0},{1,9},... | collective-permute-start | bytes 786440 | tf_op jit(solution)/shard_map/ppermute | solution.py:377
  165.6 20.1 %copy-start.20 = (bf16[128,1024]{1,0:T(8,128)(2,1)}, bf16[128,1024]{1,0:T(8,128)(2,1)S(1)}, u32[]{:S(2)}) copy-start(bf16[128,1024]{1,0:T(8,128)(2,1)S(1)} %collective-permute-done.17.refs_1_) | copy-start | bytes 786436
  165.6 6.6 %collective-permute-start.18 = (bf16[128,1024]{1,0:T(8,128)(2,1)S(1)}, bf16[128,1024]{1,0:T(8,128)(2,1)S(1)}, u32[]{:S(2)}, u32[]{:S(2)}) collective-permute-start(bf16[128,1024]{1,0:T(8,128)(2,1)S(1)} %collective-permute-done.17.refs_1_), channel_id=1, source_target_pairs={{0,56},{8,0},{16,8},{24,16},{32,24},{40,32},{48,40},{56,48},{1,57}... | collective-permute-start | bytes 786440 | tf_op jit(solution)/shard_map/ppermute | solution.py:377
  171.5 14.2 %copy-start.21 = (bf16[128,1024]{1,0:T(8,128)(2,1)}, bf16[128,1024]{1,0:T(8,128)(2,1)S(1)}, u32[]{:S(2)}) copy-start(bf16[128,1024]{1,0:T(8,128)(2,1)S(1)} %collective-permute-done.21.refs_7_) | copy-start | bytes 786436
  171.5 7.5 %collective-permute-start.22 = (bf16[128,1024]{1,0:T(8,128)(2,1)S(1)}, bf16[128,1024]{1,0:T(8,128)(2,1)S(1)}, u32[]{:S(2)}, u32[]{:S(2)}) collective-permute-start(bf16[128,1024]{1,0:T(8,128)(2,1)S(1)} %collective-permute-done.21.refs_7_), channel_id=1, source_target_pairs={{0,8},{8,16},{16,24},{24,32},{32,40},{40,48},{48,56},{56,0},{1,9},... | collective-permute-start | bytes 786440 | tf_op jit(solution)/shard_map/ppermute | solution.py:377
  172.2 13.5 %copy-start.22 = (bf16[128,1024]{1,0:T(8,128)(2,1)}, bf16[128,1024]{1,0:T(8,128)(2,1)S(1)}, u32[]{:S(2)}) copy-start(bf16[128,1024]{1,0:T(8,128)(2,1)S(1)} %collective-permute-done.18.refs_2_) | copy-start | bytes 786436
  172.2 7.1 %collective-permute-start.19 = (bf16[128,1024]{1,0:T(8,128)(2,1)S(1)}, bf16[128,1024]{1,0:T(8,128)(2,1)S(1)}, u32[]{:S(2)}, u32[]{:S(2)}) collective-permute-start(bf16[128,1024]{1,0:T(8,128)(2,1)S(1)} %collective-permute-done.18.refs_2_), channel_id=1, source_target_pairs={{0,56},{8,0},{16,8},{24,16},{32,24},{40,32},{48,40},{56,48},{1,57}... | collective-permute-start | bytes 786440 | tf_op jit(solution)/shard_map/ppermute | solution.py:377
  179.0 6.7 %copy-start.8 = (bf16[128,1024]{1,0:T(8,128)(2,1)}, bf16[128,1024]{1,0:T(8,128)(2,1)S(1)}, u32[]{:S(2)}) copy-start(bf16[128,1024]{1,0:T(8,128)(2,1)S(1)} %collective-permute-done.22.refs_6_) | copy-start | bytes 786436
  179.0 6.5 %collective-permute-start.23 = (bf16[64,1024]{1,0:T(8,128)(2,1)S(1)}, bf16[64,1024]{1,0:T(8,128)(2,1)S(1)}, u32[]{:S(2)}, u32[]{:S(2)}) collective-permute-start(bf16[64,1024]{1,0:T(8,128)(2,1)S(1)} %slice.38), channel_id=1, source_target_pairs={{0,8},{8,16},{16,24},{24,32},{32,40},{40,48},{48,56},{56,0},{1,9},... | collective-permute-start | bytes 393224 | tf_op jit(solution)/shard_map/ppermute | solution.py:377
  179.3 6.5 %copy-start.9 = (bf16[128,1024]{1,0:T(8,128)(2,1)}, bf16[128,1024]{1,0:T(8,128)(2,1)S(1)}, u32[]{:S(2)}) copy-start(bf16[128,1024]{1,0:T(8,128)(2,1)S(1)} %collective-permute-done.19.refs_3_) | copy-start | bytes 786436
  179.3 6.4 %collective-permute-start.24 = (bf16[64,1024]{1,0:T(8,128)(2,1)S(1)}, bf16[64,1024]{1,0:T(8,128)(2,1)S(1)}, u32[]{:S(2)}, u32[]{:S(2)}) collective-permute-start(bf16[64,1024]{1,0:T(8,128)(2,1)S(1)} %slice.39), channel_id=1, source_target_pairs={{0,56},{8,0},{16,8},{24,16},{32,24},{40,32},{48,40},{56,48},{1,57}... | collective-permute-start | bytes 393224 | tf_op jit(solution)/shard_map/ppermute | solution.py:377
  194.2 15.5 %collective-permute-start.25 = (bf16[1024,256]{1,0:T(8,128)(2,1)}, bf16[1024,256]{1,0:T(8,128)(2,1)S(1)}, u32[]{:S(2)}, u32[]{:S(2)}) collective-permute-start(bf16[1024,256]{1,0:T(8,128)(2,1)} %get-tuple-element.48), channel_id=1, source_target_pairs={{0,64},{64,128},{128,192},{192,0},{1,65},{65,129},{129,193},{193,1... | collective-permute-start | bytes 1572872 | tf_op jit(solution)/shard_map/ppermute | solution.py:377
  195.6 21.4 %collective-permute-start.26 = (bf16[1024,256]{1,0:T(8,128)(2,1)}, bf16[1024,256]{1,0:T(8,128)(2,1)S(1)}, u32[]{:S(2)}, u32[]{:S(2)}) collective-permute-start(bf16[1024,256]{1,0:T(8,128)(2,1)} %get-tuple-element.49), channel_id=1, source_target_pairs={{0,128},{64,192},{128,0},{192,64},{1,129},{65,193},{129,1},{193,65... | collective-permute-start | bytes 1572872 | tf_op jit(solution)/shard_map/ppermute | solution.py:377
  198.4 18.7 %collective-permute-start.27 = (bf16[1024,256]{1,0:T(8,128)(2,1)}, bf16[1024,256]{1,0:T(8,128)(2,1)S(1)}, u32[]{:S(2)}, u32[]{:S(2)}) collective-permute-start(bf16[1024,256]{1,0:T(8,128)(2,1)} %get-tuple-element.50), channel_id=1, source_target_pairs={{0,192},{64,0},{128,64},{192,128},{1,193},{65,1},{129,65},{193,129... | collective-permute-start | bytes 1572872 | tf_op jit(solution)/shard_map/ppermute | solution.py:377
  209.6 7.5 %copy-start.10 = (bf16[1024,256]{1,0:T(8,128)(2,1)}, bf16[1024,256]{1,0:T(8,128)(2,1)S(1)}, u32[]{:S(2)}) copy-start(bf16[1024,256]{1,0:T(8,128)(2,1)S(1)} %collective-permute-done.25.b_ref) | copy-start | bytes 1572868
  (12 other events, 18.6 us)

commit v2 on v1

--- a/solution.py
+++ b/solution.py
@@ -312,7 +312,7 @@
 
 
 def weight_kernel(at, *refs):
-    pieces, cot_ref, outs, gated = refs[: NZ + 1], refs[NZ + 1], refs[NZ + 2 : -1], refs[-1]
+    pieces, cot_ref, outs, gated = refs[:NZ], refs[NZ], refs[NZ + 1 : -1], refs[-1]
     step = pl.program_id(0)
 
     @pl.when(step == 0)
@@ -372,6 +372,57 @@
     )(at, *parts).reshape(c, f)
 
 
+def cut_kernel(at, *refs):
+    for i in range(NZ):
+        refs[NZ + i][...] = refs[i][...]
+
+
+def cut(at, cotangent):
+    block = SHAPE((TOK, TOK), bf16)
+    return pl.pallas_call(
+        cut_kernel,
+        grid_spec=pltpu.PrefetchScalarGridSpec(
+            num_scalar_prefetch=1,
+            grid=(1,),
+            in_specs=[
+                pl.BlockSpec((TOK, TOK), lambda i, at, r=r: (0, (at[1] + r) % NZ)) for r in range(NZ)
+            ],
+            out_specs=[pl.BlockSpec((TOK, TOK), lambda i, at: (0, 0))] * NZ,
+        ),
+        out_shape=[block] * NZ,
+        name="cut",
+    )(at, *[cotangent] * NZ)
+
+
+def join_kernel(at, *refs):
+    want = (at[1] % (NZ // NH)) * NH + at[3]
+    for r in range(NZ):
+        refs[NZ][(want - r + NZ) % NZ] = refs[r][...]
+
+
+def join(at, moved):
+    return pl.pallas_call(
+        join_kernel,
+        grid_spec=pltpu.PrefetchScalarGridSpec(
+            num_scalar_prefetch=1,
+            grid=(1,),
+            in_specs=[pl.BlockSpec((TOK, TOK), lambda i, at: (0, 0))] * NZ,
+            out_specs=pl.BlockSpec((NZ, TOK, TOK), lambda i, at: (0, 0, 0)),
+        ),
+        out_shape=SHAPE((NZ, TOK, TOK), bf16),
+        name="join",
+    )(at, *moved).reshape(NZ * TOK, TOK)
+
+
+def spread(r):
+    pairs = []
+    for z in range(NZ):
+        for core in range(NH):
+            q = (z + r) % NZ
+            pairs.append((z * NH + core, (NZ // NH * core + q // NH) * NH + q % NH))
+    return pairs
+
+
 def shift(value, axis, by):
     count = lax.axis_size(axis)
     return lax.ppermute(value, axis, [(i, (i + by) % count) for i in range(count)])
@@ -379,10 +430,6 @@
 
 def add(received, own):
     return (received.astype(f32) + own).astype(bf16)
-
-
-def after(value, *earlier):
-    return lax.optimization_barrier((value,) + earlier)[0]
 
 
 def ordered(signal, gate_values, filter_taps, skip_gain, w_out, cotangent):
@@ -390,13 +437,11 @@
     seq = ("y", "z")
     at = jnp.stack([lax.axis_index(a) for a in ("y", "z", "x", "core")]).astype(jnp.int32)
 
-    pieces = cotangent.reshape(TOK, NZ // NH, NH, TOK).transpose(2, 1, 0, 3)
-    pieces = lax.all_to_all(pieces, "core", split_axis=0, concat_axis=0, tiled=True)
-    piece = lax.all_to_all(pieces.reshape(NZ, TOK, TOK), "z", split_axis=0, concat_axis=0, tiled=True)
-    piece = piece.reshape(NZ * TOK, TOK)
-
-    cols = to_cols(after(signal, pieces), filter_taps, gate_values)
+    cols = to_cols(signal, filter_taps, gate_values)
     cols = lax.all_to_all(cols, seq, split_axis=0, concat_axis=0, tiled=True)
+    pieces = cut(at, cotangent)
+    pieces = [lax.ppermute(p, ("z", "core"), spread(r)) for r, p in enumerate(pieces)]
+    piece = join(at, pieces)
     ws = [w_out, shift(w_out, "y", -1), shift(w_out, "y", 2), shift(w_out, "y", 1)]
     skip = jnp.broadcast_to(skip_gain[:, None], (CL, TOK))
 
@@ -426,9 +471,8 @@
     for _ in range(3):
         fore.append(shift(fore[-1], "z", 1))
         aft.append(shift(aft[-1], "z", -1))
-    half = NY * CL // 2
-    far = [shift(fore[-1][:half], "z", 1), shift(aft[-1][half:], "z", -1)]
-    ring = [gated] + aft[1:] + far + fore[:0:-1]
+    far = shift(fore[-1], "z", 1)
+    ring = [gated] + aft[1:] + [far] + fore[:0:-1]
 
     part = part.reshape(NY, CL, NZ * TOK)
     grad_gated = lax.all_to_all(part, "y", split_axis=0, concat_axis=0, tiled=True)

time: 227 us -> 248 us (1.093)
  starting transfers between devices: 72.8 us -> 83.9 us
  waiting for transfers between devices: 94.6 us -> 103 us
  Pallas kernels: 40.1 us -> 44.7 us
  blocking collectives: 3.94 us -> 0 us
    ppermute x0 -> x8, starting transfers between devices: none -> 29.9 us  [ordered(): lax.ppermute(p, ('z', 'core'), spread(r))]
    all_to_all x1 -> x0, waiting for transfers between devices: 10.1 us -> none  [ordered(): lax.all_to_all(pieces.reshape(NZ, TOK, TOK), 'z', split_axis=0, concat_ax...]
    all_to_all x1 -> x0, starting transfers between devices: 8.57 us -> none  [ordered(): lax.all_to_all(pieces.reshape(NZ, TOK, TOK), 'z', split_axis=0, concat_ax...]
    ppermute x28 -> x27, waiting for transfers between devices: 84.4 us -> 90.2 us  [shift(): lax.ppermute(value, axis, [(i, (i + by) % count) for i in range(count)])]
    all_to_all x1, starting transfers between devices: 10.9 us -> 5.67 us  [ordered(): lax.all_to_all(outs, seq, split_axis=0, concat_axis=0, tiled=True)]
    all_to_all x1, waiting for transfers between devices: 0.01 us -> 4.82 us  [ordered(): gated = lax.all_to_all(gated, 'y', split_axis=0, concat_axis=0, tiled=True)]
    pallas_call x0 -> x2, Pallas kernels: none -> 4.52 us  [the longest x1 2.28 us: join(): pl.pallas_call(join_kernel, grid_spec=pltpu.PrefetchScalarGridSpec(num_sc...]
    all_to_all x1, waiting for transfers between devices: 0.15 us -> 4.41 us  [ordered(): lax.all_to_all(part, 'y', split_axis=0, concat_axis=0, tiled=True)]
  transfers between devices with their start and end apart: 33 -> 39, of which waited for: 19 -> 19; matrix products, arithmetic and copies ran while one was open for 3% -> 3% of each run, Pallas kernels for 14% -> 13%
where the time goes in v2:
time: 248 us; the launch traced here: 246 us
  waiting for transfers between devices  103 us (42%)
  starting transfers between devices  83.9 us (34%)
  Pallas kernels  44.7 us (18%)
  other arithmetic  6.85 us (3%)
  local copies, waits for them, and re-layouts  6.62 us (3%)
    ppermute x27, waiting for transfers between devices, shift(): lax.ppermute(value, axis, [(i, (i + by) % count) for i in range(count)])  90.2 us
    ppermute x27, starting transfers between devices, shift(): lax.ppermute(value, axis, [(i, (i + by) % count) for i in range(count)])  34.7 us
    ppermute x8, starting transfers between devices, ordered(): lax.ppermute(p, ('z', 'core'), spread(r))  29.9 us
    pallas_call x1, Pallas kernels, grad_weight_part(): pl.pallas_call(weight_kernel, grid_spec=pltpu.PrefetchScalarGridSpec(num_...  7.3 us
    pallas_call x1, Pallas kernels, back(): pl.pallas_call(back_kernel, grid=(STEPS,), in_specs=[WIDE, PACK, PLAIN, S...  7.05 us
    pallas_call x1, Pallas kernels, staying_part(): pl.pallas_call(staying_kernel, grid_spec=pltpu.PrefetchScalarGridSpec(num...  6.54 us
    pallas_call x1, Pallas kernels, opening_part(): pl.pallas_call(opening_kernel, grid_spec=pltpu.PrefetchScalarGridSpec(num...  6.26 us
    unnamed x68, local copies, waits for them, and re-layouts  5.87 us
  transfers between devices with their start and end apart: 39, of which 19 were waited for; matrix products, arithmetic and copies ran while one was open for 3% of the time, Pallas kernels for 13%

profile of v2, /device:TPU:32, one launch (start us, length us, event | category | flops | bytes accessed | tf_op | source)
XLA Modules:
  0.0 246.0 jit_solution(4097755716275479207)
XLA Ops:
  1.2 2.2 cut.1
  3.4 1.9 collective-permute-start.3
  6.8 8.8 %collective-permute-start.5 = (bf16[128,128]{1,0:T(8,128)(2,1)}, bf16[128,128]{1,0:T(8,128)(2,1)S(1)}, u32[]{:S(2)}, u32[]{:S(2)}) collective-permute-start(bf16[128,128]{1,0:T(8,128)(2,1)} %get-tuple-element.37), channel_id=1, source_target_pairs={{0,8},{1,40},{8,9},{9,41},{16,16},{17,48},{24,17},{25,49},{32,24},... | collective-permute-start | bytes 98312 | tf_op jit(solution)/shard_map/ppermute | solution.py:443
  15.6 2.0 collective-permute-start.6
  17.6 6.1 %collective-permute-start.7 = (bf16[128,128]{1,0:T(8,128)(2,1)}, bf16[128,128]{1,0:T(8,128)(2,1)S(1)}, u32[]{:S(2)}, u32[]{:S(2)}) collective-permute-start(bf16[128,128]{1,0:T(8,128)(2,1)} %get-tuple-element.39), channel_id=1, source_target_pairs={{0,16},{1,48},{8,17},{9,49},{16,24},{17,56},{24,25},{25,57},{32,0}... | collective-permute-start | bytes 98312 | tf_op jit(solution)/shard_map/ppermute | solution.py:443
  23.7 2.8 %collective-permute-start.8 = (bf16[128,128]{1,0:T(8,128)(2,1)}, bf16[128,128]{1,0:T(8,128)(2,1)S(1)}, u32[]{:S(2)}, u32[]{:S(2)}) collective-permute-start(bf16[128,128]{1,0:T(8,128)(2,1)} %get-tuple-element.40), channel_id=1, source_target_pairs={{0,17},{1,49},{8,24},{9,56},{16,25},{17,57},{24,0},{25,32},{32,1},... | collective-permute-start | bytes 98312 | tf_op jit(solution)/shard_map/ppermute | solution.py:443
  26.5 3.4 %collective-permute-start.9 = (bf16[128,128]{1,0:T(8,128)(2,1)}, bf16[128,128]{1,0:T(8,128)(2,1)S(1)}, u32[]{:S(2)}, u32[]{:S(2)}) collective-permute-start(bf16[128,128]{1,0:T(8,128)(2,1)} %get-tuple-element.41), channel_id=1, source_target_pairs={{0,24},{1,56},{8,25},{9,57},{16,0},{17,32},{24,1},{25,33},{32,8},{... | collective-permute-start | bytes 98312 | tf_op jit(solution)/shard_map/ppermute | solution.py:443
  29.9 3.5 %collective-permute-start.10 = (bf16[128,128]{1,0:T(8,128)(2,1)}, bf16[128,128]{1,0:T(8,128)(2,1)S(1)}, u32[]{:S(2)}, u32[]{:S(2)}) collective-permute-start(bf16[128,128]{1,0:T(8,128)(2,1)} %get-tuple-element.42), channel_id=1, source_target_pairs={{0,25},{1,57},{8,0},{9,32},{16,1},{17,33},{24,8},{25,40},{32,9},{3... | collective-permute-start | bytes 98312 | tf_op jit(solution)/shard_map/ppermute | solution.py:443
  33.6 1.9 collective-permute-done.9.refs_6_
  37.5 2.3 join.1
  39.8 2.8 %collective-permute-start.11 = (bf16[1024,128]{1,0:T(8,128)(2,1)}, bf16[1024,128]{1,0:T(8,128)(2,1)S(1)}, u32[]{:S(2)}, u32[]{:S(2)}) collective-permute-start(bf16[1024,128]{1,0:T(8,128)(2,1)} %bitcast.46), channel_id=1, source_target_pairs={{0,6},{2,0},{4,2},{6,4},{1,7},{3,1},{5,3},{7,5},{8,14},{10,8},{12,... | collective-permute-start | bytes 786440 | tf_op jit(solution)/shard_map/ppermute | solution.py:428
  43.3 3.0 %collective-permute-start = (bf16[1024,256]{1,0:T(8,128)(2,1)}, bf16[1024,256]{1,0:T(8,128)(2,1)S(1)}, u32[]{:S(2)}, u32[]{:S(2)}) collective-permute-start(bf16[1024,256]{1,0:T(8,128)(2,1)} %w0.3), channel_id=1, source_target_pairs={{0,192},{64,0},{128,64},{192,128},{1,193},{65,1},{129,65},{193,129... | collective-permute-start | bytes 1572872 | tf_op jit(solution)/shard_map/ppermute | solution.py:428
  47.9 6.5 %collective-permute-done.11.m1 = bf16[1024,128]{1,0:T(8,128)(2,1)S(1)} collective-permute-done((bf16[1024,128]{1,0:T(8,128)(2,1)}, bf16[1024,128]{1,0:T(8,128)(2,1)S(1)}, u32[]{:S(2)}, u32[]{:S(2)}) %collective-permute-start.11) | collective-permute-done | bytes 262176 | tf_op jit(solution)/shard_map/ppermute | solution.py:428
  56.9 2.1 collective-permute-done.13.m3
  59.6 10.4 %collective-permute-done.w1 = bf16[1024,256]{1,0:T(8,128)(2,1)S(1)} collective-permute-done((bf16[1024,256]{1,0:T(8,128)(2,1)}, bf16[1024,256]{1,0:T(8,128)(2,1)S(1)}, u32[]{:S(2)}, u32[]{:S(2)}) %collective-permute-start) | collective-permute-done | bytes 524320 | tf_op jit(solution)/shard_map/ppermute | solution.py:428
  70.3 3.6 %collective-permute-done.2.w3 = bf16[1024,256]{1,0:T(8,128)(2,1)S(1)} collective-permute-done((bf16[1024,256]{1,0:T(8,128)(2,1)}, bf16[1024,256]{1,0:T(8,128)(2,1)S(1)}, u32[]{:S(2)}, u32[]{:S(2)}) %collective-permute-start.2) | collective-permute-done | bytes 524320 | tf_op jit(solution)/shard_map/ppermute | solution.py:428
  75.7 6.3 %opening.1 = (bf16[4,1024,256]{2,1,0:T(8,128)(2,1)}, bf16[128,1024]{1,0:T(8,128)(2,1)}, bf16[128,1024]{1,0:T(8,128)(2,1)}) custom-call(s32[4]{0:T(128)} %pad_add_fusion.at, bf16[1024,256]{1,0:T(8,128)(2,1)} %w0.3, bf16[1024,256]{1,0:T(8,128)(2,1)} %copy-done.2, bf16[1024,256]{1,0:T(8,128)(2,1)} %copy-done.3, bf16[1024,256]{1,0:T(8,128)(2,1)} %copy-done.4, ...), custom_call_target="tpu_custom_call" | custom-call | tf_op jit(solution)/shard_map/opening/pallas_call | solution.py:276
  82.0 3.2 %collective-permute-start.18 = (bf16[128,1024]{1,0:T(8,128)(2,1)}, bf16[128,1024]{1,0:T(8,128)(2,1)S(1)}, u32[]{:S(2)}, u32[]{:S(2)}) collective-permute-start(bf16[128,1024]{1,0:T(8,128)(2,1)} %get-tuple-element.43), channel_id=1, source_target_pairs={{0,8},{8,16},{16,24},{24,32},{32,40},{40,48},{48,56},{56,0},{1,9},... | collective-permute-start | bytes 786440 | tf_op jit(solution)/shard_map/ppermute | solution.py:428
  85.2 2.1 to_cols.1
  87.3 5.8 %all-to-all-start.1 = ((bf16[32,3,32,128]{3,2,1,0:T(8,128)(2,1)}), bf16[32,3,32,128]{3,2,1,0:T(8,128)(2,1)S(1)}, u32[]{:S(2)}, u32[]{:S(2)}) async-start(bf16[32,3,32,128]{3,2,1,0:T(8,128)(2,1)} %to_cols.1), calls=%async_computation.1 | async-start | bytes 1572864 | tf_op jit(solution)/shard_map/all_to_all | solution.py:441
  93.1 6.5 %staying.1 = f32[6,128,1024]{2,1,0:T(8,128)} custom-call(s32[4]{0:T(128)} %pad_add_fusion.at, bf16[1024,256]{1,0:T(8,128)(2,1)} %w0.3, bf16[1024,256]{1,0:T(8,128)(2,1)} %copy-done.2, bf16[1024,256]{1,0:T(8,128)(2,1)} %copy-done.3, bf16[1024,256]{1,0:T(8,128)(2,1)} %copy-done.4, bf16[4,1024,256]{2,1,0:T(8,128)(2,1)} %get-tuple-element.46.cot_ref.refs_8_), custom_call_target="tpu_custom_call" | custom-call | tf_op jit(solution)/shard_map/staying/pallas_call | solution.py:300
  103.1 12.6 %collective-permute-done.20 = bf16[128,1024]{1,0:T(8,128)(2,1)S(1)} collective-permute-done((bf16[128,1024]{1,0:T(8,128)(2,1)S(1)}, bf16[128,1024]{1,0:T(8,128)(2,1)S(1)}, u32[]{:S(2)}, u32[]{:S(2)}) %collective-permute-start.20) | collective-permute-done | bytes 262176 | tf_op jit(solution)/shard_map/ppermute | solution.py:428
  118.3 1.6 collective-permute-start.22
  120.4 5.3 %collective-permute-done.22 = bf16[128,1024]{1,0:T(8,128)(2,1)S(1)} collective-permute-done((bf16[128,1024]{1,0:T(8,128)(2,1)S(1)}, bf16[128,1024]{1,0:T(8,128)(2,1)S(1)}, u32[]{:S(2)}, u32[]{:S(2)}) %collective-permute-start.22) | collective-permute-done | bytes 262176 | tf_op jit(solution)/shard_map/ppermute | solution.py:428
  125.7 1.8 collective-permute-done.23
  128.5 1.8 collective-permute-start.24
  131.3 5.9 %conv.1 = (bf16[32,32,128]{2,1,0:T(8,128)(2,1)}, bf16[4,32,1024]{2,1,0:T(8,128)(2,1)}, f32[1024,256]{1,0:T(8,128)}, f32[1024,256]{1,0:T(8,128)}) custom-call(bf16[32,3,32,128]{3,2,1,0:T(8,128)(2,1)} %copy-done, f32[32,128]{1,0:T(8,128)} %broadcast_in_dim.2.skip_ref, bf16[64,64]{1,0:T(8,128)(2,1)} %constant.28.clone.a_ref, ...), custom_call_target="tpu_custom_call" | custom-call | tf_op jit(solution)/shard_map/conv/pallas_call | solution.py:164
  137.2 4.5 %all-to-all-start.3 = ((bf16[4,32,1024]{2,1,0:T(8,128)(2,1)}), bf16[4,32,1024]{2,1,0:T(8,128)(2,1)S(1)}, u32[]{:S(2)}, u32[]{:S(2)}) async-start(bf16[4,32,1024]{2,1,0:T(8,128)(2,1)} %get-tuple-element.60), calls=%async_computation.3 | async-start | bytes 524288 | tf_op jit(solution)/shard_map/all_to_all | solution.py:451
  141.7 1.9 fusion.2
  143.6 4.8 %all-to-all-done.3 = bf16[4,32,1024]{2,1,0:T(8,128)(2,1)S(1)} async-done(((bf16[4,32,1024]{2,1,0:T(8,128)(2,1)}), bf16[4,32,1024]{2,1,0:T(8,128)(2,1)S(1)}, u32[]{:S(2)}, u32[]{:S(2)}) %all-to-all-start.3) | async-done | bytes 262176 | tf_op jit(solution)/shard_map/all_to_all | solution.py:451
  148.4 3.4 %all-to-all-start = ((bf16[4,32,1024]{2,1,0:T(8,128)(2,1)}), bf16[4,32,1024]{2,1,0:T(8,128)(2,1)S(1)}, u32[]{:S(2)}, u32[]{:S(2)}) async-start(bf16[4,32,1024]{2,1,0:T(8,128)(2,1)} %bitcast.11), calls=%async_computation | async-start | bytes 524288 | tf_op jit(solution)/shard_map/all_to_all | solution.py:478
  151.8 2.2 collective-permute-start.28
  154.0 4.4 %all-to-all-done.gg_ref = bf16[4,32,1024]{2,1,0:T(8,128)(2,1)S(1)} async-done(((bf16[4,32,1024]{2,1,0:T(8,128)(2,1)}), bf16[4,32,1024]{2,1,0:T(8,128)(2,1)S(1)}, u32[]{:S(2)}, u32[]{:S(2)}) %all-to-all-start) | async-done | bytes 262176 | tf_op jit(solution)/shard_map/all_to_all | solution.py:478
  159.1 7.1 %back.1 = (bf16[32,3,32,128]{3,2,1,0:T(8,128)(2,1)}, f32[32,128]{1,0:T(8,128)}) custom-call(bf16[4,32,1024]{2,1,0:T(8,128)(2,1)} %copy-done.6, bf16[32,3,32,128]{3,2,1,0:T(8,128)(2,1)} %copy-done, bf16[32,32,128]{2,1,0:T(8,128)(2,1)} %get-tuple-element.52.mixed_ref, f32[1024,256]{1,0:T(8,128)} %get-tuple-element.53.sig_ref, ...), custom_call_target="tpu_custom_call" | custom-call | tf_op jit(solution)/shard_map/back/pallas_call | solution.py:181
  166.2 5.7 %all-to-all-start.2 = ((bf16[32,3,32,128]{3,2,1,0:T(8,128)(2,1)}), bf16[32,3,32,128]{3,2,1,0:T(8,128)(2,1)S(1)}, u32[]{:S(2)}, u32[]{:S(2)}) async-start(bf16[32,3,32,128]{3,2,1,0:T(8,128)(2,1)} %get-tuple-element.55), calls=%async_computation.2 | async-start | bytes 1572864 | tf_op jit(solution)/shard_map/all_to_all | solution.py:480
  172.2 1.8 collective-permute-start.29
  174.0 19.6 %collective-permute-done.25.refs_1_ = bf16[128,1024]{1,0:T(8,128)(2,1)S(1)} collective-permute-done((bf16[128,1024]{1,0:T(8,128)(2,1)S(1)}, bf16[128,1024]{1,0:T(8,128)(2,1)S(1)}, u32[]{:S(2)}, u32[]{:S(2)}) %collective-permute-start.25) | collective-permute-done | bytes 262176 | tf_op jit(solution)/shard_map/ppermute | solution.py:428
  193.9 1.7 collective-permute-start.30
  195.7 5.6 %collective-permute-done.26.refs_2_ = bf16[128,1024]{1,0:T(8,128)(2,1)S(1)} collective-permute-done((bf16[128,1024]{1,0:T(8,128)(2,1)S(1)}, bf16[128,1024]{1,0:T(8,128)(2,1)S(1)}, u32[]{:S(2)}, u32[]{:S(2)}) %collective-permute-start.26) | collective-permute-done | bytes 262176 | tf_op jit(solution)/shard_map/ppermute | solution.py:428
  201.3 1.8 collective-permute-start.27
  203.3 4.3 %collective-permute-done.27.refs_3_ = bf16[128,1024]{1,0:T(8,128)(2,1)S(1)} collective-permute-done((bf16[128,1024]{1,0:T(8,128)(2,1)S(1)}, bf16[128,1024]{1,0:T(8,128)(2,1)S(1)}, u32[]{:S(2)}, u32[]{:S(2)}) %collective-permute-start.27) | collective-permute-done | bytes 262176 | tf_op jit(solution)/shard_map/ppermute | solution.py:428
  207.7 1.8 collective-permute-done.31.refs_4_
  210.2 7.3 %grad_weight.1 = (bf16[1024,256]{1,0:T(8,128)(2,1)}, bf16[1024,256]{1,0:T(8,128)(2,1)}, bf16[1024,256]{1,0:T(8,128)(2,1)}, bf16[1024,256]{1,0:T(8,128)(2,1)}) custom-call(s32[4]{0:T(128)} %pad_add_fusion.at, bf16[128,1024]{1,0:T(8,128)(2,1)} %bitcast.53, bf16[128,1024]{1,0:T(8,128)(2,1)} %copy-done.15, bf16[128,1024]{1,0:T(8,128)(2,1)} %copy-done.18, ...), custom_call_target="tpu_custom_call" | custom-call | tf_op jit(solution)/shard_map/grad_weight/pallas_call | solution.py:335
  218.9 2.7 %collective-permute-start.33 = (bf16[1024,256]{1,0:T(8,128)(2,1)}, bf16[1024,256]{1,0:T(8,128)(2,1)S(1)}, u32[]{:S(2)}, u32[]{:S(2)}) collective-permute-start(bf16[1024,256]{1,0:T(8,128)(2,1)} %get-tuple-element.63), channel_id=1, source_target_pairs={{0,128},{64,192},{128,0},{192,64},{1,129},{65,193},{129,1},{193,65... | collective-permute-start | bytes 1572872 | tf_op jit(solution)/shard_map/ppermute | solution.py:428
  223.6 9.7 %collective-permute-done.32.b_ref = bf16[1024,256]{1,0:T(8,128)(2,1)S(1)} collective-permute-done((bf16[1024,256]{1,0:T(8,128)(2,1)}, bf16[1024,256]{1,0:T(8,128)(2,1)S(1)}, u32[]{:S(2)}, u32[]{:S(2)}) %collective-permute-start.32) | collective-permute-done | bytes 524320 | tf_op jit(solution)/shard_map/ppermute | solution.py:428
  233.3 5.6 %collective-permute-done.33.c_ref = bf16[1024,256]{1,0:T(8,128)(2,1)S(1)} collective-permute-done((bf16[1024,256]{1,0:T(8,128)(2,1)}, bf16[1024,256]{1,0:T(8,128)(2,1)S(1)}, u32[]{:S(2)}, u32[]{:S(2)}) %collective-permute-start.33) | collective-permute-done | bytes 524320 | tf_op jit(solution)/shard_map/ppermute | solution.py:428
  239.9 3.1 %weight_sum.1 = f32[4,8,32,256]{3,2,1,0:T(8,128)} custom-call(s32[4]{0:T(128)} %pad_add_fusion.at, bf16[1024,256]{1,0:T(8,128)(2,1)} %get-tuple-element.61.a_ref, bf16[1024,256]{1,0:T(8,128)(2,1)} %copy-done.7, bf16[1024,256]{1,0:T(8,128)(2,1)} %copy-done.8, bf16[1024,256]{1,0:T(8,128)(2,1)} %copy-done.9), custom_call_target="tpu_custom_call" | custom-call | tf_op jit(solution)/shard_map/weight_sum/pallas_call | solution.py:362
  244.0 2.0 to_rows.1
  (115 shorter events, 27.7 us)
Async XLA Ops:
  3.4 20.2 %collective-permute-start.3 = (bf16[128,128]{1,0:T(8,128)(2,1)}, bf16[128,128]{1,0:T(8,128)(2,1)S(1)}, u32[]{:S(2)}, u32[]{:S(2)}) collective-permute-start(bf16[128,128]{1,0:T(8,128)(2,1)} %get-tuple-element.35), channel_id=1, source_target_pairs={{0,0},{1,32},{8,1},{9,33},{16,8},{17,40},{24,9},{25,41},{32,16},{3... | collective-permute-start | bytes 98312 | tf_op jit(solution)/shard_map/ppermute | solution.py:443
  5.4 21.1 %collective-permute-start.4 = (bf16[128,128]{1,0:T(8,128)(2,1)}, bf16[128,128]{1,0:T(8,128)(2,1)S(1)}, u32[]{:S(2)}, u32[]{:S(2)}) collective-permute-start(bf16[128,128]{1,0:T(8,128)(2,1)} %get-tuple-element.36), channel_id=1, source_target_pairs={{0,1},{1,33},{8,8},{9,40},{16,9},{17,41},{24,16},{25,48},{32,17},{... | collective-permute-start | bytes 98312 | tf_op jit(solution)/shard_map/ppermute | solution.py:443
  6.8 23.1 %collective-permute-start.5 = (bf16[128,128]{1,0:T(8,128)(2,1)}, bf16[128,128]{1,0:T(8,128)(2,1)S(1)}, u32[]{:S(2)}, u32[]{:S(2)}) collective-permute-start(bf16[128,128]{1,0:T(8,128)(2,1)} %get-tuple-element.37), channel_id=1, source_target_pairs={{0,8},{1,40},{8,9},{9,41},{16,16},{17,48},{24,17},{25,49},{32,24},... | collective-permute-start | bytes 98312 | tf_op jit(solution)/shard_map/ppermute | solution.py:443
  15.6 17.8 %collective-permute-start.6 = (bf16[128,128]{1,0:T(8,128)(2,1)}, bf16[128,128]{1,0:T(8,128)(2,1)S(1)}, u32[]{:S(2)}, u32[]{:S(2)}) collective-permute-start(bf16[128,128]{1,0:T(8,128)(2,1)} %get-tuple-element.38), channel_id=1, source_target_pairs={{0,9},{1,41},{8,16},{9,48},{16,17},{17,49},{24,24},{25,56},{32,25}... | collective-permute-start | bytes 98312 | tf_op jit(solution)/shard_map/ppermute | solution.py:443
  17.6 15.8 %collective-permute-start.7 = (bf16[128,128]{1,0:T(8,128)(2,1)}, bf16[128,128]{1,0:T(8,128)(2,1)S(1)}, u32[]{:S(2)}, u32[]{:S(2)}) collective-permute-start(bf16[128,128]{1,0:T(8,128)(2,1)} %get-tuple-element.39), channel_id=1, source_target_pairs={{0,16},{1,48},{8,17},{9,49},{16,24},{17,56},{24,25},{25,57},{32,0}... | collective-permute-start | bytes 98312 | tf_op jit(solution)/shard_map/ppermute | solution.py:443
  23.7 9.9 %collective-permute-start.8 = (bf16[128,128]{1,0:T(8,128)(2,1)}, bf16[128,128]{1,0:T(8,128)(2,1)S(1)}, u32[]{:S(2)}, u32[]{:S(2)}) collective-permute-start(bf16[128,128]{1,0:T(8,128)(2,1)} %get-tuple-element.40), channel_id=1, source_target_pairs={{0,17},{1,49},{8,24},{9,56},{16,25},{17,57},{24,0},{25,32},{32,1},... | collective-permute-start | bytes 98312 | tf_op jit(solution)/shard_map/ppermute | solution.py:443
  26.5 9.0 %collective-permute-start.9 = (bf16[128,128]{1,0:T(8,128)(2,1)}, bf16[128,128]{1,0:T(8,128)(2,1)S(1)}, u32[]{:S(2)}, u32[]{:S(2)}) collective-permute-start(bf16[128,128]{1,0:T(8,128)(2,1)} %get-tuple-element.41), channel_id=1, source_target_pairs={{0,24},{1,56},{8,25},{9,57},{16,0},{17,32},{24,1},{25,33},{32,8},{... | collective-permute-start | bytes 98312 | tf_op jit(solution)/shard_map/ppermute | solution.py:443
  29.9 6.9 %collective-permute-start.10 = (bf16[128,128]{1,0:T(8,128)(2,1)}, bf16[128,128]{1,0:T(8,128)(2,1)S(1)}, u32[]{:S(2)}, u32[]{:S(2)}) collective-permute-start(bf16[128,128]{1,0:T(8,128)(2,1)} %get-tuple-element.42), channel_id=1, source_target_pairs={{0,25},{1,57},{8,0},{9,32},{16,1},{17,33},{24,8},{25,40},{32,9},{3... | collective-permute-start | bytes 98312 | tf_op jit(solution)/shard_map/ppermute | solution.py:443
  39.8 14.6 %collective-permute-start.11 = (bf16[1024,128]{1,0:T(8,128)(2,1)}, bf16[1024,128]{1,0:T(8,128)(2,1)S(1)}, u32[]{:S(2)}, u32[]{:S(2)}) collective-permute-start(bf16[1024,128]{1,0:T(8,128)(2,1)} %bitcast.46), channel_id=1, source_target_pairs={{0,6},{2,0},{4,2},{6,4},{1,7},{3,1},{5,3},{7,5},{8,14},{10,8},{12,... | collective-permute-start | bytes 786440 | tf_op jit(solution)/shard_map/ppermute | solution.py:428
  42.5 12.8 %collective-permute-start.12 = (bf16[1024,128]{1,0:T(8,128)(2,1)}, bf16[1024,128]{1,0:T(8,128)(2,1)S(1)}, u32[]{:S(2)}, u32[]{:S(2)}) collective-permute-start(bf16[1024,128]{1,0:T(8,128)(2,1)} %bitcast.47), channel_id=1, source_target_pairs={{0,4},{2,6},{4,0},{6,2},{1,5},{3,7},{5,1},{7,3},{8,12},{10,14},{12... | collective-permute-start | bytes 786440 | tf_op jit(solution)/shard_map/ppermute | solution.py:428
  43.3 26.6 %collective-permute-start = (bf16[1024,256]{1,0:T(8,128)(2,1)}, bf16[1024,256]{1,0:T(8,128)(2,1)S(1)}, u32[]{:S(2)}, u32[]{:S(2)}) collective-permute-start(bf16[1024,256]{1,0:T(8,128)(2,1)} %w0.3), channel_id=1, source_target_pairs={{0,192},{64,0},{128,64},{192,128},{1,193},{65,1},{129,65},{193,129... | collective-permute-start | bytes 1572872 | tf_op jit(solution)/shard_map/ppermute | solution.py:428
  46.3 24.0 %collective-permute-start.1 = (bf16[1024,256]{1,0:T(8,128)(2,1)}, bf16[1024,256]{1,0:T(8,128)(2,1)S(1)}, u32[]{:S(2)}, u32[]{:S(2)}) collective-permute-start(bf16[1024,256]{1,0:T(8,128)(2,1)} %w0.3), channel_id=1, source_target_pairs={{0,128},{64,192},{128,0},{192,64},{1,129},{65,193},{129,1},{193,65... | collective-permute-start | bytes 1572872 | tf_op jit(solution)/shard_map/ppermute | solution.py:428
  47.0 12.1 %collective-permute-start.13 = (bf16[1024,128]{1,0:T(8,128)(2,1)}, bf16[1024,128]{1,0:T(8,128)(2,1)S(1)}, u32[]{:S(2)}, u32[]{:S(2)}) collective-permute-start(bf16[1024,128]{1,0:T(8,128)(2,1)} %bitcast.48), channel_id=1, source_target_pairs={{0,2},{2,4},{4,6},{6,0},{1,3},{3,5},{5,7},{7,1},{8,10},{10,12},{12... | collective-permute-start | bytes 786440 | tf_op jit(solution)/shard_map/ppermute | solution.py:428
  54.3 19.6 %copy-start.11 = (bf16[1024,128]{1,0:T(8,128)(2,1)}, bf16[1024,128]{1,0:T(8,128)(2,1)S(1)}, u32[]{:S(2)}) copy-start(bf16[1024,128]{1,0:T(8,128)(2,1)S(1)} %collective-permute-done.11.m1) | copy-start | bytes 786436
  54.3 4.8 %collective-permute-start.14 = (bf16[1024,128]{1,0:T(8,128)(2,1)}, bf16[1024,128]{1,0:T(8,128)(2,1)S(1)}, u32[]{:S(2)}, u32[]{:S(2)}) collective-permute-start(bf16[1024,128]{1,0:T(8,128)(2,1)} %bitcast.49), channel_id=1, source_target_pairs={{0,1},{1,0},{2,3},{3,2},{4,5},{5,4},{6,7},{7,6},{8,9},{9,8},{10,11... | collective-permute-start | bytes 786440 | tf_op jit(solution)/shard_map/ppermute | solution.py:428
  55.3 18.7 %copy-start.12 = (bf16[1024,128]{1,0:T(8,128)(2,1)}, bf16[1024,128]{1,0:T(8,128)(2,1)S(1)}, u32[]{:S(2)}) copy-start(bf16[1024,128]{1,0:T(8,128)(2,1)S(1)} %collective-permute-done.12.m2) | copy-start | bytes 786436
  55.3 18.6 %collective-permute-start.2 = (bf16[1024,256]{1,0:T(8,128)(2,1)}, bf16[1024,256]{1,0:T(8,128)(2,1)S(1)}, u32[]{:S(2)}, u32[]{:S(2)}) collective-permute-start(bf16[1024,256]{1,0:T(8,128)(2,1)} %w0.3), channel_id=1, source_target_pairs={{0,64},{64,128},{128,192},{192,0},{1,65},{65,129},{129,193},{193,1... | collective-permute-start | bytes 1572872 | tf_op jit(solution)/shard_map/ppermute | solution.py:428
  59.0 14.9 %copy-start.13 = (bf16[1024,128]{1,0:T(8,128)(2,1)}, bf16[1024,128]{1,0:T(8,128)(2,1)S(1)}, u32[]{:S(2)}) copy-start(bf16[1024,128]{1,0:T(8,128)(2,1)S(1)} %collective-permute-done.13.m3) | copy-start | bytes 786436
  59.0 14.9 %collective-permute-start.15 = (bf16[1024,128]{1,0:T(8,128)(2,1)S(1)}, bf16[1024,128]{1,0:T(8,128)(2,1)S(1)}, u32[]{:S(2)}, u32[]{:S(2)}) collective-permute-start(bf16[1024,128]{1,0:T(8,128)(2,1)S(1)} %collective-permute-done.11.m1), channel_id=1, source_target_pairs={{0,1},{1,0},{2,3},{3,2},{4,5},{5,4},{6,7},{7,6},{8,9},{9,8},{10,11... | collective-permute-start | bytes 786440 | tf_op jit(solution)/shard_map/ppermute | solution.py:428
  59.1 14.8 %collective-permute-start.16 = (bf16[1024,128]{1,0:T(8,128)(2,1)S(1)}, bf16[1024,128]{1,0:T(8,128)(2,1)S(1)}, u32[]{:S(2)}, u32[]{:S(2)}) collective-permute-start(bf16[1024,128]{1,0:T(8,128)(2,1)S(1)} %collective-permute-done.12.m2), channel_id=1, source_target_pairs={{0,1},{1,0},{2,3},{3,2},{4,5},{5,4},{6,7},{7,6},{8,9},{9,8},{10,11... | collective-permute-start | bytes 786440 | tf_op jit(solution)/shard_map/ppermute | solution.py:428
  70.0 4.0 %collective-permute-start.17 = (bf16[1024,128]{1,0:T(8,128)(2,1)S(1)}, bf16[1024,128]{1,0:T(8,128)(2,1)S(1)}, u32[]{:S(2)}, u32[]{:S(2)}) collective-permute-start(bf16[1024,128]{1,0:T(8,128)(2,1)S(1)} %collective-permute-done.13.m3), channel_id=1, source_target_pairs={{0,1},{1,0},{2,3},{3,2},{4,5},{5,4},{6,7},{7,6},{8,9},{9,8},{10,11... | collective-permute-start | bytes 786440 | tf_op jit(solution)/shard_map/ppermute | solution.py:428
  82.0 17.7 %collective-permute-start.18 = (bf16[128,1024]{1,0:T(8,128)(2,1)}, bf16[128,1024]{1,0:T(8,128)(2,1)S(1)}, u32[]{:S(2)}, u32[]{:S(2)}) collective-permute-start(bf16[128,1024]{1,0:T(8,128)(2,1)} %get-tuple-element.43), channel_id=1, source_target_pairs={{0,8},{8,16},{16,24},{24,32},{32,40},{40,48},{48,56},{56,0},{1,9},... | collective-permute-start | bytes 786440 | tf_op jit(solution)/shard_map/ppermute | solution.py:428
  85.2 14.4 %collective-permute-start.19 = (bf16[128,1024]{1,0:T(8,128)(2,1)}, bf16[128,1024]{1,0:T(8,128)(2,1)S(1)}, u32[]{:S(2)}, u32[]{:S(2)}) collective-permute-start(bf16[128,1024]{1,0:T(8,128)(2,1)} %get-tuple-element.44), channel_id=1, source_target_pairs={{0,56},{8,0},{16,8},{24,16},{32,24},{40,32},{48,40},{56,48},{1,57}... | collective-permute-start | bytes 786440 | tf_op jit(solution)/shard_map/ppermute | solution.py:428
  87.3 43.1 %all-to-all-start.1 = ((bf16[32,3,32,128]{3,2,1,0:T(8,128)(2,1)}), bf16[32,3,32,128]{3,2,1,0:T(8,128)(2,1)S(1)}, u32[]{:S(2)}, u32[]{:S(2)}) async-start(bf16[32,3,32,128]{3,2,1,0:T(8,128)(2,1)} %to_cols.1), calls=%async_computation.1 | async-start | bytes 1572864 | tf_op jit(solution)/shard_map/all_to_all | solution.py:441
  99.6 30.7 %copy-start.33 = (f32[32]{0:T(128)S(1)}, f32[32]{0:T(128)}, u32[]{:S(2)}) copy-start(f32[32]{0:T(128)} %param.14) | copy-start | bytes 388
  101.0 14.8 %collective-permute-start.20 = (bf16[128,1024]{1,0:T(8,128)(2,1)S(1)}, bf16[128,1024]{1,0:T(8,128)(2,1)S(1)}, u32[]{:S(2)}, u32[]{:S(2)}) collective-permute-start(bf16[128,1024]{1,0:T(8,128)(2,1)S(1)} %get-tuple-element.68), channel_id=1, source_target_pairs={{0,8},{8,16},{16,24},{24,32},{32,40},{40,48},{48,56},{56,0},{1,9},... | collective-permute-start | bytes 786440 | tf_op jit(solution)/shard_map/ppermute | solution.py:428
  102.6 14.4 %collective-permute-start.21 = (bf16[128,1024]{1,0:T(8,128)(2,1)S(1)}, bf16[128,1024]{1,0:T(8,128)(2,1)S(1)}, u32[]{:S(2)}, u32[]{:S(2)}) collective-permute-start(bf16[128,1024]{1,0:T(8,128)(2,1)S(1)} %get-tuple-element.67), channel_id=1, source_target_pairs={{0,56},{8,0},{16,8},{24,16},{32,24},{40,32},{48,40},{56,48},{1,57}... | collective-permute-start | bytes 786440 | tf_op jit(solution)/shard_map/ppermute | solution.py:428
  118.3 7.4 %collective-permute-start.22 = (bf16[128,1024]{1,0:T(8,128)(2,1)S(1)}, bf16[128,1024]{1,0:T(8,128)(2,1)S(1)}, u32[]{:S(2)}, u32[]{:S(2)}) collective-permute-start(bf16[128,1024]{1,0:T(8,128)(2,1)S(1)} %get-tuple-element.66), channel_id=1, source_target_pairs={{0,8},{8,16},{16,24},{24,32},{32,40},{40,48},{48,56},{56,0},{1,9},... | collective-permute-start | bytes 786440 | tf_op jit(solution)/shard_map/ppermute | solution.py:428
  119.9 7.6 %collective-permute-start.23 = (bf16[128,1024]{1,0:T(8,128)(2,1)S(1)}, bf16[128,1024]{1,0:T(8,128)(2,1)S(1)}, u32[]{:S(2)}, u32[]{:S(2)}) collective-permute-start(bf16[128,1024]{1,0:T(8,128)(2,1)S(1)} %get-tuple-element.65), channel_id=1, source_target_pairs={{0,56},{8,0},{16,8},{24,16},{32,24},{40,32},{48,40},{56,48},{1,57}... | collective-permute-start | bytes 786440 | tf_op jit(solution)/shard_map/ppermute | solution.py:428
  128.5 13.2 %collective-permute-start.24 = (bf16[128,1024]{1,0:T(8,128)(2,1)S(1)}, bf16[128,1024]{1,0:T(8,128)(2,1)S(1)}, u32[]{:S(2)}, u32[]{:S(2)}) collective-permute-start(bf16[128,1024]{1,0:T(8,128)(2,1)S(1)} %fusion.4), channel_id=1, source_target_pairs={{0,8},{8,16},{16,24},{24,32},{32,40},{40,48},{48,56},{56,0},{1,9},... | collective-permute-start | bytes 786440 | tf_op jit(solution)/shard_map/ppermute | solution.py:428
  137.2 11.2 %all-to-all-start.3 = ((bf16[4,32,1024]{2,1,0:T(8,128)(2,1)}), bf16[4,32,1024]{2,1,0:T(8,128)(2,1)S(1)}, u32[]{:S(2)}, u32[]{:S(2)}) async-start(bf16[4,32,1024]{2,1,0:T(8,128)(2,1)} %get-tuple-element.60), calls=%async_computation.3 | async-start | bytes 524288 | tf_op jit(solution)/shard_map/all_to_all | solution.py:451
  148.4 61.1 %copy-start.5 = (bf16[4,32,1024]{2,1,0:T(8,128)(2,1)}, bf16[4,32,1024]{2,1,0:T(8,128)(2,1)S(1)}, u32[]{:S(2)}) copy-start(bf16[4,32,1024]{2,1,0:T(8,128)(2,1)S(1)} %all-to-all-done.3) | copy-start | bytes 786436
  148.4 10.1 %all-to-all-start = ((bf16[4,32,1024]{2,1,0:T(8,128)(2,1)}), bf16[4,32,1024]{2,1,0:T(8,128)(2,1)S(1)}, u32[]{:S(2)}, u32[]{:S(2)}) async-start(bf16[4,32,1024]{2,1,0:T(8,128)(2,1)} %bitcast.11), calls=%async_computation | async-start | bytes 524288 | tf_op jit(solution)/shard_map/all_to_all | solution.py:478
  151.8 20.4 %collective-permute-start.28 = (bf16[128,1024]{1,0:T(8,128)(2,1)S(1)}, bf16[128,1024]{1,0:T(8,128)(2,1)S(1)}, u32[]{:S(2)}, u32[]{:S(2)}) collective-permute-start(bf16[128,1024]{1,0:T(8,128)(2,1)S(1)} %bitcast.51), channel_id=1, source_target_pairs={{0,8},{8,16},{16,24},{24,32},{32,40},{40,48},{48,56},{56,0},{1,9},... | collective-permute-start | bytes 786440 | tf_op jit(solution)/shard_map/ppermute | solution.py:428
  166.2 56.8 %copy-start.32 = (f32[32,128]{1,0:T(8,128)S(1)}, f32[32,128]{1,0:T(8,128)}, u32[]{:S(2)}) copy-start(f32[32,128]{1,0:T(8,128)} %get-tuple-element.59) | copy-start | bytes 49156
  166.2 76.8 %all-to-all-start.2 = ((bf16[32,3,32,128]{3,2,1,0:T(8,128)(2,1)}), bf16[32,3,32,128]{3,2,1,0:T(8,128)(2,1)S(1)}, u32[]{:S(2)}, u32[]{:S(2)}) async-start(bf16[32,3,32,128]{3,2,1,0:T(8,128)(2,1)} %get-tuple-element.55), calls=%async_computation.2 | async-start | bytes 1572864 | tf_op jit(solution)/shard_map/all_to_all | solution.py:480
  171.9 21.7 %collective-permute-start.25 = (bf16[128,1024]{1,0:T(8,128)(2,1)S(1)}, bf16[128,1024]{1,0:T(8,128)(2,1)S(1)}, u32[]{:S(2)}, u32[]{:S(2)}) collective-permute-start(bf16[128,1024]{1,0:T(8,128)(2,1)S(1)} %bitcast.52), channel_id=1, source_target_pairs={{0,56},{8,0},{16,8},{24,16},{32,24},{40,32},{48,40},{56,48},{1,57}... | collective-permute-start | bytes 786440 | tf_op jit(solution)/shard_map/ppermute | solution.py:428
  172.2 37.2 %copy-start.10 = (bf16[128,1024]{1,0:T(8,128)(2,1)}, bf16[128,1024]{1,0:T(8,128)(2,1)S(1)}, u32[]{:S(2)}) copy-start(bf16[128,1024]{1,0:T(8,128)(2,1)S(1)} %collective-permute-done.28.refs_7_) | copy-start | bytes 786436
  172.2 21.7 %collective-permute-start.29 = (bf16[128,1024]{1,0:T(8,128)(2,1)S(1)}, bf16[128,1024]{1,0:T(8,128)(2,1)S(1)}, u32[]{:S(2)}, u32[]{:S(2)}) collective-permute-start(bf16[128,1024]{1,0:T(8,128)(2,1)S(1)} %collective-permute-done.28.refs_7_), channel_id=1, source_target_pairs={{0,8},{8,16},{16,24},{24,32},{32,40},{40,48},{48,56},{56,0},{1,9},... | collective-permute-start | bytes 786440 | tf_op jit(solution)/shard_map/ppermute | solution.py:428
  193.6 15.8 %copy-start.15 = (bf16[128,1024]{1,0:T(8,128)(2,1)}, bf16[128,1024]{1,0:T(8,128)(2,1)S(1)}, u32[]{:S(2)}) copy-start(bf16[128,1024]{1,0:T(8,128)(2,1)S(1)} %collective-permute-done.25.refs_1_) | copy-start | bytes 786436
  193.6 7.6 %collective-permute-start.26 = (bf16[128,1024]{1,0:T(8,128)(2,1)S(1)}, bf16[128,1024]{1,0:T(8,128)(2,1)S(1)}, u32[]{:S(2)}, u32[]{:S(2)}) collective-permute-start(bf16[128,1024]{1,0:T(8,128)(2,1)S(1)} %collective-permute-done.25.refs_1_), channel_id=1, source_target_pairs={{0,56},{8,0},{16,8},{24,16},{32,24},{40,32},{48,40},{56,48},{1,57}... | collective-permute-start | bytes 786440 | tf_op jit(solution)/shard_map/ppermute | solution.py:428
  193.9 15.5 %copy-start.16 = (bf16[128,1024]{1,0:T(8,128)(2,1)}, bf16[128,1024]{1,0:T(8,128)(2,1)S(1)}, u32[]{:S(2)}) copy-start(bf16[128,1024]{1,0:T(8,128)(2,1)S(1)} %collective-permute-done.29.refs_6_) | copy-start | bytes 786436
  193.9 9.1 %collective-permute-start.30 = (bf16[128,1024]{1,0:T(8,128)(2,1)S(1)}, bf16[128,1024]{1,0:T(8,128)(2,1)S(1)}, u32[]{:S(2)}, u32[]{:S(2)}) collective-permute-start(bf16[128,1024]{1,0:T(8,128)(2,1)S(1)} %collective-permute-done.29.refs_6_), channel_id=1, source_target_pairs={{0,8},{8,16},{16,24},{24,32},{32,40},{40,48},{48,56},{56,0},{1,9},... | collective-permute-start | bytes 786440 | tf_op jit(solution)/shard_map/ppermute | solution.py:428
  201.3 6.4 %collective-permute-start.27 = (bf16[128,1024]{1,0:T(8,128)(2,1)S(1)}, bf16[128,1024]{1,0:T(8,128)(2,1)S(1)}, u32[]{:S(2)}, u32[]{:S(2)}) collective-permute-start(bf16[128,1024]{1,0:T(8,128)(2,1)S(1)} %collective-permute-done.26.refs_2_), channel_id=1, source_target_pairs={{0,56},{8,0},{16,8},{24,16},{32,24},{40,32},{48,40},{56,48},{1,57}... | collective-permute-start | bytes 786440 | tf_op jit(solution)/shard_map/ppermute | solution.py:428
  203.1 6.4 %collective-permute-start.31 = (bf16[128,1024]{1,0:T(8,128)(2,1)S(1)}, bf16[128,1024]{1,0:T(8,128)(2,1)S(1)}, u32[]{:S(2)}, u32[]{:S(2)}) collective-permute-start(bf16[128,1024]{1,0:T(8,128)(2,1)S(1)} %collective-permute-done.30.refs_5_), channel_id=1, source_target_pairs={{0,8},{8,16},{16,24},{24,32},{32,40},{40,48},{48,56},{56,0},{1,9},... | collective-permute-start | bytes 786440 | tf_op jit(solution)/shard_map/ppermute | solution.py:428
  217.5 15.8 %collective-permute-start.32 = (bf16[1024,256]{1,0:T(8,128)(2,1)}, bf16[1024,256]{1,0:T(8,128)(2,1)S(1)}, u32[]{:S(2)}, u32[]{:S(2)}) collective-permute-start(bf16[1024,256]{1,0:T(8,128)(2,1)} %get-tuple-element.62), channel_id=1, source_target_pairs={{0,64},{64,128},{128,192},{192,0},{1,65},{65,129},{129,193},{193,1... | collective-permute-start | bytes 1572872 | tf_op jit(solution)/shard_map/ppermute | solution.py:428
  218.9 20.0 %collective-permute-start.33 = (bf16[1024,256]{1,0:T(8,128)(2,1)}, bf16[1024,256]{1,0:T(8,128)(2,1)S(1)}, u32[]{:S(2)}, u32[]{:S(2)}) collective-permute-start(bf16[1024,256]{1,0:T(8,128)(2,1)} %get-tuple-element.63), channel_id=1, source_target_pairs={{0,128},{64,192},{128,0},{192,64},{1,129},{65,193},{129,1},{193,65... | collective-permute-start | bytes 1572872 | tf_op jit(solution)/shard_map/ppermute | solution.py:428
  221.6 17.3 %collective-permute-start.34 = (bf16[1024,256]{1,0:T(8,128)(2,1)}, bf16[1024,256]{1,0:T(8,128)(2,1)S(1)}, u32[]{:S(2)}, u32[]{:S(2)}) collective-permute-start(bf16[1024,256]{1,0:T(8,128)(2,1)} %get-tuple-element.64), channel_id=1, source_target_pairs={{0,192},{64,0},{128,64},{192,128},{1,193},{65,1},{129,65},{193,129... | collective-permute-start | bytes 1572872 | tf_op jit(solution)/shard_map/ppermute | solution.py:428
  (25 other events, 95.7 us)

commit v3 on v1

--- a/solution.py
+++ b/solution.py
@@ -271,7 +271,7 @@
 def opening_part(at, ws, mine, other):
     c, f = ws[0].shape
     t = mine[0].shape[0]
-    span = 2 * TOK
+    span = 4 * TOK
     chain = pl.BlockSpec((NY * CL, span), lambda i, at: (0, i))
     return pl.pallas_call(
         opening_kernel,
@@ -296,7 +296,7 @@
 def staying_part(at, ws, cot_all):
     c, f = ws[0].shape
     t = cot_all.shape[1]
-    span = 2 * TOK
+    span = 4 * TOK
     return pl.pallas_call(
         staying_kernel,
         grid_spec=pltpu.PrefetchScalarGridSpec(
@@ -312,7 +312,7 @@
 
 
 def weight_kernel(at, *refs):
-    pieces, cot_ref, outs, gated = refs[: NZ + 1], refs[NZ + 1], refs[NZ + 2 : -1], refs[-1]
+    pieces, cot_ref, outs, gated = refs[:NZ], refs[NZ], refs[NZ + 1 : -1], refs[-1]
     step = pl.program_id(0)
 
     @pl.when(step == 0)
@@ -426,15 +426,15 @@
     for _ in range(3):
         fore.append(shift(fore[-1], "z", 1))
         aft.append(shift(aft[-1], "z", -1))
-    half = NY * CL // 2
-    far = [shift(fore[-1][:half], "z", 1), shift(aft[-1][half:], "z", -1)]
-    ring = [gated] + aft[1:] + far + fore[:0:-1]
+    far = shift(fore[-1], "z", 1)
+    ring = [gated] + aft[1:] + [far] + fore[:0:-1]
 
     part = part.reshape(NY, CL, NZ * TOK)
     grad_gated = lax.all_to_all(part, "y", split_axis=0, concat_axis=0, tiled=True)
-    outs, skip_sum = back(grad_gated, cols, mixed, sig_spec, tap_spec, skip, tabs)
+    skip_again = jnp.broadcast_to(after(skip_gain, gated)[:, None], (CL, TOK))
+    outs, skip_sum = back(grad_gated, cols, mixed, sig_spec, tap_spec, skip_again, tabs)
     outs_rows = lax.all_to_all(outs, seq, split_axis=0, concat_axis=0, tiled=True)
-    kept, up1, up2, up3 = grad_weight_part(at, ring, cot_all)
+    kept, up1, up2, up3 = grad_weight_part(after(at, skip_sum), ring, cot_all)
     moved = [shift(up1, "y", 1), shift(up2, "y", 2), shift(up3, "y", -1)]
     weight = weight_sum(at, [kept] + moved)
     grad_input, grad_filter, grad_gate = to_rows(outs_rows)

time: 227 us -> 220 us (0.969)
  starting transfers between devices: 72.8 us -> 61.3 us
  waiting for transfers between devices: 94.6 us -> 99.5 us
    all_to_all x1, starting transfers between devices: 10.9 us -> 5.74 us  [ordered(): lax.all_to_all(outs, seq, split_axis=0, concat_axis=0, tiled=True)]
    all_to_all x1, waiting for transfers between devices: 0.01 us -> 4.82 us  [ordered(): gated = lax.all_to_all(gated, 'y', split_axis=0, concat_axis=0, tiled=True)]
    ppermute x28 -> x27, starting transfers between devices: 35.6 us -> 31.1 us  [shift(): lax.ppermute(value, axis, [(i, (i + by) % count) for i in range(count)])]
    all_to_all x1, waiting for transfers between devices: 0.15 us -> 4.33 us  [ordered(): lax.all_to_all(part, 'y', split_axis=0, concat_axis=0, tiled=True)]
    ppermute x28 -> x27, waiting for transfers between devices: 84.4 us -> 80.3 us  [shift(): lax.ppermute(value, axis, [(i, (i + by) % count) for i in range(count)])]
  transfers between devices with their start and end apart: 33 -> 32, of which waited for: 19 -> 20; matrix products, arithmetic and copies ran while one was open for 3% -> 5% of each run, Pallas kernels for 14% -> 14%
where the time goes in v3:
time: 220 us; the launch traced here: 217 us
  waiting for transfers between devices  99.5 us (45%)
  starting transfers between devices  61.3 us (28%)
  Pallas kernels  38.6 us (18%)
  other arithmetic  6.84 us (3%)
  local copies, waits for them, and re-layouts  6.34 us (3%)
  blocking collectives  3.94 us (2%)
    ppermute x27, waiting for transfers between devices, shift(): lax.ppermute(value, axis, [(i, (i + by) % count) for i in range(count)])  80.3 us
    ppermute x27, starting transfers between devices, shift(): lax.ppermute(value, axis, [(i, (i + by) % count) for i in range(count)])  31.1 us
    all_to_all x1, waiting for transfers between devices, ordered(): lax.all_to_all(pieces.reshape(NZ, TOK, TOK), 'z', split_axis=0, concat_ax...  10.1 us
    all_to_all x1, starting transfers between devices, ordered(): lax.all_to_all(pieces.reshape(NZ, TOK, TOK), 'z', split_axis=0, concat_ax...  8.57 us
    all_to_all x1, starting transfers between devices, ordered(): cols = lax.all_to_all(cols, seq, split_axis=0, concat_axis=0, tiled=True)  8.02 us
    pallas_call x1, Pallas kernels, grad_weight_part(): pl.pallas_call(weight_kernel, grid_spec=pltpu.PrefetchScalarGridSpec(num_...  7.29 us
    pallas_call x1, Pallas kernels, back(): pl.pallas_call(back_kernel, grid=(STEPS,), in_specs=[WIDE, PACK, PLAIN, S...  7.04 us
    pallas_call x1, Pallas kernels, conv(): pl.pallas_call(conv_kernel, grid=(STEPS,), in_specs=[PACK, LANE] + [whole...  5.88 us
  transfers between devices with their start and end apart: 32, of which 20 were waited for; matrix products, arithmetic and copies ran while one was open for 5% of the time, Pallas kernels for 14%

profile of v3, /device:TPU:32, one launch (start us, length us, event | category | flops | bytes accessed | tf_op | source)
XLA Modules:
  0.0 217.5 jit_solution(7436755604282392036)
XLA Ops:
  0.6 3.1 %collective-permute-start = (bf16[1024,256]{1,0:T(8,128)(2,1)}, bf16[1024,256]{1,0:T(8,128)(2,1)S(1)}, u32[]{:S(2)}, u32[]{:S(2)}) collective-permute-start(bf16[1024,256]{1,0:T(8,128)(2,1)} %w0.3), channel_id=1, source_target_pairs={{0,192},{64,0},{128,64},{192,128},{1,193},{65,1},{129,65},{193,129... | collective-permute-start | bytes 1572872 | tf_op jit(solution)/shard_map/ppermute | solution.py:377
  3.7 1.1 copy.17
  5.1 3.9 %all_to_all.30 = bf16[2,4,128,128]{3,1,2,0:T(4,128)(2,1)S(1)} all-to-all(bf16[2,4,128,128]{3,1,2,0:T(4,128)(2,1)S(1)} %copy.18), channel_id=1, replica_groups=mesh['y'=4,'z'=8,'x'=4,'core'=2] {'core'}, dimensions={0} | all-to-all | bytes 524288 | tf_op jit(solution)/shard_map/all_to_all | solution.py:394
  9.7 8.6 %all-to-all-start.1 = ((bf16[8,128,128]{2,1,0:T(8,128)(2,1)}), bf16[8,128,128]{2,1,0:T(8,128)(2,1)S(1)}, u32[]{:S(2)}, u32[]{:S(2)}) async-start(bf16[8,128,128]{2,1,0:T(8,128)(2,1)} %bitcast.6), calls=%async_computation.1 | async-start | bytes 524288 | tf_op jit(solution)/shard_map/all_to_all | solution.py:395
  18.9 10.1 %all-to-all-done.1 = bf16[8,128,128]{2,1,0:T(8,128)(2,1)S(1)} async-done(((bf16[8,128,128]{2,1,0:T(8,128)(2,1)}), bf16[8,128,128]{2,1,0:T(8,128)(2,1)S(1)}, u32[]{:S(2)}, u32[]{:S(2)}) %all-to-all-start.1) | async-done | bytes 262176 | tf_op jit(solution)/shard_map/all_to_all | solution.py:395
  29.0 2.8 %collective-permute-start.3 = (bf16[1024,128]{1,0:T(8,128)(2,1)S(1)}, bf16[1024,128]{1,0:T(8,128)(2,1)S(1)}, u32[]{:S(2)}, u32[]{:S(2)}) collective-permute-start(bf16[1024,128]{1,0:T(8,128)(2,1)S(1)} %bitcast.50), channel_id=1, source_target_pairs={{0,6},{2,0},{4,2},{6,4},{1,7},{3,1},{5,3},{7,5},{8,14},{10,8},{12,... | collective-permute-start | bytes 786440 | tf_op jit(solution)/shard_map/ppermute | solution.py:377
  33.5 1.3 collective-permute-done.1.w2
  34.8 5.7 %collective-permute-done.3.m1 = bf16[1024,128]{1,0:T(8,128)(2,1)S(1)} collective-permute-done((bf16[1024,128]{1,0:T(8,128)(2,1)S(1)}, bf16[1024,128]{1,0:T(8,128)(2,1)S(1)}, u32[]{:S(2)}, u32[]{:S(2)}) %collective-permute-start.3) | collective-permute-done | bytes 262176 | tf_op jit(solution)/shard_map/ppermute | solution.py:377
  41.5 2.8 %collective-permute-done.5.m3 = bf16[1024,128]{1,0:T(8,128)(2,1)S(1)} collective-permute-done((bf16[1024,128]{1,0:T(8,128)(2,1)S(1)}, bf16[1024,128]{1,0:T(8,128)(2,1)S(1)}, u32[]{:S(2)}, u32[]{:S(2)}) %collective-permute-start.5) | collective-permute-done | bytes 262176 | tf_op jit(solution)/shard_map/ppermute | solution.py:377
  46.2 5.4 %opening.1 = (bf16[4,1024,256]{2,1,0:T(8,128)(2,1)}, bf16[128,1024]{1,0:T(8,128)(2,1)}, bf16[128,1024]{1,0:T(8,128)(2,1)}) custom-call(s32[4]{0:T(128)} %pad_add_fusion.at, bf16[1024,256]{1,0:T(8,128)(2,1)} %w0.3, bf16[1024,256]{1,0:T(8,128)(2,1)} %copy-done.2, bf16[1024,256]{1,0:T(8,128)(2,1)} %copy-done.3, bf16[1024,256]{1,0:T(8,128)(2,1)} %copy-done.4, ...), custom_call_target="tpu_custom_call" | custom-call | tf_op jit(solution)/shard_map/opening/pallas_call | solution.py:276
  51.6 1.1 collective-permute-start.10
  52.8 1.7 collective-permute-start.11
  54.5 2.1 to_cols.1
  56.6 8.0 %all-to-all-start.3 = ((bf16[32,3,32,128]{3,2,1,0:T(8,128)(2,1)}), bf16[32,3,32,128]{3,2,1,0:T(8,128)(2,1)S(1)}, u32[]{:S(2)}, u32[]{:S(2)}) async-start(bf16[32,3,32,128]{3,2,1,0:T(8,128)(2,1)} %to_cols.1), calls=%async_computation.3 | async-start | bytes 1572864 | tf_op jit(solution)/shard_map/all_to_all | solution.py:399
  64.6 5.8 %staying.1 = f32[6,128,1024]{2,1,0:T(8,128)} custom-call(s32[4]{0:T(128)} %pad_add_fusion.at, bf16[1024,256]{1,0:T(8,128)(2,1)} %w0.3, bf16[1024,256]{1,0:T(8,128)(2,1)} %copy-done.2, bf16[1024,256]{1,0:T(8,128)(2,1)} %copy-done.3, bf16[1024,256]{1,0:T(8,128)(2,1)} %copy-done.4, bf16[4,1024,256]{2,1,0:T(8,128)(2,1)} %get-tuple-element.33.cot_ref.refs_8_), custom_call_target="tpu_custom_call" | custom-call | tf_op jit(solution)/shard_map/staying/pallas_call | solution.py:300
  70.4 1.4 fusion.10
  71.8 1.5 collective-permute-start.12
  73.9 13.8 %collective-permute-done.12 = bf16[128,1024]{1,0:T(8,128)(2,1)S(1)} collective-permute-done((bf16[128,1024]{1,0:T(8,128)(2,1)S(1)}, bf16[128,1024]{1,0:T(8,128)(2,1)S(1)}, u32[]{:S(2)}, u32[]{:S(2)}) %collective-permute-start.12) | collective-permute-done | bytes 262176 | tf_op jit(solution)/shard_map/ppermute | solution.py:377
  87.7 1.2 collective-permute-done.13
  88.9 1.3 fusion.6
  90.2 1.6 collective-permute-start.14
  92.4 5.3 %collective-permute-done.14 = bf16[128,1024]{1,0:T(8,128)(2,1)S(1)} collective-permute-done((bf16[128,1024]{1,0:T(8,128)(2,1)S(1)}, bf16[128,1024]{1,0:T(8,128)(2,1)S(1)}, u32[]{:S(2)}, u32[]{:S(2)}) %collective-permute-start.14) | collective-permute-done | bytes 262176 | tf_op jit(solution)/shard_map/ppermute | solution.py:377
  97.7 2.0 collective-permute-done.15
  100.8 1.8 collective-permute-start.16
  103.5 5.9 %conv.1 = (bf16[32,32,128]{2,1,0:T(8,128)(2,1)}, bf16[4,32,1024]{2,1,0:T(8,128)(2,1)}, f32[1024,256]{1,0:T(8,128)}, f32[1024,256]{1,0:T(8,128)}) custom-call(bf16[32,3,32,128]{3,2,1,0:T(8,128)(2,1)} %copy-done, f32[32,128]{1,0:T(8,128)} %broadcast_in_dim.4.skip_ref, bf16[64,64]{1,0:T(8,128)(2,1)} %constant.28.clone.a_ref, ...), custom_call_target="tpu_custom_call" | custom-call | tf_op jit(solution)/shard_map/conv/pallas_call | solution.py:164
  109.4 4.4 %all-to-all-start.4 = ((bf16[4,32,1024]{2,1,0:T(8,128)(2,1)}), bf16[4,32,1024]{2,1,0:T(8,128)(2,1)S(1)}, u32[]{:S(2)}, u32[]{:S(2)}) async-start(bf16[4,32,1024]{2,1,0:T(8,128)(2,1)} %get-tuple-element.43), calls=%async_computation.4 | async-start | bytes 524288 | tf_op jit(solution)/shard_map/all_to_all | solution.py:406
  113.8 1.9 fusion.2
  115.7 4.8 %all-to-all-done.4 = bf16[4,32,1024]{2,1,0:T(8,128)(2,1)S(1)} async-done(((bf16[4,32,1024]{2,1,0:T(8,128)(2,1)}), bf16[4,32,1024]{2,1,0:T(8,128)(2,1)S(1)}, u32[]{:S(2)}, u32[]{:S(2)}) %all-to-all-start.4) | async-done | bytes 262176 | tf_op jit(solution)/shard_map/all_to_all | solution.py:406
  120.5 3.4 %all-to-all-start.2 = ((bf16[4,32,1024]{2,1,0:T(8,128)(2,1)}), bf16[4,32,1024]{2,1,0:T(8,128)(2,1)S(1)}, u32[]{:S(2)}, u32[]{:S(2)}) async-start(bf16[4,32,1024]{2,1,0:T(8,128)(2,1)} %bitcast.14), calls=%async_computation.2 | async-start | bytes 524288 | tf_op jit(solution)/shard_map/all_to_all | solution.py:433
  123.9 2.3 %collective-permute-start.20 = (bf16[128,1024]{1,0:T(8,128)(2,1)S(1)}, bf16[128,1024]{1,0:T(8,128)(2,1)S(1)}, u32[]{:S(2)}, u32[]{:S(2)}) collective-permute-start(bf16[128,1024]{1,0:T(8,128)(2,1)S(1)} %bitcast.55), channel_id=1, source_target_pairs={{0,8},{8,16},{16,24},{24,32},{32,40},{40,48},{48,56},{56,0},{1,9},... | collective-permute-start | bytes 786440 | tf_op jit(solution)/shard_map/ppermute | solution.py:377
  126.2 4.3 %all-to-all-done.2.gg_ref = bf16[4,32,1024]{2,1,0:T(8,128)(2,1)S(1)} async-done(((bf16[4,32,1024]{2,1,0:T(8,128)(2,1)}), bf16[4,32,1024]{2,1,0:T(8,128)(2,1)S(1)}, u32[]{:S(2)}, u32[]{:S(2)}) %all-to-all-start.2) | async-done | bytes 262176 | tf_op jit(solution)/shard_map/all_to_all | solution.py:433
  131.3 7.0 %back.1 = (bf16[32,3,32,128]{3,2,1,0:T(8,128)(2,1)}, f32[32,128]{1,0:T(8,128)}) custom-call(bf16[4,32,1024]{2,1,0:T(8,128)(2,1)} %copy-done.7, bf16[32,3,32,128]{3,2,1,0:T(8,128)(2,1)} %copy-done, bf16[32,32,128]{2,1,0:T(8,128)(2,1)} %get-tuple-element.40.mixed_ref, f32[1024,256]{1,0:T(8,128)} %get-tuple-element.41.sig_ref, ...), custom_call_target="tpu_custom_call" | custom-call | tf_op jit(solution)/shard_map/back/pallas_call | solution.py:181
  138.3 5.7 %all-to-all-start.5 = ((bf16[32,3,32,128]{3,2,1,0:T(8,128)(2,1)}), bf16[32,3,32,128]{3,2,1,0:T(8,128)(2,1)S(1)}, u32[]{:S(2)}, u32[]{:S(2)}) async-start(bf16[32,3,32,128]{3,2,1,0:T(8,128)(2,1)} %get-tuple-element.45), calls=%async_computation.5 | async-start | bytes 1572864 | tf_op jit(solution)/shard_map/all_to_all | solution.py:436
  144.4 1.8 collective-permute-start.21
  146.2 19.3 %collective-permute-done.17.refs_1_ = bf16[128,1024]{1,0:T(8,128)(2,1)S(1)} collective-permute-done((bf16[128,1024]{1,0:T(8,128)(2,1)S(1)}, bf16[128,1024]{1,0:T(8,128)(2,1)S(1)}, u32[]{:S(2)}, u32[]{:S(2)}) %collective-permute-start.17) | collective-permute-done | bytes 262176 | tf_op jit(solution)/shard_map/ppermute | solution.py:377
  166.2 1.3 collective-permute-start.22
  167.5 5.1 %collective-permute-done.18.refs_2_ = bf16[128,1024]{1,0:T(8,128)(2,1)S(1)} collective-permute-done((bf16[128,1024]{1,0:T(8,128)(2,1)S(1)}, bf16[128,1024]{1,0:T(8,128)(2,1)S(1)}, u32[]{:S(2)}, u32[]{:S(2)}) %collective-permute-start.18) | collective-permute-done | bytes 262176 | tf_op jit(solution)/shard_map/ppermute | solution.py:377
  172.6 2.5 %collective-permute-start.19 = (bf16[128,1024]{1,0:T(8,128)(2,1)S(1)}, bf16[128,1024]{1,0:T(8,128)(2,1)S(1)}, u32[]{:S(2)}, u32[]{:S(2)}) collective-permute-start(bf16[128,1024]{1,0:T(8,128)(2,1)S(1)} %collective-permute-done.18.refs_2_), channel_id=1, source_target_pairs={{0,56},{8,0},{16,8},{24,16},{32,24},{40,32},{48,40},{56,48},{1,57}... | collective-permute-start | bytes 786440 | tf_op jit(solution)/shard_map/ppermute | solution.py:377
  175.1 3.9 %collective-permute-done.19.refs_3_ = bf16[128,1024]{1,0:T(8,128)(2,1)S(1)} collective-permute-done((bf16[128,1024]{1,0:T(8,128)(2,1)S(1)}, bf16[128,1024]{1,0:T(8,128)(2,1)S(1)}, u32[]{:S(2)}, u32[]{:S(2)}) %collective-permute-start.19) | collective-permute-done | bytes 262176 | tf_op jit(solution)/shard_map/ppermute | solution.py:377
  179.0 2.5 %collective-permute-done.23.refs_4_ = bf16[128,1024]{1,0:T(8,128)(2,1)S(1)} collective-permute-done((bf16[128,1024]{1,0:T(8,128)(2,1)S(1)}, bf16[128,1024]{1,0:T(8,128)(2,1)S(1)}, u32[]{:S(2)}, u32[]{:S(2)}) %collective-permute-start.23) | collective-permute-done | bytes 262176 | tf_op jit(solution)/shard_map/ppermute | solution.py:377
  182.2 7.3 %grad_weight.1 = (bf16[1024,256]{1,0:T(8,128)(2,1)}, bf16[1024,256]{1,0:T(8,128)(2,1)}, bf16[1024,256]{1,0:T(8,128)(2,1)}, bf16[1024,256]{1,0:T(8,128)(2,1)}) custom-call(s32[4]{0:T(128)} %pad_add_fusion.at, bf16[128,1024]{1,0:T(8,128)(2,1)} %bitcast.57, bf16[128,1024]{1,0:T(8,128)(2,1)} %copy-done.18, bf16[128,1024]{1,0:T(8,128)(2,1)} %copy-done.20, ...), custom_call_target="tpu_custom_call" | custom-call | tf_op jit(solution)/shard_map/grad_weight/pallas_call | solution.py:335
  189.5 1.2 collective-permute-start.24
  190.7 2.6 %collective-permute-start.25 = (bf16[1024,256]{1,0:T(8,128)(2,1)}, bf16[1024,256]{1,0:T(8,128)(2,1)S(1)}, u32[]{:S(2)}, u32[]{:S(2)}) collective-permute-start(bf16[1024,256]{1,0:T(8,128)(2,1)} %get-tuple-element.53), channel_id=1, source_target_pairs={{0,128},{64,192},{128,0},{192,64},{1,129},{65,193},{129,1},{193,65... | collective-permute-start | bytes 1572872 | tf_op jit(solution)/shard_map/ppermute | solution.py:377
  193.3 1.3 collective-permute-start.26
  195.3 9.6 %collective-permute-done.24.b_ref = bf16[1024,256]{1,0:T(8,128)(2,1)S(1)} collective-permute-done((bf16[1024,256]{1,0:T(8,128)(2,1)}, bf16[1024,256]{1,0:T(8,128)(2,1)S(1)}, u32[]{:S(2)}, u32[]{:S(2)}) %collective-permute-start.24) | collective-permute-done | bytes 524320 | tf_op jit(solution)/shard_map/ppermute | solution.py:377
  204.9 5.6 %collective-permute-done.25.c_ref = bf16[1024,256]{1,0:T(8,128)(2,1)S(1)} collective-permute-done((bf16[1024,256]{1,0:T(8,128)(2,1)}, bf16[1024,256]{1,0:T(8,128)(2,1)S(1)}, u32[]{:S(2)}, u32[]{:S(2)}) %collective-permute-start.25) | collective-permute-done | bytes 524320 | tf_op jit(solution)/shard_map/ppermute | solution.py:377
  211.4 3.1 %weight_sum.1 = f32[4,8,32,256]{3,2,1,0:T(8,128)} custom-call(s32[4]{0:T(128)} %pad_add_fusion.at, bf16[1024,256]{1,0:T(8,128)(2,1)} %get-tuple-element.51.a_ref, bf16[1024,256]{1,0:T(8,128)(2,1)} %copy-done.8, bf16[1024,256]{1,0:T(8,128)(2,1)} %copy-done.9, bf16[1024,256]{1,0:T(8,128)(2,1)} %copy-done.10), custom_call_target="tpu_custom_call" | custom-call | tf_op jit(solution)/shard_map/weight_sum/pallas_call | solution.py:362
  215.5 2.0 to_rows.1
  (88 shorter events, 14.1 us)
Async XLA Ops:
  0.6 32.0 %collective-permute-start = (bf16[1024,256]{1,0:T(8,128)(2,1)}, bf16[1024,256]{1,0:T(8,128)(2,1)S(1)}, u32[]{:S(2)}, u32[]{:S(2)}) collective-permute-start(bf16[1024,256]{1,0:T(8,128)(2,1)} %w0.3), channel_id=1, source_target_pairs={{0,192},{64,0},{128,64},{192,128},{1,193},{65,1},{129,65},{193,129... | collective-permute-start | bytes 1572872 | tf_op jit(solution)/shard_map/ppermute | solution.py:377
  9.7 19.3 %all-to-all-start.1 = ((bf16[8,128,128]{2,1,0:T(8,128)(2,1)}), bf16[8,128,128]{2,1,0:T(8,128)(2,1)S(1)}, u32[]{:S(2)}, u32[]{:S(2)}) async-start(bf16[8,128,128]{2,1,0:T(8,128)(2,1)} %bitcast.6), calls=%async_computation.1 | async-start | bytes 524288 | tf_op jit(solution)/shard_map/all_to_all | solution.py:395
  18.3 16.5 %collective-permute-start.1 = (bf16[1024,256]{1,0:T(8,128)(2,1)}, bf16[1024,256]{1,0:T(8,128)(2,1)S(1)}, u32[]{:S(2)}, u32[]{:S(2)}) collective-permute-start(bf16[1024,256]{1,0:T(8,128)(2,1)} %w0.3), channel_id=1, source_target_pairs={{0,128},{64,192},{128,0},{192,64},{1,129},{65,193},{129,1},{193,65... | collective-permute-start | bytes 1572872 | tf_op jit(solution)/shard_map/ppermute | solution.py:377
  29.0 16.9 %copy-start.5 = (bf16[8,128,128]{2,1,0:T(8,128)(2,1)}, bf16[8,128,128]{2,1,0:T(8,128)(2,1)S(1)}, u32[]{:S(2)}) copy-start(bf16[8,128,128]{2,1,0:T(8,128)(2,1)S(1)} %all-to-all-done.1) | copy-start | bytes 786436
  29.0 11.5 %collective-permute-start.3 = (bf16[1024,128]{1,0:T(8,128)(2,1)S(1)}, bf16[1024,128]{1,0:T(8,128)(2,1)S(1)}, u32[]{:S(2)}, u32[]{:S(2)}) collective-permute-start(bf16[1024,128]{1,0:T(8,128)(2,1)S(1)} %bitcast.50), channel_id=1, source_target_pairs={{0,6},{2,0},{4,2},{6,4},{1,7},{3,1},{5,3},{7,5},{8,14},{10,8},{12,... | collective-permute-start | bytes 786440 | tf_op jit(solution)/shard_map/ppermute | solution.py:377
  31.8 13.3 %collective-permute-start.2 = (bf16[1024,256]{1,0:T(8,128)(2,1)}, bf16[1024,256]{1,0:T(8,128)(2,1)S(1)}, u32[]{:S(2)}, u32[]{:S(2)}) collective-permute-start(bf16[1024,256]{1,0:T(8,128)(2,1)} %w0.3), channel_id=1, source_target_pairs={{0,64},{64,128},{128,192},{192,0},{1,65},{65,129},{129,193},{193,1... | collective-permute-start | bytes 1572872 | tf_op jit(solution)/shard_map/ppermute | solution.py:377
  31.8 9.7 %collective-permute-start.4 = (bf16[1024,128]{1,0:T(8,128)(2,1)S(1)}, bf16[1024,128]{1,0:T(8,128)(2,1)S(1)}, u32[]{:S(2)}, u32[]{:S(2)}) collective-permute-start(bf16[1024,128]{1,0:T(8,128)(2,1)S(1)} %bitcast.51), channel_id=1, source_target_pairs={{0,4},{2,6},{4,0},{6,2},{1,5},{3,7},{5,1},{7,3},{8,12},{10,14},{12... | collective-permute-start | bytes 786440 | tf_op jit(solution)/shard_map/ppermute | solution.py:377
  32.6 13.3 %copy-start.2 = (bf16[1024,256]{1,0:T(8,128)(2,1)}, bf16[1024,256]{1,0:T(8,128)(2,1)S(1)}, u32[]{:S(2)}) copy-start(bf16[1024,256]{1,0:T(8,128)(2,1)S(1)} %collective-permute-done.w1) | copy-start | bytes 1572868
  32.6 11.6 %collective-permute-start.5 = (bf16[1024,128]{1,0:T(8,128)(2,1)S(1)}, bf16[1024,128]{1,0:T(8,128)(2,1)S(1)}, u32[]{:S(2)}, u32[]{:S(2)}) collective-permute-start(bf16[1024,128]{1,0:T(8,128)(2,1)S(1)} %bitcast.52), channel_id=1, source_target_pairs={{0,2},{2,4},{4,6},{6,0},{1,3},{3,5},{5,7},{7,1},{8,10},{10,12},{12... | collective-permute-start | bytes 786440 | tf_op jit(solution)/shard_map/ppermute | solution.py:377
  34.8 11.1 %copy-start.3 = (bf16[1024,256]{1,0:T(8,128)(2,1)}, bf16[1024,256]{1,0:T(8,128)(2,1)S(1)}, u32[]{:S(2)}) copy-start(bf16[1024,256]{1,0:T(8,128)(2,1)S(1)} %collective-permute-done.1.w2) | copy-start | bytes 1572868
  34.8 10.3 %collective-permute-start.6 = (bf16[1024,128]{1,0:T(8,128)(2,1)S(1)}, bf16[1024,128]{1,0:T(8,128)(2,1)S(1)}, u32[]{:S(2)}, u32[]{:S(2)}) collective-permute-start(bf16[1024,128]{1,0:T(8,128)(2,1)S(1)} %bitcast.53), channel_id=1, source_target_pairs={{0,1},{1,0},{2,3},{3,2},{4,5},{5,4},{6,7},{7,6},{8,9},{9,8},{10,11... | collective-permute-start | bytes 786440 | tf_op jit(solution)/shard_map/ppermute | solution.py:377
  40.5 5.4 %copy-start.11 = (bf16[1024,128]{1,0:T(8,128)(2,1)}, bf16[1024,128]{1,0:T(8,128)(2,1)S(1)}, u32[]{:S(2)}) copy-start(bf16[1024,128]{1,0:T(8,128)(2,1)S(1)} %collective-permute-done.3.m1) | copy-start | bytes 786436
  40.5 4.6 %collective-permute-start.7 = (bf16[1024,128]{1,0:T(8,128)(2,1)S(1)}, bf16[1024,128]{1,0:T(8,128)(2,1)S(1)}, u32[]{:S(2)}, u32[]{:S(2)}) collective-permute-start(bf16[1024,128]{1,0:T(8,128)(2,1)S(1)} %collective-permute-done.3.m1), channel_id=1, source_target_pairs={{0,1},{1,0},{2,3},{3,2},{4,5},{5,4},{6,7},{7,6},{8,9},{9,8},{10,11... | collective-permute-start | bytes 786440 | tf_op jit(solution)/shard_map/ppermute | solution.py:377
  41.5 4.5 %copy-start.12 = (bf16[1024,128]{1,0:T(8,128)(2,1)}, bf16[1024,128]{1,0:T(8,128)(2,1)S(1)}, u32[]{:S(2)}) copy-start(bf16[1024,128]{1,0:T(8,128)(2,1)S(1)} %collective-permute-done.4.m2) | copy-start | bytes 786436
  41.5 3.7 %collective-permute-start.8 = (bf16[1024,128]{1,0:T(8,128)(2,1)S(1)}, bf16[1024,128]{1,0:T(8,128)(2,1)S(1)}, u32[]{:S(2)}, u32[]{:S(2)}) collective-permute-start(bf16[1024,128]{1,0:T(8,128)(2,1)S(1)} %collective-permute-done.4.m2), channel_id=1, source_target_pairs={{0,1},{1,0},{2,3},{3,2},{4,5},{5,4},{6,7},{7,6},{8,9},{9,8},{10,11... | collective-permute-start | bytes 786440 | tf_op jit(solution)/shard_map/ppermute | solution.py:377
  44.2 1.7 copy-start.13
  44.2 1.7 collective-permute-start.9
  51.6 18.8 %collective-permute-start.10 = (bf16[128,1024]{1,0:T(8,128)(2,1)}, bf16[128,1024]{1,0:T(8,128)(2,1)S(1)}, u32[]{:S(2)}, u32[]{:S(2)}) collective-permute-start(bf16[128,1024]{1,0:T(8,128)(2,1)} %get-tuple-element.30), channel_id=1, source_target_pairs={{0,8},{8,16},{16,24},{24,32},{32,40},{40,48},{48,56},{56,0},{1,9},... | collective-permute-start | bytes 786440 | tf_op jit(solution)/shard_map/ppermute | solution.py:377
  52.8 17.7 %collective-permute-start.11 = (bf16[128,1024]{1,0:T(8,128)(2,1)}, bf16[128,1024]{1,0:T(8,128)(2,1)S(1)}, u32[]{:S(2)}, u32[]{:S(2)}) collective-permute-start(bf16[128,1024]{1,0:T(8,128)(2,1)} %get-tuple-element.31), channel_id=1, source_target_pairs={{0,56},{8,0},{16,8},{24,16},{32,24},{40,32},{48,40},{56,48},{1,57}... | collective-permute-start | bytes 786440 | tf_op jit(solution)/shard_map/ppermute | solution.py:377
  56.6 46.0 %all-to-all-start.3 = ((bf16[32,3,32,128]{3,2,1,0:T(8,128)(2,1)}), bf16[32,3,32,128]{3,2,1,0:T(8,128)(2,1)S(1)}, u32[]{:S(2)}, u32[]{:S(2)}) async-start(bf16[32,3,32,128]{3,2,1,0:T(8,128)(2,1)} %to_cols.1), calls=%async_computation.3 | async-start | bytes 1572864 | tf_op jit(solution)/shard_map/all_to_all | solution.py:399
  70.4 32.2 %copy-start.25 = (f32[32]{0:T(128)S(1)}, f32[32]{0:T(128)}, u32[]{:S(2)}) copy-start(f32[32]{0:T(128)} %param.14) | copy-start | bytes 388
  71.8 15.9 %collective-permute-start.12 = (bf16[128,1024]{1,0:T(8,128)(2,1)S(1)}, bf16[128,1024]{1,0:T(8,128)(2,1)S(1)}, u32[]{:S(2)}, u32[]{:S(2)}) collective-permute-start(bf16[128,1024]{1,0:T(8,128)(2,1)S(1)} %get-tuple-element.58), channel_id=1, source_target_pairs={{0,8},{8,16},{16,24},{24,32},{32,40},{40,48},{48,56},{56,0},{1,9},... | collective-permute-start | bytes 786440 | tf_op jit(solution)/shard_map/ppermute | solution.py:377
  73.3 15.6 %collective-permute-start.13 = (bf16[128,1024]{1,0:T(8,128)(2,1)S(1)}, bf16[128,1024]{1,0:T(8,128)(2,1)S(1)}, u32[]{:S(2)}, u32[]{:S(2)}) collective-permute-start(bf16[128,1024]{1,0:T(8,128)(2,1)S(1)} %get-tuple-element.57), channel_id=1, source_target_pairs={{0,56},{8,0},{16,8},{24,16},{32,24},{40,32},{48,40},{56,48},{1,57}... | collective-permute-start | bytes 786440 | tf_op jit(solution)/shard_map/ppermute | solution.py:377
  90.2 7.4 %collective-permute-start.14 = (bf16[128,1024]{1,0:T(8,128)(2,1)S(1)}, bf16[128,1024]{1,0:T(8,128)(2,1)S(1)}, u32[]{:S(2)}, u32[]{:S(2)}) collective-permute-start(bf16[128,1024]{1,0:T(8,128)(2,1)S(1)} %get-tuple-element.56), channel_id=1, source_target_pairs={{0,8},{8,16},{16,24},{24,32},{32,40},{40,48},{48,56},{56,0},{1,9},... | collective-permute-start | bytes 786440 | tf_op jit(solution)/shard_map/ppermute | solution.py:377
  91.8 7.9 %collective-permute-start.15 = (bf16[128,1024]{1,0:T(8,128)(2,1)S(1)}, bf16[128,1024]{1,0:T(8,128)(2,1)S(1)}, u32[]{:S(2)}, u32[]{:S(2)}) collective-permute-start(bf16[128,1024]{1,0:T(8,128)(2,1)S(1)} %get-tuple-element.55), channel_id=1, source_target_pairs={{0,56},{8,0},{16,8},{24,16},{32,24},{40,32},{48,40},{56,48},{1,57}... | collective-permute-start | bytes 786440 | tf_op jit(solution)/shard_map/ppermute | solution.py:377
  100.8 13.0 %collective-permute-start.16 = (bf16[128,1024]{1,0:T(8,128)(2,1)S(1)}, bf16[128,1024]{1,0:T(8,128)(2,1)S(1)}, u32[]{:S(2)}, u32[]{:S(2)}) collective-permute-start(bf16[128,1024]{1,0:T(8,128)(2,1)S(1)} %fusion.4), channel_id=1, source_target_pairs={{0,8},{8,16},{16,24},{24,32},{32,40},{40,48},{48,56},{56,0},{1,9},... | collective-permute-start | bytes 786440 | tf_op jit(solution)/shard_map/ppermute | solution.py:377
  109.4 11.1 %all-to-all-start.4 = ((bf16[4,32,1024]{2,1,0:T(8,128)(2,1)}), bf16[4,32,1024]{2,1,0:T(8,128)(2,1)S(1)}, u32[]{:S(2)}, u32[]{:S(2)}) async-start(bf16[4,32,1024]{2,1,0:T(8,128)(2,1)} %get-tuple-element.43), calls=%async_computation.4 | async-start | bytes 524288 | tf_op jit(solution)/shard_map/all_to_all | solution.py:406
  120.5 61.0 %copy-start.6 = (bf16[4,32,1024]{2,1,0:T(8,128)(2,1)}, bf16[4,32,1024]{2,1,0:T(8,128)(2,1)S(1)}, u32[]{:S(2)}) copy-start(bf16[4,32,1024]{2,1,0:T(8,128)(2,1)S(1)} %all-to-all-done.4) | copy-start | bytes 786436
  120.5 10.1 %all-to-all-start.2 = ((bf16[4,32,1024]{2,1,0:T(8,128)(2,1)}), bf16[4,32,1024]{2,1,0:T(8,128)(2,1)S(1)}, u32[]{:S(2)}, u32[]{:S(2)}) async-start(bf16[4,32,1024]{2,1,0:T(8,128)(2,1)} %bitcast.14), calls=%async_computation.2 | async-start | bytes 524288 | tf_op jit(solution)/shard_map/all_to_all | solution.py:433
  123.9 20.5 %collective-permute-start.20 = (bf16[128,1024]{1,0:T(8,128)(2,1)S(1)}, bf16[128,1024]{1,0:T(8,128)(2,1)S(1)}, u32[]{:S(2)}, u32[]{:S(2)}) collective-permute-start(bf16[128,1024]{1,0:T(8,128)(2,1)S(1)} %bitcast.55), channel_id=1, source_target_pairs={{0,8},{8,16},{16,24},{24,32},{32,40},{40,48},{48,56},{56,0},{1,9},... | collective-permute-start | bytes 786440 | tf_op jit(solution)/shard_map/ppermute | solution.py:377
  138.3 56.3 %copy-start.24 = (f32[32,128]{1,0:T(8,128)S(1)}, f32[32,128]{1,0:T(8,128)}, u32[]{:S(2)}) copy-start(f32[32,128]{1,0:T(8,128)} %get-tuple-element.49) | copy-start | bytes 49156
  138.3 76.2 %all-to-all-start.5 = ((bf16[32,3,32,128]{3,2,1,0:T(8,128)(2,1)}), bf16[32,3,32,128]{3,2,1,0:T(8,128)(2,1)S(1)}, u32[]{:S(2)}, u32[]{:S(2)}) async-start(bf16[32,3,32,128]{3,2,1,0:T(8,128)(2,1)} %get-tuple-element.45), calls=%async_computation.5 | async-start | bytes 1572864 | tf_op jit(solution)/shard_map/all_to_all | solution.py:436
  144.1 21.4 %collective-permute-start.17 = (bf16[128,1024]{1,0:T(8,128)(2,1)S(1)}, bf16[128,1024]{1,0:T(8,128)(2,1)S(1)}, u32[]{:S(2)}, u32[]{:S(2)}) collective-permute-start(bf16[128,1024]{1,0:T(8,128)(2,1)S(1)} %bitcast.56), channel_id=1, source_target_pairs={{0,56},{8,0},{16,8},{24,16},{32,24},{40,32},{48,40},{56,48},{1,57}... | collective-permute-start | bytes 786440 | tf_op jit(solution)/shard_map/ppermute | solution.py:377
  144.4 37.1 %copy-start.14 = (bf16[128,1024]{1,0:T(8,128)(2,1)}, bf16[128,1024]{1,0:T(8,128)(2,1)S(1)}, u32[]{:S(2)}) copy-start(bf16[128,1024]{1,0:T(8,128)(2,1)S(1)} %collective-permute-done.20.refs_7_) | copy-start | bytes 786436
  144.4 21.8 %collective-permute-start.21 = (bf16[128,1024]{1,0:T(8,128)(2,1)S(1)}, bf16[128,1024]{1,0:T(8,128)(2,1)S(1)}, u32[]{:S(2)}, u32[]{:S(2)}) collective-permute-start(bf16[128,1024]{1,0:T(8,128)(2,1)S(1)} %collective-permute-done.20.refs_7_), channel_id=1, source_target_pairs={{0,8},{8,16},{16,24},{24,32},{32,40},{40,48},{48,56},{56,0},{1,9},... | collective-permute-start | bytes 786440 | tf_op jit(solution)/shard_map/ppermute | solution.py:377
  165.5 16.0 %copy-start.18 = (bf16[128,1024]{1,0:T(8,128)(2,1)}, bf16[128,1024]{1,0:T(8,128)(2,1)S(1)}, u32[]{:S(2)}) copy-start(bf16[128,1024]{1,0:T(8,128)(2,1)S(1)} %collective-permute-done.17.refs_1_) | copy-start | bytes 786436
  165.5 7.1 %collective-permute-start.18 = (bf16[128,1024]{1,0:T(8,128)(2,1)S(1)}, bf16[128,1024]{1,0:T(8,128)(2,1)S(1)}, u32[]{:S(2)}, u32[]{:S(2)}) collective-permute-start(bf16[128,1024]{1,0:T(8,128)(2,1)S(1)} %collective-permute-done.17.refs_1_), channel_id=1, source_target_pairs={{0,56},{8,0},{16,8},{24,16},{32,24},{40,32},{48,40},{56,48},{1,57}... | collective-permute-start | bytes 786440 | tf_op jit(solution)/shard_map/ppermute | solution.py:377
  166.2 15.3 %copy-start.19 = (bf16[128,1024]{1,0:T(8,128)(2,1)}, bf16[128,1024]{1,0:T(8,128)(2,1)S(1)}, u32[]{:S(2)}) copy-start(bf16[128,1024]{1,0:T(8,128)(2,1)S(1)} %collective-permute-done.21.refs_6_) | copy-start | bytes 786436
  166.2 8.9 %collective-permute-start.22 = (bf16[128,1024]{1,0:T(8,128)(2,1)S(1)}, bf16[128,1024]{1,0:T(8,128)(2,1)S(1)}, u32[]{:S(2)}, u32[]{:S(2)}) collective-permute-start(bf16[128,1024]{1,0:T(8,128)(2,1)S(1)} %collective-permute-done.21.refs_6_), channel_id=1, source_target_pairs={{0,8},{8,16},{16,24},{24,32},{32,40},{40,48},{48,56},{56,0},{1,9},... | collective-permute-start | bytes 786440 | tf_op jit(solution)/shard_map/ppermute | solution.py:377
  172.6 8.9 %copy-start.20 = (bf16[128,1024]{1,0:T(8,128)(2,1)}, bf16[128,1024]{1,0:T(8,128)(2,1)S(1)}, u32[]{:S(2)}) copy-start(bf16[128,1024]{1,0:T(8,128)(2,1)S(1)} %collective-permute-done.18.refs_2_) | copy-start | bytes 786436
  172.6 6.4 %collective-permute-start.19 = (bf16[128,1024]{1,0:T(8,128)(2,1)S(1)}, bf16[128,1024]{1,0:T(8,128)(2,1)S(1)}, u32[]{:S(2)}, u32[]{:S(2)}) collective-permute-start(bf16[128,1024]{1,0:T(8,128)(2,1)S(1)} %collective-permute-done.18.refs_2_), channel_id=1, source_target_pairs={{0,56},{8,0},{16,8},{24,16},{32,24},{40,32},{48,40},{56,48},{1,57}... | collective-permute-start | bytes 786440 | tf_op jit(solution)/shard_map/ppermute | solution.py:377
  175.1 6.4 %copy-start.21 = (bf16[128,1024]{1,0:T(8,128)(2,1)}, bf16[128,1024]{1,0:T(8,128)(2,1)S(1)}, u32[]{:S(2)}) copy-start(bf16[128,1024]{1,0:T(8,128)(2,1)S(1)} %collective-permute-done.22.refs_5_) | copy-start | bytes 786436
  175.1 6.4 %collective-permute-start.23 = (bf16[128,1024]{1,0:T(8,128)(2,1)S(1)}, bf16[128,1024]{1,0:T(8,128)(2,1)S(1)}, u32[]{:S(2)}, u32[]{:S(2)}) collective-permute-start(bf16[128,1024]{1,0:T(8,128)(2,1)S(1)} %collective-permute-done.22.refs_5_), channel_id=1, source_target_pairs={{0,8},{8,16},{16,24},{24,32},{32,40},{40,48},{48,56},{56,0},{1,9},... | collective-permute-start | bytes 786440 | tf_op jit(solution)/shard_map/ppermute | solution.py:377
  179.0 2.5 %copy-start.22 = (bf16[128,1024]{1,0:T(8,128)(2,1)}, bf16[128,1024]{1,0:T(8,128)(2,1)S(1)}, u32[]{:S(2)}) copy-start(bf16[128,1024]{1,0:T(8,128)(2,1)S(1)} %collective-permute-done.19.refs_3_) | copy-start | bytes 786436
  189.5 15.3 %collective-permute-start.24 = (bf16[1024,256]{1,0:T(8,128)(2,1)}, bf16[1024,256]{1,0:T(8,128)(2,1)S(1)}, u32[]{:S(2)}, u32[]{:S(2)}) collective-permute-start(bf16[1024,256]{1,0:T(8,128)(2,1)} %get-tuple-element.52), channel_id=1, source_target_pairs={{0,64},{64,128},{128,192},{192,0},{1,65},{65,129},{129,193},{193,1... | collective-permute-start | bytes 1572872 | tf_op jit(solution)/shard_map/ppermute | solution.py:377
  190.7 19.8 %collective-permute-start.25 = (bf16[1024,256]{1,0:T(8,128)(2,1)}, bf16[1024,256]{1,0:T(8,128)(2,1)S(1)}, u32[]{:S(2)}, u32[]{:S(2)}) collective-permute-start(bf16[1024,256]{1,0:T(8,128)(2,1)} %get-tuple-element.53), channel_id=1, source_target_pairs={{0,128},{64,192},{128,0},{192,64},{1,129},{65,193},{129,1},{193,65... | collective-permute-start | bytes 1572872 | tf_op jit(solution)/shard_map/ppermute | solution.py:377
  193.3 17.3 %collective-permute-start.26 = (bf16[1024,256]{1,0:T(8,128)(2,1)}, bf16[1024,256]{1,0:T(8,128)(2,1)S(1)}, u32[]{:S(2)}, u32[]{:S(2)}) collective-permute-start(bf16[1024,256]{1,0:T(8,128)(2,1)} %get-tuple-element.54), channel_id=1, source_target_pairs={{0,192},{64,0},{128,64},{192,128},{1,193},{65,1},{129,65},{193,129... | collective-permute-start | bytes 1572872 | tf_op jit(solution)/shard_map/ppermute | solution.py:377
  204.9 5.8 %copy-start.8 = (bf16[1024,256]{1,0:T(8,128)(2,1)}, bf16[1024,256]{1,0:T(8,128)(2,1)S(1)}, u32[]{:S(2)}) copy-start(bf16[1024,256]{1,0:T(8,128)(2,1)S(1)} %collective-permute-done.24.b_ref) | copy-start | bytes 1572868
  (10 other events, 8.6 us)
